TPU v7x, 128 devices: a whole 4x4x4 slice. The times are simulated.
128 devices in a mesh: plane: 8 (over x, core), tile: 16 (over y, z).
Axes of the slice: x: 4, y: 4, z: 4, core: 2. Of those that a mesh axis runs over, the one named last changes fastest.
Arguments:
- primal: float32 [5, 16, 64, 512], P(None, 'plane', 'tile'), may hold values from -6 to 6
- dual: float32 [5, 16, 16, 1024], P(None, 'plane', 'tile'), may hold values from -6 to 6
- measured: float32 [16, 16, 1024], P('plane', 'tile'), may hold values from -6 to 6
- footprint_weights: float32 [16, 16, 12, 128, 128], P('tile'), may hold values from -0.15625 to 0.15625
- pixel_index: int32 [16, 16, 12], P('tile'), may hold values from 0 to 15
- bin_index: int32 [16, 16, 12], replicated, may hold values from 0 to 7
- slot_count: int32 [16, 16], P('tile'), may hold values from 6 to 12, as said below
- dual_kernel: float32 [32, 7, 3, 3, 3], replicated, may hold values from -0.4375 to 0.4375
- dual_bias: float32 [32], replicated, may hold values from -1.5 to 1.5
- dual_slope: float32 [32], replicated, may hold values from 0.05 to 0.8
- dual_mixing: float32 [5, 32], replicated, may hold values from -1 to 1
- dual_shift: float32 [5], replicated, may hold values from -1.5 to 1.5
- primal_kernel: float32 [32, 6, 3, 3, 3], replicated, may hold values from -0.5 to 0.5
- primal_bias: float32 [32], replicated, may hold values from -1.5 to 1.5
- primal_slope: float32 [32], replicated, may hold values from 0.05 to 0.8
- primal_mixing: float32 [5, 32], replicated, may hold values from -1 to 1
- primal_shift: float32 [5], replicated, may hold values from -1.5 to 1.5
Outputs:
- new_primal: float32 [5, 16, 64, 512], P(None, 'plane', 'tile')
- new_dual: float32 [5, 16, 16, 1024], P(None, 'plane', 'tile')
Inputs may be any that keep to these rules, and one draw needn't show every extreme that they name: slot_count is at least 6 everywhere, and equals 12 for some strip and angle in every draw.
All inputs are finite; a program needn't handle non-finite values.
Results may differ from a plain program's by a relative error of at most 0.0003.
Values sent between devices are 32-bit elements; how exact they have to be, the bound alone decides.
No kernel may reach another device: no remote copies, remote signals or barrier semaphores. Data moves between devices by JAX's collectives and lax.ppermute only.
A program may use at most 64 MiB of HBM per device.

v0:
```python
import jax
import jax.numpy as jnp
from jax import lax
from jax.sharding import PartitionSpec as P

HIGHEST = lax.Precision.HIGHEST


def in_blocks(array, dim, devices):
    before, after = (array.shape[:dim], array.shape[dim + 1 :])
    return jnp.moveaxis(array.reshape(*before, devices, -1, *after), dim, 0)


def sent_and_summed(array, axis, dim):
    devices = lax.axis_size(axis)
    pieces = lax.all_to_all(in_blocks(array, dim, devices), axis, 0, 0, tiled=True)
    return jnp.sum(pieces, axis=0)


def with_halo(cells, sides, width):
    for axis, dim in sides:
        count = lax.axis_size(axis)
        ends = count - 1
        head = lax.slice_in_dim(cells, 0, width, axis=dim)
        tail = lax.slice_in_dim(cells, cells.shape[dim] - width, cells.shape[dim], axis=dim)
        cells = jnp.concatenate(
            [
                lax.ppermute(tail, axis, [(i, (i + 1) % count) for i in range(ends)]),
                cells,
                lax.ppermute(head, axis, [((i + 1) % count, i) for i in range(ends)]),
            ],
            axis=dim,
        )
    return cells


def copy_for_each(array, axis):
    devices = lax.axis_size(axis)
    return lax.all_to_all(
        jnp.broadcast_to(array[None], (devices, *array.shape)), axis, 0, 0, tiled=True
    )


def laid_out(pieces, dim):
    pieces = jnp.moveaxis(pieces, 0, dim)
    shape = pieces.shape
    return pieces.reshape(*shape[:dim], shape[dim] * shape[dim + 1], *shape[dim + 2 :])


def collect(array, axis, dim):
    pieces = copy_for_each(array, axis)
    return laid_out(pieces, dim)


def indicator(indices, total_count):
    return (indices[..., None] == jnp.arange(total_count, dtype=jnp.int32)).astype(jnp.float32)


def network(padded, kernel, bias_first, leak_slope, mixing, bias_last):
    hidden = lax.conv_general_dilated(
        padded[None],
        kernel,
        (1, 1, 1),
        "VALID",
        dimension_numbers=("NCDHW", "OIDHW", "NCDHW"),
        precision=HIGHEST,
    )[0]
    hidden = hidden + bias_first[:, None, None, None]
    hidden = jnp.where(hidden > 0, hidden, leak_slope[:, None, None, None] * hidden)
    return (
        jnp.einsum("oc,czyx->ozyx", mixing, hidden, precision=HIGHEST)
        + bias_last[:, None, None, None]
    )


def per_device(
    primal,
    dual,
    measured,
    footprint_weights,
    pixel_index,
    bin_index,
    slot_count,
    dual_kernel,
    dual_bias,
    dual_slope,
    dual_mixing,
    dual_shift,
    primal_kernel,
    primal_bias,
    primal_slope,
    primal_mixing,
    primal_shift,
):
    planes_here = primal.shape[1]
    rows_here = primal.shape[2]
    columns = primal.shape[3]
    bin_count = dual.shape[3]
    local_angles = dual.shape[2]
    block_size = footprint_weights.shape[-1]
    slot_total = footprint_weights.shape[2]
    pixel_blocks = rows_here * columns // block_size
    bin_blocks = bin_count // block_size
    strip_index = lax.axis_index("tile")
    weights = footprint_weights[0]
    pixel_rows = pixel_index[0]
    own_bins = lax.dynamic_slice_in_dim(bin_index, strip_index, 1, 0)[0]
    live_slots = (jnp.arange(slot_total, dtype=jnp.int32)[None, :] < slot_count[0][:, None]).astype(
        jnp.float32
    )
    source = primal[1].reshape(planes_here, pixel_blocks, block_size)
    picked = source[:, pixel_rows, :]
    weight_part = weights
    live_part = live_slots
    products = jnp.einsum("zasj,asjk->aszk", picked, weight_part, precision=HIGHEST)
    products = products * live_part[:, :, None, None]
    bins_part = own_bins
    terms = jnp.einsum(
        "aszk,asb->azbk", products, indicator(bins_part, bin_blocks), precision=HIGHEST
    )
    projected = sent_and_summed(
        terms.reshape(local_angles * lax.axis_size("tile"), planes_here, bin_count), "tile", 0
    )
    projected = jnp.transpose(projected, (1, 0, 2))
    stacked = jnp.concatenate([dual, projected[None], measured[None]], 0)
    rimmed = with_halo(stacked, (("plane", 1), ("tile", 2)), 1)
    rimmed = jnp.pad(rimmed, ((0, 0), (0, 0), (0, 0), (1, 1)))
    new_dual = dual + network(rimmed, dual_kernel, dual_bias, dual_slope, dual_mixing, dual_shift)
    leading = jnp.transpose(new_dual[0], (1, 0, 2))
    start_back = jnp.zeros((planes_here, pixel_blocks, block_size), jnp.float32)
    piece = collect(leading, "tile", 0)
    row_count = piece.shape[0]
    blocks_in = piece.reshape(row_count, planes_here, bin_blocks, block_size)
    bins_part = lax.slice_in_dim(own_bins, 0, row_count, axis=0)
    pixels_part = lax.slice_in_dim(pixel_rows, 0, row_count, axis=0)
    weight_part = lax.slice_in_dim(weights, 0, row_count, axis=0)
    live_part = lax.slice_in_dim(live_slots, 0, row_count, axis=0)
    picked = jax.vmap(lambda blocks_one, index_one: blocks_one[:, index_one, :])(
        blocks_in, bins_part
    )
    spread = (
        jnp.einsum("azsk,asjk->azsj", picked, weight_part, precision=HIGHEST)
        * live_part[:, None, :, None]
    )
    back = start_back + jnp.einsum(
        "azsj,asq->zqj", spread, indicator(pixels_part, pixel_blocks), precision=HIGHEST
    )
    stacked_primal = jnp.concatenate(
        [primal, back.reshape(planes_here, rows_here, columns)[None]], 0
    )
    rimmed_primal = with_halo(stacked_primal, (("plane", 1), ("tile", 2)), 1)
    rimmed_primal = jnp.pad(rimmed_primal, ((0, 0), (0, 0), (0, 0), (1, 1)))
    new_primal = primal + network(
        rimmed_primal, primal_kernel, primal_bias, primal_slope, primal_mixing, primal_shift
    )
    return (new_primal, new_dual)


def solution(mesh):
    in_specs = (
        P(None, "plane", "tile", None),
        P(None, "plane", "tile", None),
        P("plane", "tile", None),
        P("tile", None, None, None, None),
        P("tile", None, None),
        P(),
        P("tile", None),
        P(),
        P(),
        P(),
        P(),
        P(),
        P(),
        P(),
        P(),
        P(),
        P(),
    )
    out_specs = (P(None, "plane", "tile", None), P(None, "plane", "tile", None))
    return jax.shard_map(
        per_device, mesh=mesh, in_specs=in_specs, out_specs=out_specs, check_vma=False
    )
```

profile of v0, /device:TPU:0, one launch (start us, length us, event | category | flops | bytes accessed | tf_op | source)
XLA Modules:
  0.0 173.0 jit_solution(4826630621091497559)
XLA Ops:
  4.8 13.0 %fusion.28 = f32[16,12,2,128]{3,2,1,0:T(2,128)S(1)} fusion(f32[2,16,12,128]{3,0,2,1:T(2,128)S(1)} %bitcast.122, f32[1,16,12,128,128]{4,3,2,1,0:T(8,128)} %param.20, f32[16,12]{1,0:T(8,128)S(1)} %fusion.60), kind=kOutput, calls=%fused_computation.33 | convolution fusion | flops 75546624 | bytes 12976896 | tf_op jit(solution)/shard_map/zasj,asjk->aszk/dot_general | solution.py:115
  18.2 15.8 %all_to_all.10 = f32[16,1,2,1024]{3,2,1,0:T(2,128)S(1)} all-to-all(f32[16,1,2,1024]{3,2,1,0:T(2,128)S(1)} %bitcast.123), channel_id=1, replica_groups=mesh['plane'=8,'tile'=16] {'tile'}, dimensions={0} | all-to-all | bytes 262144 | tf_op jit(solution)/shard_map/all_to_all | solution.py:16
  34.2 1.3 collective-permute-start
  35.5 1.3 collective-permute-start.1
  36.8 3.5 %collective-permute-done.1 = f32[7,1,1,1024]{3,2,1,0:T(1,128)S(1)} collective-permute-done((f32[7,1,1,1024]{3,2,1,0:T(1,128)S(1)}, f32[7,1,1,1024]{3,2,1,0:T(1,128)S(1)}, u32[]{:S(2)}, u32[]{:S(2)}) %collective-permute-start.1) | collective-permute-done | bytes 28704 | tf_op jit(solution)/shard_map/ppermute | solution.py:30
  40.4 1.3 collective-permute-start.3
  41.7 4.7 %collective-permute-start.2 = (f32[7,4,1,1024]{3,2,1,0:T(1,128)S(1)}, f32[7,4,1,1024]{3,2,1,0:T(1,128)S(1)}, u32[]{:S(2)}, u32[]{:S(2)}) collective-permute-start(f32[7,4,1,1024]{3,2,1,0:T(1,128)S(1)} %pad_maximum_fusion), channel_id=1, source_target_pairs={{0,1},{1,2},{2,3},{3,4},{4,5},{5,6},{6,7},{7,8},{8,9},{9,10},{10,1... | collective-permute-start | bytes 344072 | tf_op jit(solution)/shard_map/ppermute | solution.py:28
  47.1 1.5 collective-permute-done.2
  48.6 1.0 fusion.39
  50.2 5.3 %copy.92 = f32[7,4,3,1,8,129]{0,4,5,2,1,3:T(8,128)} copy(f32[7,4,3,1,8,129]{5,4,2,1,0,3:T(8,128)S(1)} %reshape.181) | data formatting | bytes 693504 | tf_op jit(solution)/shard_map/conv_general_dilated | solution.py:60
  56.5 17.4 %fusion.21 = f32[2,1,8,129,32]{4,2,3,1,0:T(8,128)S(1)} fusion(f32[32,7,3,3,3]{0,1,4,3,2:T(8,128)S(1)} %copy-done.5, f32[7,4,3,1,7,2]{0,4,5,2,1,3:T(8,128)S(1)} %slice.42, f32[7,4,3,1,8,129]{0,4,5,2,1,3:T(8,128)} %copy.92, pred[8,129]{0,1:T(8,128)(4,1)S(1)} %copy-done.14), kind=kOutput, calls=%fused_computation.24 | convolution fusion | flops 150127008 | bytes 640872 | tf_op jit(solution)/shard_map/conv_general_dilated | solution.py:60
  76.0 7.0 %all-to-all-start.1 = ((f32[16,1,2,1024]{3,2,1,0:T(2,128)}), f32[16,1,2,1024]{3,2,1,0:T(2,128)S(1)}, u32[]{:S(2)}, u32[]{:S(2)}) async-start(f32[16,1,2,1024]{3,2,1,0:T(2,128)} %broadcast_in_dim.13), calls=%async_computation.1 | async-start | bytes 262144 | tf_op jit(solution)/shard_map/all_to_all | solution.py:39
  83.2 8.1 %all-to-all-done.1 = f32[16,1,2,1024]{3,2,1,0:T(2,128)S(1)} async-done(((f32[16,1,2,1024]{3,2,1,0:T(2,128)}), f32[16,1,2,1024]{3,2,1,0:T(2,128)S(1)}, u32[]{:S(2)}, u32[]{:S(2)}) %all-to-all-start.1) | async-done | bytes 131104 | tf_op jit(solution)/shard_map/all_to_all | solution.py:39
  91.4 1.8 %gather_fusion.1 = f32[192,2,128]{2,1,0:T(2,128)S(1)} fusion(f32[16,2,8,128]{3,1,2,0:T(2,128)S(1)} %bitcast.120, s32[192]{0:T(256)S(1)} %reshape.169), kind=kCustom, calls=%fused_computation.1 | custom fusion | bytes 394752 | tf_op jit(solution)/shard_map/vmap()/gather | solution.py:138
  93.2 22.0 %fusion.34 = f32[16,2,12,128]{3,1,2,0:T(2,128)S(1)} fusion(f32[16,2,12,128]{3,1,2,0:T(2,128)S(1)} %bitcast.121, f32[1,16,12,128,128]{4,3,2,1,0:T(8,128)} %param.20, f32[16,12]{1,0:T(8,128)S(1)} %fusion.60), kind=kOutput, calls=%fused_computation.35 | convolution fusion | flops 75546624 | bytes 12976896 | tf_op jit(solution)/shard_map/azsk,asjk->azsj/dot_general | solution.py:142
  115.5 1.8 %collective-permute-start.4 = (f32[6,1,4,512]{3,2,1,0:T(4,128)S(1)}, f32[6,1,4,512]{3,2,1,0:T(4,128)S(1)}, u32[]{:S(2)}, u32[]{:S(2)}) collective-permute-start(f32[6,1,4,512]{3,2,1,0:T(4,128)S(1)} %get-tuple-element.16), channel_id=1, source_target_pairs={{0,16},{16,32},{32,48},{48,64},{64,80},{80,96},{96,112},{1,17},{17... | collective-permute-start | bytes 147464 | tf_op jit(solution)/shard_map/ppermute | solution.py:28
  117.3 1.3 collective-permute-start.5
  118.6 4.4 %collective-permute-done.5 = f32[6,1,4,512]{3,2,1,0:T(4,128)S(1)} collective-permute-done((f32[6,1,4,512]{3,2,1,0:T(4,128)S(1)}, f32[6,1,4,512]{3,2,1,0:T(4,128)S(1)}, u32[]{:S(2)}, u32[]{:S(2)}) %collective-permute-start.5) | collective-permute-done | bytes 49184 | tf_op jit(solution)/shard_map/ppermute | solution.py:30
  123.1 2.4 %collective-permute-start.6 = (f32[6,4,1,512]{3,2,1,0:T(1,128)S(1)}, f32[6,4,1,512]{3,2,1,0:T(1,128)S(1)}, u32[]{:S(2)}, u32[]{:S(2)}) collective-permute-start(f32[6,4,1,512]{3,2,1,0:T(1,128)S(1)} %get-tuple-element.14), channel_id=1, source_target_pairs={{0,1},{1,2},{2,3},{3,4},{4,5},{5,6},{6,7},{7,8},{8,9},{9,10},{10,1... | collective-permute-start | bytes 147464 | tf_op jit(solution)/shard_map/ppermute | solution.py:28
  125.5 1.3 collective-permute-start.7
  127.4 4.0 %collective-permute-done.7 = f32[6,4,1,512]{3,2,1,0:T(1,128)S(1)} collective-permute-done((f32[6,4,1,512]{3,2,1,0:T(1,128)S(1)}, f32[6,4,1,512]{3,2,1,0:T(1,128)S(1)}, u32[]{:S(2)}, u32[]{:S(2)}) %collective-permute-start.7) | collective-permute-done | bytes 49184 | tf_op jit(solution)/shard_map/ppermute | solution.py:30
  132.3 4.7 %copy.100 = f32[6,4,6,1,8,65]{0,4,5,2,1,3:T(8,128)} copy(f32[6,4,6,1,8,65]{5,4,2,1,0,3:T(8,128)S(1)} %reshape.182) | data formatting | bytes 599040 | tf_op jit(solution)/shard_map/conv_general_dilated | solution.py:60
  138.0 32.4 %fusion.18 = f32[2,4,8,65,32]{4,2,3,1,0:T(8,128)S(1)} fusion(f32[6,4,6,1,7,2]{0,4,5,2,1,3:T(8,128)S(1)} %slice.47, f32[6,4,6,1,8,65]{0,4,5,2,1,3:T(8,128)} %copy.100, pred[8,65]{0,1:T(8,128)(4,1)S(1)} %copy-done.15, f32[32,6,3,3,3]{0,4,3,2,1:T(4,128)S(1)} %copy-done), kind=kOutput, calls=%fused_computation.23 | convolution fusion | flops 259149952 | bytes 861320 | tf_op jit(solution)/shard_map/conv_general_dilated | solution.py:60
  170.4 1.0 copy.102
  (80 shorter events, 13.4 us)
Async XLA Ops:
  0.6 137.3 %copy-start = (f32[32,6,3,3,3]{0,4,3,2,1:T(4,128)S(1)}, f32[32,6,3,3,3]{0,4,3,2,1:T(4,128)}, u32[]{:S(2)}) copy-start(f32[32,6,3,3,3]{0,4,3,2,1:T(4,128)} %param.29) | copy-start | bytes 62212
  4.8 29.3 %copy-start.1 = (f32[5,2,1,1024]{3,2,1,0:T(1,128)S(1)}, f32[5,2,1,1024]{3,2,1,0:T(1,128)}, u32[]{:S(2)}) copy-start(f32[5,2,1,1024]{3,2,1,0:T(1,128)} %param.18) | copy-start | bytes 122884
  4.8 29.3 %copy-start.3 = (f32[2,1,1024]{2,1,0:T(1,128)S(1)}, f32[2,1,1024]{2,1,0:T(1,128)}, u32[]{:S(2)}) copy-start(f32[2,1,1024]{2,1,0:T(1,128)} %param.19) | copy-start | bytes 24580
  17.9 38.6 %copy-start.5 = (f32[32,7,3,3,3]{0,1,4,3,2:T(8,128)S(1)}, f32[32,7,3,3,3]{0,1,4,3,2:T(8,128)}, u32[]{:S(2)}) copy-start(f32[32,7,3,3,3]{0,1,4,3,2:T(8,128)} %param.24) | copy-start | bytes 72580
  17.9 38.6 %copy-start.14 = (pred[8,129]{0,1:T(8,128)(4,1)S(1)}, pred[8,129]{0,1:T(8,128)(4,1)}, u32[]{:S(2)}) copy-start(pred[8,129]{0,1:T(8,128)(4,1)} %constant.36) | copy-start | bytes 3100
  34.2 2.6 %collective-permute-start = (f32[7,1,1,1024]{3,2,1,0:T(1,128)S(1)}, f32[7,1,1,1024]{3,2,1,0:T(1,128)S(1)}, u32[]{:S(2)}, u32[]{:S(2)}) collective-permute-start(f32[7,1,1,1024]{3,2,1,0:T(1,128)S(1)} %get-tuple-element.18), channel_id=1, source_target_pairs={{0,16},{16,32},{32,48},{48,64},{64,80},{80,96},{96,112},{1,17},{17... | collective-permute-start | bytes 86024 | tf_op jit(solution)/shard_map/ppermute | solution.py:28
  35.5 4.8 %collective-permute-start.1 = (f32[7,1,1,1024]{3,2,1,0:T(1,128)S(1)}, f32[7,1,1,1024]{3,2,1,0:T(1,128)S(1)}, u32[]{:S(2)}, u32[]{:S(2)}) collective-permute-start(f32[7,1,1,1024]{3,2,1,0:T(1,128)S(1)} %get-tuple-element.19), channel_id=1, source_target_pairs={{16,0},{32,16},{48,32},{64,48},{80,64},{96,80},{112,96},{17,1},{33... | collective-permute-start | bytes 86024 | tf_op jit(solution)/shard_map/ppermute | solution.py:30
  40.4 6.7 %collective-permute-start.3 = (f32[7,4,1,1024]{3,2,1,0:T(1,128)S(1)}, f32[7,4,1,1024]{3,2,1,0:T(1,128)S(1)}, u32[]{:S(2)}, u32[]{:S(2)}) collective-permute-start(f32[7,4,1,1024]{3,2,1,0:T(1,128)S(1)} %pad_maximum_fusion), channel_id=1, source_target_pairs={{1,0},{2,1},{3,2},{4,3},{5,4},{6,5},{7,6},{8,7},{9,8},{10,9},{11,1... | collective-permute-start | bytes 344072 | tf_op jit(solution)/shard_map/ppermute | solution.py:30
  41.7 6.9 %collective-permute-start.2 = (f32[7,4,1,1024]{3,2,1,0:T(1,128)S(1)}, f32[7,4,1,1024]{3,2,1,0:T(1,128)S(1)}, u32[]{:S(2)}, u32[]{:S(2)}) collective-permute-start(f32[7,4,1,1024]{3,2,1,0:T(1,128)S(1)} %pad_maximum_fusion), channel_id=1, source_target_pairs={{0,1},{1,2},{2,3},{3,4},{4,5},{5,6},{6,7},{7,8},{8,9},{9,10},{10,1... | collective-permute-start | bytes 344072 | tf_op jit(solution)/shard_map/ppermute | solution.py:28
  56.5 18.4 %copy-start.6 = (f32[5,32]{1,0:T(8,128)S(1)}, f32[5,32]{1,0:T(8,128)}, u32[]{:S(2)}) copy-start(f32[5,32]{1,0:T(8,128)} %param.27) | copy-start | bytes 1924
  56.5 18.4 %copy-start.8 = (f32[32]{0:T(128)S(1)}, f32[32]{0:T(128)}, u32[]{:S(2)}) copy-start(f32[32]{0:T(128)} %param.26) | copy-start | bytes 388
  56.5 18.4 %copy-start.9 = (f32[32]{0:T(128)S(1)}, f32[32]{0:T(128)}, u32[]{:S(2)}) copy-start(f32[32]{0:T(128)} %param.25) | copy-start | bytes 388
  56.5 26.5 %copy-start.4 = (s32[1,16,12]{1,0,2:T(1,128)S(1)}, s32[1,16,12]{1,0,2:T(1,128)}, u32[]{:S(2)}) copy-start(s32[1,16,12]{1,0,2:T(1,128)} %param.21) | copy-start | bytes 2308
  56.5 26.7 %copy-start.2 = (f32[5,2,4,512]{3,2,1,0:T(4,128)S(1)}, f32[5,2,4,512]{3,2,1,0:T(4,128)}, u32[]{:S(2)}) copy-start(f32[5,2,4,512]{3,2,1,0:T(4,128)} %param.17) | copy-start | bytes 245764
  76.0 15.4 %all-to-all-start.1 = ((f32[16,1,2,1024]{3,2,1,0:T(2,128)}), f32[16,1,2,1024]{3,2,1,0:T(2,128)S(1)}, u32[]{:S(2)}, u32[]{:S(2)}) async-start(f32[16,1,2,1024]{3,2,1,0:T(2,128)} %broadcast_in_dim.13), calls=%async_computation.1 | async-start | bytes 262144 | tf_op jit(solution)/shard_map/all_to_all | solution.py:39
  115.2 22.7 %copy-start.15 = (pred[8,65]{0,1:T(8,128)(4,1)S(1)}, pred[8,65]{0,1:T(8,128)(4,1)}, u32[]{:S(2)}) copy-start(pred[8,65]{0,1:T(8,128)(4,1)} %constant.35) | copy-start | bytes 1564
  115.5 3.2 %collective-permute-start.4 = (f32[6,1,4,512]{3,2,1,0:T(4,128)S(1)}, f32[6,1,4,512]{3,2,1,0:T(4,128)S(1)}, u32[]{:S(2)}, u32[]{:S(2)}) collective-permute-start(f32[6,1,4,512]{3,2,1,0:T(4,128)S(1)} %get-tuple-element.16), channel_id=1, source_target_pairs={{0,16},{16,32},{32,48},{48,64},{64,80},{80,96},{96,112},{1,17},{17... | collective-permute-start | bytes 147464 | tf_op jit(solution)/shard_map/ppermute | solution.py:28
  117.3 5.7 %collective-permute-start.5 = (f32[6,1,4,512]{3,2,1,0:T(4,128)S(1)}, f32[6,1,4,512]{3,2,1,0:T(4,128)S(1)}, u32[]{:S(2)}, u32[]{:S(2)}) collective-permute-start(f32[6,1,4,512]{3,2,1,0:T(4,128)S(1)} %get-tuple-element.17), channel_id=1, source_target_pairs={{16,0},{32,16},{48,32},{64,48},{80,64},{96,80},{112,96},{17,1},{33... | collective-permute-start | bytes 147464 | tf_op jit(solution)/shard_map/ppermute | solution.py:30
  123.1 4.4 %collective-permute-start.6 = (f32[6,4,1,512]{3,2,1,0:T(1,128)S(1)}, f32[6,4,1,512]{3,2,1,0:T(1,128)S(1)}, u32[]{:S(2)}, u32[]{:S(2)}) collective-permute-start(f32[6,4,1,512]{3,2,1,0:T(1,128)S(1)} %get-tuple-element.14), channel_id=1, source_target_pairs={{0,1},{1,2},{2,3},{3,4},{4,5},{5,6},{6,7},{7,8},{8,9},{9,10},{10,1... | collective-permute-start | bytes 147464 | tf_op jit(solution)/shard_map/ppermute | solution.py:28
  125.5 6.0 %collective-permute-start.7 = (f32[6,4,1,512]{3,2,1,0:T(1,128)S(1)}, f32[6,4,1,512]{3,2,1,0:T(1,128)S(1)}, u32[]{:S(2)}, u32[]{:S(2)}) collective-permute-start(f32[6,4,1,512]{3,2,1,0:T(1,128)S(1)} %get-tuple-element.15), channel_id=1, source_target_pairs={{1,0},{2,1},{3,2},{4,3},{5,4},{6,5},{7,6},{8,7},{9,8},{10,9},{11,1... | collective-permute-start | bytes 147464 | tf_op jit(solution)/shard_map/ppermute | solution.py:30
  137.9 33.8 %copy-start.7 = (f32[5,32]{1,0:T(8,128)S(1)}, f32[5,32]{1,0:T(8,128)}, u32[]{:S(2)}) copy-start(f32[5,32]{1,0:T(8,128)} %param.32) | copy-start | bytes 1924
  137.9 33.8 %copy-start.11 = (f32[32]{0:T(128)S(1)}, f32[32]{0:T(128)}, u32[]{:S(2)}) copy-start(f32[32]{0:T(128)} %param.31) | copy-start | bytes 388
  137.9 33.8 %copy-start.12 = (f32[32]{0:T(128)S(1)}, f32[32]{0:T(128)}, u32[]{:S(2)}) copy-start(f32[32]{0:T(128)} %param.30) | copy-start | bytes 388
  137.9 33.8 %copy-start.13 = (f32[5]{0:T(128)S(1)}, f32[5]{0:T(128)}, u32[]{:S(2)}) copy-start(f32[5]{0:T(128)} %param.33) | copy-start | bytes 64
  (1 other events, 18.4 us)
where the time goes:
time: 176 us; the launch traced here: 173 us
  matrix products  86.2 us (49%)
  starting transfers between devices  22.5 us (13%)
  waiting for transfers between devices  22.2 us (13%)
  local copies, waits for them, and re-layouts  21.1 us (12%)
  blocking collectives  15.8 us (9%)
  other arithmetic  4.04 us (2%)
    conv_general_dilated x2, matrix products, network(): lax.conv_general_dilated(padded[None], kernel, (1, 1, 1), 'VALID', dimens...  49.8 us
    dot_general x1, matrix products, per_device(): jnp.einsum('azsk,asjk->azsj', picked, weight_part, precision=HIGHEST)  22 us
    all_to_all x1, blocking collectives, sent_and_summed(): lax.all_to_all(in_blocks(array, dim, devices), axis, 0, 0, tiled=True)  15.8 us
    conv_general_dilated x10, local copies, waits for them, and re-layouts, network(): lax.conv_general_dilated(padded[None], kernel, (1, 1, 1), 'VALID', dimens...  14.9 us
    dot_general x1, matrix products, per_device(): jnp.einsum('zasj,asjk->aszk', picked, weight_part, precision=HIGHEST)  13 us
    ppermute x4, waiting for transfers between devices, with_halo(): lax.ppermute(head, axis, [((i + 1) % count, i) for i in range(ends)])  12.5 us
    ppermute x4, starting transfers between devices, with_halo(): lax.ppermute(tail, axis, [(i, (i + 1) % count) for i in range(ends)])  10.3 us
    all_to_all x1, waiting for transfers between devices, copy_for_each(): lax.all_to_all(jnp.broadcast_to(array[None], (devices, *array.shape)), ax...  8.12 us
  transfers between devices with their start and end apart: 9, of which 6 were waited for; matrix products, arithmetic and copies ran while one was open for 0% of the time, Pallas kernels for 0%

commit v1 on v0

v1 whole, which is shorter than its diff:
```python
import functools

import jax
import jax.numpy as jnp
from jax import lax
from jax.experimental import pallas as pl
from jax.experimental.pallas import tpu as pltpu
from jax.sharding import PartitionSpec as P

F32 = jnp.float32
BF16 = jnp.bfloat16
VMEM = pl.BlockSpec(memory_space=pltpu.VMEM)
SMEM = pl.BlockSpec(memory_space=pltpu.SMEM)


def split(x):
    hi = x.astype(BF16)
    return hi, (x - hi.astype(F32)).astype(BF16)


def dot3(a, b, dims):
    (a_hi, a_lo), (b_hi, b_lo) = a, b
    dot = functools.partial(
        lax.dot_general, dimension_numbers=(dims, ((), ())), preferred_element_type=F32
    )
    return dot(a_hi, b_hi) + dot(a_lo, b_hi) + dot(a_hi, b_lo)


def column(ref, count):
    rows = -(-count // 8) * 8
    index = lax.broadcasted_iota(jnp.int32, (rows, 128), 0)
    out = jnp.zeros((rows, 128), F32)
    for i in range(count):
        out = jnp.where(index == i, ref[i], out)
    return out[:, 0:1]


def shifted_sum(stack):
    left, mid, right = stack
    width = mid.shape[1]
    lane = lax.broadcasted_iota(jnp.int32, mid.shape, 1)
    left = jnp.where(lane == 0, 0.0, pltpu.roll(left, 1, 1))
    right = jnp.where(lane == width - 1, 0.0, pltpu.roll(right, width - 1, 1))
    return left + mid + right


def pack_kernel(dual_ref, measured_ref, primal_ref, out_ref):
    zero = jnp.zeros((1, 1024), F32)
    for z in range(2):
        for c in range(5):
            out_ref[z * 8 + c : z * 8 + c + 1, :] = dual_ref[c, z]
        out_ref[z * 8 + 5 : z * 8 + 6, :] = zero
        out_ref[z * 8 + 6 : z * 8 + 7, :] = measured_ref[z]
        out_ref[z * 8 + 7 : z * 8 + 8, :] = zero
    for k, row in enumerate((0, 3)):
        for c in range(5):
            for z in range(2):
                i = 16 + k * 5 + c
                out_ref[i : i + 1, z * 512 : (z + 1) * 512] = primal_ref[c, z, row : row + 1, :]
    out_ref[26:32, :] = jnp.zeros((6, 1024), F32)


def project_kernel(pix_ref, bin_ref, cnt_ref, primal_ref, w_ref, out_ref, hi_ref, lo_ref, hot_ref):
    a = pl.program_id(0)
    t = lax.axis_index("tile")

    @pl.when(a == 0)
    def _():
        for q in range(16):
            r, col = q // 4, (q % 4) * 128
            v = jnp.concatenate(
                [
                    jnp.broadcast_to(primal_ref[1, z, r : r + 1, col : col + 128], (8, 128))
                    for z in range(2)
                ],
                0,
            )
            hi_ref[q], lo_ref[q] = split(v)
        row = lax.broadcasted_iota(jnp.int32, (16, 128), 0)
        for b in range(9):
            hot_ref[b] = jnp.where((row & 7) == b, 1.0, 0.0).astype(BF16)
        out_ref[0, 0] = jnp.zeros((16, 128), F32)
        out_ref[15, 2] = jnp.zeros((16, 128), F32)

    count = cnt_ref[0, a]
    parts = []
    for s in range(12):
        q = pix_ref[s, 0, a]
        b = jnp.where(s < count, bin_ref[s, t, a], 8)
        hot = hot_ref[b]
        parts.append(jnp.concatenate([hi_ref[q] * hot, lo_ref[q] * hot], 0))
    left = jnp.concatenate(parts, 1)
    w_hi, w_lo = split(w_ref[0, 0].reshape(12 * 128, 128))
    right = jnp.concatenate([w_hi, w_lo], 1)
    d = jnp.dot(left, right, preferred_element_type=F32)
    res = d[0:16, 0:128] + (d[0:16, 128:256] + d[16:32, 0:128])
    out_ref[a, 1] = res

    @pl.when(a > 0)
    def _():
        out_ref[jnp.maximum(a - 1, 0), 2] = res

    @pl.when(a < 15)
    def _():
        out_ref[jnp.minimum(a + 1, 15), 0] = res


def assemble_kernel(got_ref, own_ref, left_ref, right_ref, primal_ref, sp_ref, sm_ref):
    t = lax.axis_index("tile")
    total = got_ref[0]
    for i in range(1, 16):
        total = total + got_ref[i]
    ok = (t > 0, None, t < 15)
    for k, src in enumerate((left_ref, own_ref, right_ref)):
        keep = (lambda v: v) if ok[k] is None else (lambda v, m=ok[k]: jnp.where(m, v, 0.0))
        for z in range(2):
            base = z * 24 + k * 8
            block = keep(src[z * 8 : z * 8 + 8, :])
            for out in (sp_ref, sm_ref):
                out[base : base + 8, :] = block
                for b in range(8):
                    i = z * 8 + b
                    out[base + 5 : base + 6, b * 128 : (b + 1) * 128] = keep(total[k, i : i + 1, :])
    for z, out in ((0, sm_ref), (1, sp_ref)):
        for row in range(6):
            for c in range(5):
                if row == 0:
                    v = jnp.where(ok[0], left_ref[21 + c : 22 + c, z * 512 : (z + 1) * 512], 0.0)
                elif row == 5:
                    v = jnp.where(ok[2], right_ref[16 + c : 17 + c, z * 512 : (z + 1) * 512], 0.0)
                else:
                    v = primal_ref[c, z, row - 1 : row, :]
                i = row * 5 + c
                lane = (i // 16) * 512
                out[48 + i % 16 : 49 + i % 16, lane : lane + 512] = v
        out[62:64, 512:1024] = jnp.zeros((2, 512), F32)


def dual_kernel_body(
    own_ref, prev_ref, next_ref, kern_ref, mix_ref, bias_ref, slope_ref, shift_ref,
    new_ref, send_ref, tt_ref,
):
    p = lax.axis_index("plane")
    tt_ref[...] = jnp.zeros((72, 96), F32)
    for dz in range(3):
        for da in range(3):
            base = dz * 24 + da * 8
            tt_ref[base : base + 7, :] = jnp.concatenate(
                [kern_ref[dz, da, db] for db in range(3)], 1
            )
    x = jnp.concatenate(
        [
            jnp.where(p > 0, prev_ref[0:48, :], 0.0),
            own_ref[0:48, :],
            jnp.where(p < 7, next_ref[0:48, :], 0.0),
        ],
        0,
    )
    x_hi, x_lo = split(x)
    tt = split(tt_ref[...].T)
    bias, slope, shift = column(bias_ref, 32), column(slope_ref, 32), column(shift_ref, 5)
    mix = split(jnp.concatenate([mix_ref[...], jnp.zeros((3, 32), F32)], 0))
    for z in range(4):
        rows = slice(z * 24, z * 24 + 72)
        h = dot3(tt, (x_hi[rows], x_lo[rows]), ((1,), (0,)))
        h = shifted_sum([h[i * 32 : (i + 1) * 32] for i in range(3)]) + bias
        h = jnp.where(h > 0, h, slope * h)
        out = dot3(mix, split(h), ((1,), (0,))) + shift
        out = out + x[(z + 1) * 24 + 8 : (z + 1) * 24 + 16]
        if z in (1, 2):
            for c in range(5):
                new_ref[c, z - 1] = out[c : c + 1, :]
        for b in range(8):
            piece = jnp.broadcast_to(out[0:1, b * 128 : (b + 1) * 128], (16, 128))
            send_ref[:, b, z, :] = piece


def back_kernel(pix_ref, bin_ref, cnt_ref, nd_ref, w_ref, out_ref, up_ref, down_ref, tab_ref, hot_ref, acc_ref):
    a = pl.program_id(0)
    t = lax.axis_index("tile")

    @pl.when(a == 0)
    def _():
        row = lax.broadcasted_iota(jnp.int32, (16, 128), 0)
        for q in range(17):
            hot_ref[q] = jnp.where(row == q, 1.0, 0.0).astype(BF16)
        acc_ref[...] = jnp.zeros_like(acc_ref)

    for b in range(8):
        hi, lo = split(
            jnp.concatenate(
                [jnp.broadcast_to(nd_ref[0, b, z : z + 1, :], (16, 128)) for z in range(4)], 0
            )
        )
        tab_ref[b, 0:64] = hi
        tab_ref[b, 64:128] = lo
    count = cnt_ref[0, a]
    parts = []
    for s in range(12):
        q = jnp.where(s < count, pix_ref[s, 0, a], 16)
        hot = hot_ref[q]
        parts.append(tab_ref[bin_ref[s, t, a]] * jnp.concatenate([hot] * 8, 0))
    left = jnp.concatenate(parts, 1)
    rights = []
    for s in range(12):
        w_hi, w_lo = split(w_ref[0, 0, s])
        rights.append(jnp.concatenate([w_hi, w_lo], 0))
    right = jnp.concatenate(rights, 1)
    acc_ref[...] += lax.dot_general(
        left, right, (((1,), (1,)), ((), ())), preferred_element_type=F32
    )

    @pl.when(a == 15)
    def _():
        d = acc_ref[...]
        res = d[0:64, 0:128] + (d[0:64, 128:256] + d[64:128, 0:128])
        out_ref[...] = res
        for z in range(4):
            up_ref[z * 4 : z * 4 + 4, :] = res[z * 16 : z * 16 + 4]
            down_ref[z * 4 : z * 4 + 4, :] = res[z * 16 + 12 : z * 16 + 16]


def primal_kernel_body(
    sp_ref, sm_ref, prev_ref, next_ref, back_ref, above_ref, below_ref, primal_ref, kern_ref,
    mix_ref, bias_ref, slope_ref, shift_ref, new_ref, tt_ref, tb_ref, x_ref, y_ref,
):
    p = lax.axis_index("plane")
    t = lax.axis_index("tile")
    keeps = (p > 0, None, None, p < 7)
    for plane, src in enumerate((prev_ref, sm_ref, sp_ref, next_ref)):
        for half in range(2):
            v = src[48:64, half * 512 : (half + 1) * 512]
            if keeps[plane] is not None:
                v = jnp.where(keeps[plane], v, 0.0)
            x_ref[plane * 32 + half * 16 : plane * 32 + half * 16 + 16, :] = v
    y_ref[...] = jnp.zeros((32, 512), F32)
    for plane in range(4):
        for row in range(6):
            for col in range(4):
                if row == 0:
                    v = jnp.where(t > 0, above_ref[plane * 4 + col : plane * 4 + col + 1, :], 0.0)
                elif row == 5:
                    v = jnp.where(t < 15, below_ref[plane * 4 + col : plane * 4 + col + 1, :], 0.0)
                else:
                    i = plane * 16 + (row - 1) * 4 + col
                    v = back_ref[i : i + 1, :]
                if keeps[plane] is not None:
                    v = jnp.where(keeps[plane], v, 0.0)
                y_ref[plane * 8 + row : plane * 8 + row + 1, col * 128 : (col + 1) * 128] = v
    tt_ref[...] = jnp.zeros((96, 384), F32)
    tb_ref[...] = jnp.zeros((24, 384), F32)
    for dz in range(3):
        for dr in range(3):
            rows = [
                jnp.concatenate([kern_ref[c, dz, dr, db : db + 1, :] for db in range(3)], 1)
                for c in range(6)
            ]
            block = jnp.concatenate(rows, 0)
            for r in range(4):
                i = dz * 32 + (r + dr) * 5
                tt_ref[i : i + 5, r * 96 : (r + 1) * 96] = block[0:5]
                i = dz * 8 + r + dr
                tb_ref[i : i + 1, r * 96 : (r + 1) * 96] = block[5:6]
    tt = split(tt_ref[...].T)
    tb = split(tb_ref[...].T)
    x_hi, x_lo = split(x_ref[...])
    y_hi, y_lo = split(y_ref[...])
    bias, slope, shift = column(bias_ref, 32), column(slope_ref, 32), column(shift_ref, 5)
    mix = split(jnp.concatenate([mix_ref[...], jnp.zeros((3, 32), F32)], 0))
    for z in range(2):
        rows = slice(z * 32, z * 32 + 96)
        h = dot3(tt, (x_hi[rows], x_lo[rows]), ((1,), (0,)))
        rows = slice(z * 8, z * 8 + 24)
        h = h + dot3(tb, (y_hi[rows], y_lo[rows]), ((1,), (0,)))
        for r in range(4):
            g = shifted_sum([h[r * 96 + i * 32 : r * 96 + (i + 1) * 32] for i in range(3)]) + bias
            g = jnp.where(g > 0, g, slope * g)
            out = dot3(mix, split(g), ((1,), (0,))) + shift
            for c in range(5):
                new_ref[c, z, r : r + 1, :] = out[c : c + 1, :] + primal_ref[c, z, r : r + 1, :]


def call(body, name, outs, in_specs, scratch=(), limit=16 << 20):
    return pl.pallas_call(
        body,
        name=name,
        out_shape=tuple(jax.ShapeDtypeStruct(s, F32) for s in outs),
        in_specs=in_specs,
        out_specs=tuple(VMEM for _ in outs),
        scratch_shapes=list(scratch),
        compiler_params=pltpu.CompilerParams(vmem_limit_bytes=limit),
    )


def ring(array, axis, step):
    count = lax.axis_size(axis)
    return lax.ppermute(array, axis, [(i, (i + step) % count) for i in range(count)])


def per_device(
    primal, dual, measured, footprint_weights, pixel_index, bin_index, slot_count,
    dual_kernel, dual_bias, dual_slope, dual_mixing, dual_shift,
    primal_kernel, primal_bias, primal_slope, primal_mixing, primal_shift,
):
    pix = jnp.transpose(pixel_index, (2, 0, 1))
    bins = jnp.transpose(bin_index, (2, 0, 1))

    own = call(pack_kernel, "pack", [(32, 1024)], [VMEM] * 3)(dual, measured, primal)[0]
    left = ring(own, "tile", 1)
    right = ring(own, "tile", -1)

    w_spec = pl.BlockSpec((1, 1, 12, 128, 128), lambda a: (0, a, 0, 0, 0))
    terms = pl.pallas_call(
        project_kernel,
        name="project",
        grid=(16,),
        out_shape=jax.ShapeDtypeStruct((16, 3, 16, 128), F32),
        in_specs=[SMEM, SMEM, SMEM, VMEM, w_spec],
        out_specs=VMEM,
        scratch_shapes=[pltpu.VMEM((16, 16, 128), BF16)] * 3,
        compiler_params=pltpu.CompilerParams(
            vmem_limit_bytes=16 << 20, dimension_semantics=("arbitrary",)
        ),
    )(pix, bins, slot_count, primal, footprint_weights)
    got = lax.all_to_all(terms, "tile", 0, 0, tiled=True)

    sp, sm = call(assemble_kernel, "assemble", [(64, 1024)] * 2, [VMEM] * 5)(
        got, own, left, right, primal
    )
    prev = ring(sp, "plane", 1)
    after = ring(sm, "plane", -1)

    new_dual, send = call(
        dual_kernel_body, "dual_net", [(5, 2, 1, 1024), (16, 8, 4, 128)],
        [VMEM] * 5 + [SMEM] * 3, [pltpu.VMEM((72, 96), F32)],
    )(
        sp, prev, after, jnp.transpose(dual_kernel, (2, 3, 4, 1, 0)), dual_mixing,
        dual_bias, dual_slope, dual_shift,
    )
    leading = lax.all_to_all(send, "tile", 0, 0, tiled=True)

    back, up, down = pl.pallas_call(
        back_kernel,
        name="back",
        grid=(16,),
        out_shape=(
            jax.ShapeDtypeStruct((64, 128), F32),
            jax.ShapeDtypeStruct((16, 128), F32),
            jax.ShapeDtypeStruct((16, 128), F32),
        ),
        in_specs=[SMEM, SMEM, SMEM, pl.BlockSpec((1, 8, 4, 128), lambda a: (a, 0, 0, 0)), w_spec],
        out_specs=(VMEM, VMEM, VMEM),
        scratch_shapes=[
            pltpu.VMEM((8, 128, 128), BF16),
            pltpu.VMEM((17, 16, 128), BF16),
            pltpu.VMEM((128, 256), F32),
        ],
        compiler_params=pltpu.CompilerParams(
            vmem_limit_bytes=16 << 20, dimension_semantics=("arbitrary",)
        ),
    )(pix, bins, slot_count, leading, footprint_weights)
    above = ring(down, "tile", 1)
    below = ring(up, "tile", -1)

    new_primal = call(
        primal_kernel_body, "primal_net", [(5, 2, 4, 512)], [VMEM] * 10 + [SMEM] * 3,
        [
            pltpu.VMEM((96, 384), F32),
            pltpu.VMEM((24, 384), F32),
            pltpu.VMEM((128, 512), F32),
            pltpu.VMEM((32, 512), F32),
        ],
    )(
        sp, sm, prev, after, back, above, below, primal,
        jnp.transpose(primal_kernel, (1, 2, 3, 4, 0)), primal_mixing,
        primal_bias, primal_slope, primal_shift,
    )[0]
    return new_primal, new_dual


def solution(mesh):
    grid = P(None, "plane", "tile", None)
    in_specs = (
        grid, grid, P("plane", "tile", None), P("tile", None, None, None, None),
        P("tile", None, None), P(), P("tile", None),
    ) + (P(),) * 10
    return jax.shard_map(
        per_device, mesh=mesh, in_specs=in_specs, out_specs=(grid, grid), check_vma=False
    )
```

time: 176 us -> 84.5 us (0.48); the launches traced: 173 us -> 84.1 us
  matrix products: 86.2 us -> 0 us
  Pallas kernels: 0 us -> 22.8 us
  local copies, waits for them, and re-layouts: 21.1 us -> 12.4 us
  waiting for transfers between devices: 22.2 us -> 16.6 us
  other arithmetic: 4.04 us -> 0 us
  blocking collectives: 15.8 us -> 12 us
  starting transfers between devices: 22.5 us -> 19.4 us
    conv_general_dilated x2 -> x0, matrix products: 49.8 us -> none  [network(): lax.conv_general_dilated(padded[None], kernel, (1, 1, 1), 'VALID', dimens...]
    dot_general x6 -> x0, matrix products: 36.4 us -> none  [the longest x1 22 us: per_device(): jnp.einsum('azsk,asjk->azsj', picked, weight_part, precision=HIGHEST)]
    pallas_call x0 -> x6, Pallas kernels: none -> 22.8 us  [the longest x1 9.33 us: per_device(): pl.pallas_call(back_kernel, name='back', grid=(16,), out_shape=(jax.Shape...]
    conv_general_dilated x10 -> x0, local copies, waits for them, and re-layouts: 14.9 us -> none  [network(): lax.conv_general_dilated(padded[None], kernel, (1, 1, 1), 'VALID', dimens...]
    unnamed x38 -> x44, local copies, waits for them, and re-layouts: 1.55 us -> 12.4 us
    all_to_all x1, waiting for transfers between devices: 8.12 us -> 0.01 us  [per_device(): got = lax.all_to_all(terms, 'tile', 0, 0, tiled=True)]
    ppermute x8 -> x6, starting transfers between devices: 15.4 us -> 11.3 us  [ring(): lax.ppermute(array, axis, [(i, (i + step) % count) for i in range(count)])]
    all_to_all x1, blocking collectives: 15.8 us -> 12 us  [per_device(): leading = lax.all_to_all(send, 'tile', 0, 0, tiled=True)]
  transfers between devices with their start and end apart: 9 -> 7, of which waited for: 6 -> 5; matrix products, arithmetic and copies ran while one was open for 0% -> 0% of each run, Pallas kernels for 0% -> 0%
where the time goes in v1:
time: 84.5 us; the launch traced here: 84.1 us
  Pallas kernels  22.8 us (27%)
  starting transfers between devices  19.4 us (23%)
  waiting for transfers between devices  16.6 us (20%)
  local copies, waits for them, and re-layouts  12.4 us (15%)
  blocking collectives  12 us (14%)
  between operations  0.87 us (1%)
    ppermute x6, waiting for transfers between devices, ring(): lax.ppermute(array, axis, [(i, (i + step) % count) for i in range(count)])  16.6 us
    unnamed x44, local copies, waits for them, and re-layouts  12.4 us
    all_to_all x1, blocking collectives, per_device(): leading = lax.all_to_all(send, 'tile', 0, 0, tiled=True)  12 us
    ppermute x6, starting transfers between devices, ring(): lax.ppermute(array, axis, [(i, (i + step) % count) for i in range(count)])  11.3 us
    pallas_call x1, Pallas kernels, per_device(): pl.pallas_call(back_kernel, name='back', grid=(16,), out_shape=(jax.Shape...  9.33 us
    all_to_all x1, starting transfers between devices, per_device(): got = lax.all_to_all(terms, 'tile', 0, 0, tiled=True)  8.18 us
    pallas_call x1, Pallas kernels, per_device(): pl.pallas_call(project_kernel, name='project', grid=(16,), out_shape=jax....  7.03 us
    pallas_call x1, Pallas kernels, per_device(): call(primal_kernel_body, 'primal_net', [(5, 2, 4, 512)], [VMEM] * 10 + [S...  3.48 us
  transfers between devices with their start and end apart: 7, of which 5 were waited for; matrix products, arithmetic and copies ran while one was open for 0% of the time, Pallas kernels for 0%

profile of v1, /device:TPU:0, one launch (start us, length us, event | category | flops | bytes accessed | tf_op | source)
XLA Modules:
  0.0 84.1 jit_solution(12970692158630161838)
XLA Ops:
  0.7 0.0 copy-start
  0.7 4.6 %copy-done = f32[1,16,12,128,128]{4,3,2,1,0:T(8,128)S(1)} copy-done((f32[1,16,12,128,128]{4,3,2,1,0:T(8,128)S(1)}, f32[1,16,12,128,128]{4,3,2,1,0:T(8,128)}, u32[]{:S(2)}) %copy-start) | copy-done | bytes 12582936
  5.3 0.9 %copy-done.2 = f32[5,2,4,512]{3,2,1,0:T(4,128)S(1)} copy-done((f32[5,2,4,512]{3,2,1,0:T(4,128)S(1)}, f32[5,2,4,512]{3,2,1,0:T(4,128)}, u32[]{:S(2)}) %copy-start.2) | copy-done | bytes 81944
  6.2 0.9 %copy-done.4 = s32[16,16,12]{1,0,2:T(8,128)S(1)} copy-done((s32[16,16,12]{1,0,2:T(8,128)S(1)}, s32[16,16,12]{1,0,2:T(8,128)}, u32[]{:S(2)}) %copy-start.4) | copy-done | bytes 12312
  7.1 0.7 copy-done.9
  7.8 0.7 copy-done.14
  8.5 7.0 %project.1 = f32[16,3,16,128]{3,2,1,0:T(8,128)} custom-call(s32[12,1,16]{2,1,0:T(1,128)S(1)} %bitcast.8, s32[12,16,16]{2,1,0:T(8,128)S(1)} %bitcast.4, s32[1,16]{1,0:T(1,128)S(1)} %copy-done.14, f32[5,2,4,512]{3,2,1,0:T(4,128)S(1)} %copy-done.2, f32[1,16,12,128,128]{4,3,2,1,0:T(8,128)S(1)} %copy-done), custom_call_target="tpu_custom_call" | custom-call | tf_op jit(solution)/shard_map/project/pallas_call | solution.py:313
  15.5 8.2 %all-to-all-start = ((f32[16,3,16,128]{3,2,1,0:T(8,128)}), f32[16,3,16,128]{3,2,1,0:T(8,128)S(1)}, u32[]{:S(2)}, u32[]{:S(2)}) async-start(f32[16,3,16,128]{3,2,1,0:T(8,128)} %project.1), calls=%async_computation | async-start | bytes 786432 | tf_op jit(solution)/shard_map/all_to_all | solution.py:325
  23.8 5.3 %collective-permute-start.1 = (f32[32,1024]{1,0:T(8,128)S(1)}, f32[32,1024]{1,0:T(8,128)S(1)}, u32[]{:S(2)}, u32[]{:S(2)}) collective-permute-start(f32[32,1024]{1,0:T(8,128)S(1)} %pack.1.own_ref), channel_id=1, source_target_pairs={{0,15},{1,0},{2,1},{3,2},{4,3},{5,4},{6,5},{7,6},{8,7},{9,8},{10,9... | collective-permute-start | bytes 393224 | tf_op jit(solution)/shard_map/ppermute | solution.py:297
  29.1 3.9 %collective-permute-done.1.right_ref = f32[32,1024]{1,0:T(8,128)S(1)} collective-permute-done((f32[32,1024]{1,0:T(8,128)S(1)}, f32[32,1024]{1,0:T(8,128)S(1)}, u32[]{:S(2)}, u32[]{:S(2)}) %collective-permute-start.1) | collective-permute-done | bytes 131104 | tf_op jit(solution)/shard_map/ppermute | solution.py:297
  33.0 4.4 %collective-permute-done.left_ref = f32[32,1024]{1,0:T(8,128)S(1)} collective-permute-done((f32[32,1024]{1,0:T(8,128)S(1)}, f32[32,1024]{1,0:T(8,128)S(1)}, u32[]{:S(2)}, u32[]{:S(2)}) %collective-permute-start) | collective-permute-done | bytes 131104 | tf_op jit(solution)/shard_map/ppermute | solution.py:297
  37.4 0.1 assemble.1
  37.5 0.2 collective-permute-start.3
  37.7 0.3 collective-permute-start.2
  38.0 3.6 %collective-permute-done.3.next_ref = f32[64,1024]{1,0:T(8,128)S(1)} collective-permute-done((f32[64,1024]{1,0:T(8,128)S(1)}, f32[64,1024]{1,0:T(8,128)S(1)}, u32[]{:S(2)}, u32[]{:S(2)}) %collective-permute-start.3) | collective-permute-done | bytes 262176 | tf_op jit(solution)/shard_map/ppermute | solution.py:297
  41.6 3.1 %collective-permute-done.2.prev_ref = f32[64,1024]{1,0:T(8,128)S(1)} collective-permute-done((f32[64,1024]{1,0:T(8,128)S(1)}, f32[64,1024]{1,0:T(8,128)S(1)}, u32[]{:S(2)}, u32[]{:S(2)}) %collective-permute-start.2) | collective-permute-done | bytes 262176 | tf_op jit(solution)/shard_map/ppermute | solution.py:297
  44.7 2.9 %dual_net.1 = (f32[5,2,1,1024]{3,2,1,0:T(1,128)}, f32[16,8,4,128]{3,2,1,0:T(4,128)S(1)}) custom-call(f32[64,1024]{1,0:T(8,128)S(1)} %get-tuple-element.9.own_ref.sp_ref, f32[64,1024]{1,0:T(8,128)S(1)} %collective-permute-done.2.prev_ref, f32[64,1024]{1,0:T(8,128)S(1)} %collective-permute-done.3.next_ref, f32[3,3,3,7,32]{4,3,2,1,0:T(8,128)S(1)} %bitcast.7, ...), custom_call_target="tpu_custom_call" | custom-call | tf_op jit(solution)/shard_map/dual_net/pallas_call | solution.py:333
  47.6 12.0 %all_to_all.10.nd_ref = f32[16,8,4,128]{3,2,1,0:T(4,128)S(1)} all-to-all(f32[16,8,4,128]{3,2,1,0:T(4,128)S(1)} %get-tuple-element.11), channel_id=1, replica_groups=mesh['plane'=8,'tile'=16] {'tile'}, dimensions={0} | all-to-all | bytes 524288 | tf_op jit(solution)/shard_map/all_to_all | solution.py:340
  59.6 4.6 %copy-done.1 = f32[1,16,12,128,128]{4,3,2,1,0:T(8,128)S(1)} copy-done((f32[1,16,12,128,128]{4,3,2,1,0:T(8,128)S(1)}, f32[1,16,12,128,128]{4,3,2,1,0:T(8,128)}, u32[]{:S(2)}) %copy-start.1) | copy-done | bytes 12582936
  64.2 9.3 %back.1 = (f32[64,128]{1,0:T(8,128)S(1)}, f32[16,128]{1,0:T(8,128)S(1)}, f32[16,128]{1,0:T(8,128)S(1)}) custom-call(s32[12,1,16]{2,1,0:T(1,128)S(1)} %bitcast.9, s32[12,16,16]{2,1,0:T(8,128)S(1)} %bitcast.5, s32[1,16]{1,0:T(1,128)S(1)} %copy-done.15, f32[16,8,4,128]{3,2,1,0:T(4,128)S(1)} %all_to_all.10.nd_ref, f32[1,16,12,128,128]{4,3,2,1,0:T(8,128)S(1)} %copy-done.1), custom_call_target="tpu_custom_call" | custom-call | tf_op jit(solution)/shard_map/back/pallas_call | solution.py:342
  73.5 0.5 collective-permute-start.4
  74.0 4.9 %collective-permute-start.5 = (f32[16,128]{1,0:T(8,128)S(1)}, f32[16,128]{1,0:T(8,128)S(1)}, u32[]{:S(2)}, u32[]{:S(2)}) collective-permute-start(f32[16,128]{1,0:T(8,128)S(1)} %get-tuple-element.14), channel_id=1, source_target_pairs={{0,15},{1,0},{2,1},{3,2},{4,3},{5,4},{6,5},{7,6},{8,7},{9,8},{10,9... | collective-permute-start | bytes 24584 | tf_op jit(solution)/shard_map/ppermute | solution.py:297
  79.0 1.6 %collective-permute-done.4.above_ref = f32[16,128]{1,0:T(8,128)S(1)} collective-permute-done((f32[16,128]{1,0:T(8,128)S(1)}, f32[16,128]{1,0:T(8,128)S(1)}, u32[]{:S(2)}, u32[]{:S(2)}) %collective-permute-start.4) | collective-permute-done | bytes 8224 | tf_op jit(solution)/shard_map/ppermute | solution.py:297
  80.6 3.5 %primal_net.1 = f32[5,2,4,512]{3,2,1,0:T(4,128)} custom-call(f32[64,1024]{1,0:T(8,128)S(1)} %get-tuple-element.9.own_ref.sp_ref, f32[64,1024]{1,0:T(8,128)S(1)} %get-tuple-element.10.sm_ref, f32[64,1024]{1,0:T(8,128)S(1)} %collective-permute-done.2.prev_ref, f32[64,1024]{1,0:T(8,128)S(1)} %collective-permute-done.3.next_ref, ...), custom_call_target="tpu_custom_call" | custom-call | tf_op jit(solution)/shard_map/primal_net/pallas_call | solution.py:365
  (41 shorter events, 0.1 us)
Async XLA Ops:
  0.6 59.0 %copy-start.15 = (s32[1,16]{1,0:T(1,128)S(1)}, s32[1,16]{1,0:T(1,128)}, u32[]{:S(2)}) copy-start(s32[1,16]{1,0:T(1,128)} %cnt_ref.3) | copy-start | bytes 196
  0.6 44.1 %copy-start.18 = (f32[5]{0:T(128)S(1)}, f32[5]{0:T(128)}, u32[]{:S(2)}) copy-start(f32[5]{0:T(128)} %shift_ref.2) | copy-start | bytes 64
  0.7 44.0 %copy-start.17 = (f32[32]{0:T(128)S(1)}, f32[32]{0:T(128)}, u32[]{:S(2)}) copy-start(f32[32]{0:T(128)} %slope_ref.2) | copy-start | bytes 388
  0.7 44.0 %copy-start.16 = (f32[32]{0:T(128)S(1)}, f32[32]{0:T(128)}, u32[]{:S(2)}) copy-start(f32[32]{0:T(128)} %bias_ref.2) | copy-start | bytes 388
  0.7 4.6 %copy-start = (f32[1,16,12,128,128]{4,3,2,1,0:T(8,128)S(1)}, f32[1,16,12,128,128]{4,3,2,1,0:T(8,128)}, u32[]{:S(2)}) copy-start(f32[1,16,12,128,128]{4,3,2,1,0:T(8,128)} %w_ref.3) | copy-start | bytes 37748740
  8.4 15.3 %copy-start.3 = (f32[5,2,4,512]{3,2,1,0:T(4,128)S(1)}, f32[5,2,4,512]{3,2,1,0:T(4,128)}, u32[]{:S(2)}) copy-start(f32[5,2,4,512]{3,2,1,0:T(4,128)} %primal_ref.7) | copy-start | bytes 245764
  8.4 15.3 %copy-start.8 = (f32[5,2,1,1024]{3,2,1,0:T(1,128)S(1)}, f32[5,2,1,1024]{3,2,1,0:T(1,128)}, u32[]{:S(2)}) copy-start(f32[5,2,1,1024]{3,2,1,0:T(1,128)} %dual_ref.1) | copy-start | bytes 122884
  8.4 15.3 %copy-start.11 = (f32[2,1,1024]{2,1,0:T(1,128)S(1)}, f32[2,1,1024]{2,1,0:T(1,128)}, u32[]{:S(2)}) copy-start(f32[2,1,1024]{2,1,0:T(1,128)} %measured_ref.1) | copy-start | bytes 24580
  8.4 36.3 %copy-start.7 = (f32[32,7,3,3,3]{0,1,4,3,2:T(8,128)S(1)}, f32[32,7,3,3,3]{0,1,4,3,2:T(8,128)}, u32[]{:S(2)}) copy-start(f32[32,7,3,3,3]{0,1,4,3,2:T(8,128)} %param.24) | copy-start | bytes 72580
  8.4 36.3 %copy-start.12 = (f32[5,32]{1,0:T(8,128)S(1)}, f32[5,32]{1,0:T(8,128)}, u32[]{:S(2)}) copy-start(f32[5,32]{1,0:T(8,128)} %mix_ref.2) | copy-start | bytes 1924
  8.4 51.2 %copy-start.5 = (s32[16,16,12]{1,0,2:T(8,128)S(1)}, s32[16,16,12]{1,0,2:T(8,128)}, u32[]{:S(2)}) copy-start(s32[16,16,12]{1,0,2:T(8,128)} %param.22) | copy-start | bytes 36868
  8.4 51.2 %copy-start.10 = (s32[1,16,12]{1,0,2:T(1,128)S(1)}, s32[1,16,12]{1,0,2:T(1,128)}, u32[]{:S(2)}) copy-start(s32[1,16,12]{1,0,2:T(1,128)} %param.21) | copy-start | bytes 2308
  8.4 72.1 %copy-start.6 = (f32[32,6,3,3,3]{0,4,3,2,1:T(4,128)S(1)}, f32[32,6,3,3,3]{0,4,3,2,1:T(4,128)}, u32[]{:S(2)}) copy-start(f32[32,6,3,3,3]{0,4,3,2,1:T(4,128)} %param.29) | copy-start | bytes 62212
  8.5 72.1 %copy-start.13 = (f32[5,32]{1,0:T(8,128)S(1)}, f32[5,32]{1,0:T(8,128)}, u32[]{:S(2)}) copy-start(f32[5,32]{1,0:T(8,128)} %mix_ref.3) | copy-start | bytes 1924
  8.5 72.1 %copy-start.19 = (f32[32]{0:T(128)S(1)}, f32[32]{0:T(128)}, u32[]{:S(2)}) copy-start(f32[32]{0:T(128)} %bias_ref.3) | copy-start | bytes 388
  8.5 72.1 %copy-start.20 = (f32[32]{0:T(128)S(1)}, f32[32]{0:T(128)}, u32[]{:S(2)}) copy-start(f32[32]{0:T(128)} %slope_ref.3) | copy-start | bytes 388
  8.5 72.1 %copy-start.21 = (f32[5]{0:T(128)S(1)}, f32[5]{0:T(128)}, u32[]{:S(2)}) copy-start(f32[5]{0:T(128)} %shift_ref.3) | copy-start | bytes 64
  15.5 21.9 %all-to-all-start = ((f32[16,3,16,128]{3,2,1,0:T(8,128)}), f32[16,3,16,128]{3,2,1,0:T(8,128)S(1)}, u32[]{:S(2)}, u32[]{:S(2)}) async-start(f32[16,3,16,128]{3,2,1,0:T(8,128)} %project.1), calls=%async_computation | async-start | bytes 786432 | tf_op jit(solution)/shard_map/all_to_all | solution.py:325
  23.8 9.2 %collective-permute-start.1 = (f32[32,1024]{1,0:T(8,128)S(1)}, f32[32,1024]{1,0:T(8,128)S(1)}, u32[]{:S(2)}, u32[]{:S(2)}) collective-permute-start(f32[32,1024]{1,0:T(8,128)S(1)} %pack.1.own_ref), channel_id=1, source_target_pairs={{0,15},{1,0},{2,1},{3,2},{4,3},{5,4},{6,5},{7,6},{8,7},{9,8},{10,9... | collective-permute-start | bytes 393224 | tf_op jit(solution)/shard_map/ppermute | solution.py:297
  29.1 8.3 %collective-permute-start = (f32[32,1024]{1,0:T(8,128)S(1)}, f32[32,1024]{1,0:T(8,128)S(1)}, u32[]{:S(2)}, u32[]{:S(2)}) collective-permute-start(f32[32,1024]{1,0:T(8,128)S(1)} %pack.1.own_ref), channel_id=1, source_target_pairs={{0,1},{1,2},{2,3},{3,4},{4,5},{5,6},{6,7},{7,8},{8,9},{9,10},{10,1... | collective-permute-start | bytes 393224 | tf_op jit(solution)/shard_map/ppermute | solution.py:297
  37.5 4.1 %collective-permute-start.3 = (f32[64,1024]{1,0:T(8,128)S(1)}, f32[64,1024]{1,0:T(8,128)S(1)}, u32[]{:S(2)}, u32[]{:S(2)}) collective-permute-start(f32[64,1024]{1,0:T(8,128)S(1)} %get-tuple-element.10.sm_ref), channel_id=1, source_target_pairs={{0,112},{16,0},{32,16},{48,32},{64,48},{80,64},{96,80},{112,96},{1... | collective-permute-start | bytes 786440 | tf_op jit(solution)/shard_map/ppermute | solution.py:297
  37.7 7.0 %collective-permute-start.2 = (f32[64,1024]{1,0:T(8,128)S(1)}, f32[64,1024]{1,0:T(8,128)S(1)}, u32[]{:S(2)}, u32[]{:S(2)}) collective-permute-start(f32[64,1024]{1,0:T(8,128)S(1)} %get-tuple-element.9.own_ref.sp_ref), channel_id=1, source_target_pairs={{0,16},{16,32},{32,48},{48,64},{64,80},{80,96},{96,112},{112,0},{1... | collective-permute-start | bytes 786440 | tf_op jit(solution)/shard_map/ppermute | solution.py:297
  73.5 7.0 %collective-permute-start.4 = (f32[16,128]{1,0:T(8,128)S(1)}, f32[16,128]{1,0:T(8,128)S(1)}, u32[]{:S(2)}, u32[]{:S(2)}) collective-permute-start(f32[16,128]{1,0:T(8,128)S(1)} %get-tuple-element.13), channel_id=1, source_target_pairs={{0,1},{1,2},{2,3},{3,4},{4,5},{5,6},{6,7},{7,8},{8,9},{9,10},{10,1... | collective-permute-start | bytes 24584 | tf_op jit(solution)/shard_map/ppermute | solution.py:297
  74.0 6.5 %collective-permute-start.5 = (f32[16,128]{1,0:T(8,128)S(1)}, f32[16,128]{1,0:T(8,128)S(1)}, u32[]{:S(2)}, u32[]{:S(2)}) collective-permute-start(f32[16,128]{1,0:T(8,128)S(1)} %get-tuple-element.14), channel_id=1, source_target_pairs={{0,15},{1,0},{2,1},{3,2},{4,3},{5,4},{6,5},{7,6},{8,7},{9,8},{10,9... | collective-permute-start | bytes 24584 | tf_op jit(solution)/shard_map/ppermute | solution.py:297
  (5 other events, 7.7 us)

commit v2 on v1

--- a/solution.py
+++ b/solution.py
@@ -7,10 +7,12 @@
 from jax.experimental.pallas import tpu as pltpu
 from jax.sharding import PartitionSpec as P
 
+
 F32 = jnp.float32
 BF16 = jnp.bfloat16
 VMEM = pl.BlockSpec(memory_space=pltpu.VMEM)
 SMEM = pl.BlockSpec(memory_space=pltpu.SMEM)
+HBM = pl.BlockSpec(memory_space=pltpu.HBM)
 
 
 def split(x):
@@ -44,7 +46,17 @@
     return left + mid + right
 
 
-def pack_kernel(dual_ref, measured_ref, primal_ref, out_ref):
+def pack_kernel(dual_hbm, measured_hbm, primal_hbm, out_ref, dual_ref, measured_ref, primal_ref, sem):
+    copies = [
+        pltpu.make_async_copy(src, dst, sem.at[i])
+        for i, (src, dst) in enumerate(
+            ((dual_hbm, dual_ref), (measured_hbm, measured_ref), (primal_hbm, primal_ref))
+        )
+    ]
+    for copy in copies:
+        copy.start()
+    for copy in copies:
+        copy.wait()
     zero = jnp.zeros((1, 1024), F32)
     for z in range(2):
         for c in range(5):
@@ -60,49 +72,78 @@
     out_ref[26:32, :] = jnp.zeros((6, 1024), F32)
 
 
-def project_kernel(pix_ref, bin_ref, cnt_ref, primal_ref, w_ref, out_ref, hi_ref, lo_ref, hot_ref):
-    a = pl.program_id(0)
+def project_kernel(
+    pix_hbm, bin_hbm, cnt_hbm, primal_hbm, w_hbm, after_ref,
+    out_ref, wh_ref, wl_ref,
+    hi_ref, lo_ref, hot_ref, pix_ref, bin_ref, cnt_ref, primal_ref, w_ref, sem, w_sem,
+):
+    del after_ref
     t = lax.axis_index("tile")
-
-    @pl.when(a == 0)
-    def _():
-        for q in range(16):
-            r, col = q // 4, (q % 4) * 128
-            v = jnp.concatenate(
-                [
-                    jnp.broadcast_to(primal_ref[1, z, r : r + 1, col : col + 128], (8, 128))
-                    for z in range(2)
-                ],
-                0,
+    copies = [
+        pltpu.make_async_copy(src, dst, sem.at[i])
+        for i, (src, dst) in enumerate(
+            (
+                (primal_hbm.at[1], primal_ref),
+                (pix_hbm, pix_ref),
+                (bin_hbm.at[:, pl.ds(t, 1), :], bin_ref),
+                (cnt_hbm, cnt_ref),
             )
-            hi_ref[q], lo_ref[q] = split(v)
-        row = lax.broadcasted_iota(jnp.int32, (16, 128), 0)
-        for b in range(9):
-            hot_ref[b] = jnp.where((row & 7) == b, 1.0, 0.0).astype(BF16)
-        out_ref[0, 0] = jnp.zeros((16, 128), F32)
-        out_ref[15, 2] = jnp.zeros((16, 128), F32)
-
-    count = cnt_ref[0, a]
-    parts = []
-    for s in range(12):
-        q = pix_ref[s, 0, a]
-        b = jnp.where(s < count, bin_ref[s, t, a], 8)
-        hot = hot_ref[b]
-        parts.append(jnp.concatenate([hi_ref[q] * hot, lo_ref[q] * hot], 0))
-    left = jnp.concatenate(parts, 1)
-    w_hi, w_lo = split(w_ref[0, 0].reshape(12 * 128, 128))
-    right = jnp.concatenate([w_hi, w_lo], 1)
-    d = jnp.dot(left, right, preferred_element_type=F32)
-    res = d[0:16, 0:128] + (d[0:16, 128:256] + d[16:32, 0:128])
-    out_ref[a, 1] = res
-
-    @pl.when(a > 0)
-    def _():
-        out_ref[jnp.maximum(a - 1, 0), 2] = res
-
-    @pl.when(a < 15)
-    def _():
-        out_ref[jnp.minimum(a + 1, 15), 0] = res
+        )
+    ]
+    for copy in copies:
+        copy.start()
+
+    def fetch(a):
+        return pltpu.make_async_copy(w_hbm.at[0, a], w_ref.at[a], w_sem.at[a])
+
+    for a in range(16):
+        fetch(a).start()
+    row = lax.broadcasted_iota(jnp.int32, (16, 128), 0)
+    for b in range(9):
+        hot_ref[b] = jnp.where((row & 7) == b, 1.0, 0.0).astype(BF16)
+    out_ref[0, 0] = jnp.zeros((16, 128), F32)
+    out_ref[15, 2] = jnp.zeros((16, 128), F32)
+    for copy in copies:
+        copy.wait()
+    for q in range(16):
+        r, col = q // 4, (q % 4) * 128
+        v = jnp.concatenate(
+            [
+                jnp.broadcast_to(primal_ref[z, r : r + 1, col : col + 128], (8, 128))
+                for z in range(2)
+            ],
+            0,
+        )
+        hi_ref[q], lo_ref[q] = split(v)
+
+    def angle(a, carry):
+        count = cnt_ref[0, a]
+        parts = []
+        for s in range(12):
+            q = pix_ref[s, 0, a]
+            b = jnp.where(s < count, bin_ref[s, 0, a], 8)
+            hot = hot_ref[b]
+            parts.append(jnp.concatenate([hi_ref[q] * hot, lo_ref[q] * hot], 0))
+        left = jnp.concatenate(parts, 1)
+        fetch(a).wait()
+        w_hi, w_lo = split(w_ref[a].reshape(12 * 128, 128))
+        wh_ref[a], wl_ref[a] = w_hi, w_lo
+        right = jnp.concatenate([w_hi, w_lo], 1)
+        d = jnp.dot(left, right, preferred_element_type=F32)
+        res = d[0:16, 0:128] + (d[0:16, 128:256] + d[16:32, 0:128])
+        out_ref[a, 1] = res
+
+        @pl.when(a > 0)
+        def _():
+            out_ref[jnp.maximum(a - 1, 0), 2] = res
+
+        @pl.when(a < 15)
+        def _():
+            out_ref[jnp.minimum(a + 1, 15), 0] = res
+
+        return carry
+
+    lax.fori_loop(0, 16, angle, 0)
 
 
 def assemble_kernel(got_ref, own_ref, left_ref, right_ref, primal_ref, sp_ref, sm_ref):
@@ -175,7 +216,10 @@
             send_ref[:, b, z, :] = piece
 
 
-def back_kernel(pix_ref, bin_ref, cnt_ref, nd_ref, w_ref, out_ref, up_ref, down_ref, tab_ref, hot_ref, acc_ref):
+def back_kernel(
+    pix_ref, bin_ref, cnt_ref, nd_ref, wh_ref, wl_ref,
+    out_ref, up_ref, down_ref, tab_ref, hot_ref, acc_ref,
+):
     a = pl.program_id(0)
     t = lax.axis_index("tile")
 
@@ -189,7 +233,7 @@
     for b in range(8):
         hi, lo = split(
             jnp.concatenate(
-                [jnp.broadcast_to(nd_ref[0, b, z : z + 1, :], (16, 128)) for z in range(4)], 0
+                [jnp.broadcast_to(nd_ref[a, b, z : z + 1, :], (16, 128)) for z in range(4)], 0
             )
         )
         tab_ref[b, 0:64] = hi
@@ -201,11 +245,13 @@
         hot = hot_ref[q]
         parts.append(tab_ref[bin_ref[s, t, a]] * jnp.concatenate([hot] * 8, 0))
     left = jnp.concatenate(parts, 1)
-    rights = []
-    for s in range(12):
-        w_hi, w_lo = split(w_ref[0, 0, s])
-        rights.append(jnp.concatenate([w_hi, w_lo], 0))
-    right = jnp.concatenate(rights, 1)
+    right = jnp.concatenate(
+        [
+            jnp.concatenate([w[a, s * 128 : (s + 1) * 128, :] for s in range(12)], 1)
+            for w in (wh_ref, wl_ref)
+        ],
+        0,
+    )
     acc_ref[...] += lax.dot_general(
         left, right, (((1,), (1,)), ((), ())), preferred_element_type=F32
     )
@@ -280,10 +326,9 @@
                 new_ref[c, z, r : r + 1, :] = out[c : c + 1, :] + primal_ref[c, z, r : r + 1, :]
 
 
-def call(body, name, outs, in_specs, scratch=(), limit=16 << 20):
+def call(body, outs, in_specs, scratch=(), limit=8 << 20):
     return pl.pallas_call(
         body,
-        name=name,
         out_shape=tuple(jax.ShapeDtypeStruct(s, F32) for s in outs),
         in_specs=in_specs,
         out_specs=tuple(VMEM for _ in outs),
@@ -304,34 +349,52 @@
 ):
     pix = jnp.transpose(pixel_index, (2, 0, 1))
     bins = jnp.transpose(bin_index, (2, 0, 1))
-
-    own = call(pack_kernel, "pack", [(32, 1024)], [VMEM] * 3)(dual, measured, primal)[0]
+    hbm = lambda x: pltpu.with_memory_space_constraint(x, pltpu.HBM)
+
+    own = call(
+        pack_kernel, [(32, 1024)], [HBM] * 3,
+        [
+            pltpu.VMEM((5, 2, 1, 1024), F32),
+            pltpu.VMEM((2, 1, 1024), F32),
+            pltpu.VMEM((5, 2, 4, 512), F32),
+            pltpu.SemaphoreType.DMA((3,)),
+        ],
+    )(hbm(dual), hbm(measured), hbm(primal))[0]
     left = ring(own, "tile", 1)
     right = ring(own, "tile", -1)
 
-    w_spec = pl.BlockSpec((1, 1, 12, 128, 128), lambda a: (0, a, 0, 0, 0))
-    terms = pl.pallas_call(
+    terms, w_hi, w_lo = pl.pallas_call(
         project_kernel,
         name="project",
-        grid=(16,),
-        out_shape=jax.ShapeDtypeStruct((16, 3, 16, 128), F32),
-        in_specs=[SMEM, SMEM, SMEM, VMEM, w_spec],
-        out_specs=VMEM,
-        scratch_shapes=[pltpu.VMEM((16, 16, 128), BF16)] * 3,
-        compiler_params=pltpu.CompilerParams(
-            vmem_limit_bytes=16 << 20, dimension_semantics=("arbitrary",)
+        out_shape=(
+            jax.ShapeDtypeStruct((16, 3, 16, 128), F32),
+            jax.ShapeDtypeStruct((16, 1536, 128), BF16),
+            jax.ShapeDtypeStruct((16, 1536, 128), BF16),
         ),
-    )(pix, bins, slot_count, primal, footprint_weights)
+        in_specs=[HBM] * 5 + [VMEM],
+        out_specs=(VMEM, VMEM, VMEM),
+        scratch_shapes=[pltpu.VMEM((16, 16, 128), BF16)] * 3
+        + [
+            pltpu.SMEM((12, 1, 16), jnp.int32),
+            pltpu.SMEM((12, 1, 16), jnp.int32),
+            pltpu.SMEM((1, 16), jnp.int32),
+            pltpu.VMEM((2, 4, 512), F32),
+            pltpu.VMEM((16, 12, 128, 128), F32),
+            pltpu.SemaphoreType.DMA((4,)),
+            pltpu.SemaphoreType.DMA((16,)),
+        ],
+        compiler_params=pltpu.CompilerParams(vmem_limit_bytes=18 << 20),
+        cost_estimate=pl.CostEstimate(flops=1 << 31, bytes_accessed=25 << 20, transcendentals=0),
+    )(hbm(pix), hbm(bins), hbm(slot_count), hbm(primal), hbm(footprint_weights), own)
+    terms, left, right = lax.optimization_barrier((terms, left, right))
     got = lax.all_to_all(terms, "tile", 0, 0, tiled=True)
 
-    sp, sm = call(assemble_kernel, "assemble", [(64, 1024)] * 2, [VMEM] * 5)(
-        got, own, left, right, primal
-    )
+    sp, sm = call(assemble_kernel, [(64, 1024)] * 2, [VMEM] * 5)(got, own, left, right, primal)
     prev = ring(sp, "plane", 1)
     after = ring(sm, "plane", -1)
 
     new_dual, send = call(
-        dual_kernel_body, "dual_net", [(5, 2, 1, 1024), (16, 8, 4, 128)],
+        dual_kernel_body, [(5, 2, 1, 1024), (16, 8, 4, 128)],
         [VMEM] * 5 + [SMEM] * 3, [pltpu.VMEM((72, 96), F32)],
     )(
         sp, prev, after, jnp.transpose(dual_kernel, (2, 3, 4, 1, 0)), dual_mixing,
@@ -348,7 +411,7 @@
             jax.ShapeDtypeStruct((16, 128), F32),
             jax.ShapeDtypeStruct((16, 128), F32),
         ),
-        in_specs=[SMEM, SMEM, SMEM, pl.BlockSpec((1, 8, 4, 128), lambda a: (a, 0, 0, 0)), w_spec],
+        in_specs=[SMEM, SMEM, SMEM, VMEM, VMEM, VMEM],
         out_specs=(VMEM, VMEM, VMEM),
         scratch_shapes=[
             pltpu.VMEM((8, 128, 128), BF16),
@@ -356,14 +419,14 @@
             pltpu.VMEM((128, 256), F32),
         ],
         compiler_params=pltpu.CompilerParams(
-            vmem_limit_bytes=16 << 20, dimension_semantics=("arbitrary",)
+            vmem_limit_bytes=4 << 20, dimension_semantics=("arbitrary",)
         ),
-    )(pix, bins, slot_count, leading, footprint_weights)
+    )(pix, bins, slot_count, leading, w_hi, w_lo)
     above = ring(down, "tile", 1)
     below = ring(up, "tile", -1)
 
     new_primal = call(
-        primal_kernel_body, "primal_net", [(5, 2, 4, 512)], [VMEM] * 10 + [SMEM] * 3,
+        primal_kernel_body, [(5, 2, 4, 512)], [VMEM] * 10 + [SMEM] * 3,
         [
             pltpu.VMEM((96, 384), F32),
             pltpu.VMEM((24, 384), F32),

time: 84.5 us -> 75.1 us (0.89)
  blocking collectives: 12 us -> 28 us
  local copies, waits for them, and re-layouts: 12.4 us -> 0.08 us
  waiting for transfers between devices: 16.6 us -> 8.36 us
  starting transfers between devices: 19.4 us -> 12.6 us
  Pallas kernels: 22.8 us -> 25 us
    all_to_all x0 -> x1, blocking collectives: none -> 15.8 us  [per_device(): got = lax.all_to_all(terms, 'tile', 0, 0, tiled=True)]
    unnamed x44 -> x28, local copies, waits for them, and re-layouts: 12.4 us -> 0.08 us
    ppermute x6, waiting for transfers between devices: 16.6 us -> 8.36 us  [ring(): lax.ppermute(array, axis, [(i, (i + step) % count) for i in range(count)])]
    all_to_all x1 -> x0, starting transfers between devices: 8.18 us -> none  [per_device(): got = lax.all_to_all(terms, 'tile', 0, 0, tiled=True)]
    pallas_call x5, Pallas kernels: 13.5 us -> 15.9 us  [the longest x1 8.49 us: per_device(): pl.pallas_call(project_kernel, name='project', out_shape=(jax.ShapeDtypeS...]
    ppermute x6, starting transfers between devices: 11.3 us -> 12.6 us  [ring(): lax.ppermute(array, axis, [(i, (i + step) % count) for i in range(count)])]
  transfers between devices with their start and end apart: 7 -> 6, of which waited for: 5 -> 3; matrix products, arithmetic and copies ran while one was open for 0% -> 0% of each run, Pallas kernels for 0% -> 11%
where the time goes in v2:
time: 75.1 us; the launch traced here: 74.9 us
  blocking collectives  28 us (37%)
  Pallas kernels  25 us (33%)
  starting transfers between devices  12.6 us (17%)
  waiting for transfers between devices  8.36 us (11%)
  between operations  0.83 us (1%)
    all_to_all x1, blocking collectives, per_device(): got = lax.all_to_all(terms, 'tile', 0, 0, tiled=True)  15.8 us
    ppermute x6, starting transfers between devices, ring(): lax.ppermute(array, axis, [(i, (i + step) % count) for i in range(count)])  12.6 us
    all_to_all x1, blocking collectives, per_device(): leading = lax.all_to_all(send, 'tile', 0, 0, tiled=True)  12.2 us
    pallas_call x1, Pallas kernels, per_device(): pl.pallas_call(back_kernel, name='back', grid=(16,), out_shape=(jax.Shape...  9.04 us
    pallas_call x1, Pallas kernels, per_device(): pl.pallas_call(project_kernel, name='project', out_shape=(jax.ShapeDtypeS...  8.49 us
    ppermute x6, waiting for transfers between devices, ring(): lax.ppermute(array, axis, [(i, (i + step) % count) for i in range(count)])  8.36 us
    pallas_call x1, Pallas kernels, per_device(): call(primal_kernel_body, [(5, 2, 4, 512)], [VMEM] * 10 + [SMEM] * 3, [plt...  3.48 us
    pallas_call x1, Pallas kernels, per_device(): call(dual_kernel_body, [(5, 2, 1, 1024), (16, 8, 4, 128)], [VMEM] * 5 + [...  2.89 us
  transfers between devices with their start and end apart: 6, of which 3 were waited for; matrix products, arithmetic and copies ran while one was open for 0% of the time, Pallas kernels for 11%

profile of v2, /device:TPU:0, one launch (start us, length us, event | category | flops | bytes accessed | tf_op | source)
XLA Modules:
  0.0 74.9 jit_solution(18001808974116328300)
XLA Ops:
  0.6 1.0 %shard_map.176.after_ref.own_ref = f32[32,1024]{1,0:T(8,128)S(1)} custom-call(f32[5,2,1,1024]{3,2,1,0:T(1,128)} %dual_hbm.1, f32[2,1,1024]{2,1,0:T(1,128)} %measured_hbm.1, f32[5,2,4,512]{3,2,1,0:T(4,128)} %primal_ref.3), custom_call_target="tpu_custom_call" | custom-call | tf_op jit(solution)/shard_map/pallas_call | solution.py:354
  1.6 6.7 %collective-permute-start.1 = (f32[32,1024]{1,0:T(8,128)S(1)}, f32[32,1024]{1,0:T(8,128)S(1)}, u32[]{:S(2)}, u32[]{:S(2)}) collective-permute-start(f32[32,1024]{1,0:T(8,128)S(1)} %shard_map.176.after_ref.own_ref), channel_id=1, source_target_pairs={{0,15},{1,0},{2,1},{3,2},{4,3},{5,4},{6,5},{7,6},{8,7},{9,8},{10,9... | collective-permute-start | bytes 393224 | tf_op jit(solution)/shard_map/ppermute | solution.py:342
  8.3 0.0 copy-start.8
  8.3 0.0 copy-start.9
  8.3 0.0 copy-start.10
  8.3 0.0 copy-start.1
  8.3 0.0 copy-start.4
  8.4 8.5 %project.1 = (f32[16,3,16,128]{3,2,1,0:T(8,128)S(1)}, bf16[16,1536,128]{2,1,0:T(8,128)(2,1)S(1)}, bf16[16,1536,128]{2,1,0:T(8,128)(2,1)S(1)}) custom-call(s32[12,1,16]{2,1,0:T(1,128)} %bitcast.8, s32[12,16,16]{2,1,0:T(8,128)} %bitcast.4, s32[1,16]{1,0:T(1,128)} %cnt_ref.1, f32[5,2,4,512]{3,2,1,0:T(4,128)} %primal_ref.3, f32[1,16,12,128,128]{4,3,2,1,0:T(8,128)} %w_hbm.1, ...), custom_call_target="tpu_custom_call" | custom-call | flops 2147483648 | bytes 26214400 | tf_op jit(solution)/shard_map/project/pallas_call | solution.py:366
  16.9 15.8 %all_to_all.10.got_ref = f32[16,3,16,128]{3,2,1,0:T(8,128)S(1)} all-to-all(f32[16,3,16,128]{3,2,1,0:T(8,128)S(1)} %get-tuple-element.16), channel_id=1, replica_groups=mesh['plane'=8,'tile'=16] {'tile'}, dimensions={0} | all-to-all | bytes 786432 | tf_op jit(solution)/shard_map/all_to_all | solution.py:390
  32.7 0.1 shard_map.177
  32.8 0.2 collective-permute-start.3
  33.0 0.3 collective-permute-start.2
  33.3 3.6 %collective-permute-done.3.next_ref = f32[64,1024]{1,0:T(8,128)S(1)} collective-permute-done((f32[64,1024]{1,0:T(8,128)S(1)}, f32[64,1024]{1,0:T(8,128)S(1)}, u32[]{:S(2)}, u32[]{:S(2)}) %collective-permute-start.3) | collective-permute-done | bytes 262176 | tf_op jit(solution)/shard_map/ppermute | solution.py:342
  36.9 3.1 %collective-permute-done.2.prev_ref = f32[64,1024]{1,0:T(8,128)S(1)} collective-permute-done((f32[64,1024]{1,0:T(8,128)S(1)}, f32[64,1024]{1,0:T(8,128)S(1)}, u32[]{:S(2)}, u32[]{:S(2)}) %collective-permute-start.2) | collective-permute-done | bytes 262176 | tf_op jit(solution)/shard_map/ppermute | solution.py:342
  40.1 2.9 %shard_map.178 = (f32[5,2,1,1024]{3,2,1,0:T(1,128)}, f32[16,8,4,128]{3,2,1,0:T(4,128)S(1)}) custom-call(f32[64,1024]{1,0:T(8,128)S(1)} %get-tuple-element.19.own_ref.sp_ref, f32[64,1024]{1,0:T(8,128)S(1)} %collective-permute-done.2.prev_ref, f32[64,1024]{1,0:T(8,128)S(1)} %collective-permute-done.3.next_ref, f32[3,3,3,7,32]{4,3,2,1,0:T(8,128)S(1)} %bitcast.7, ...), custom_call_target="tpu_custom_call" | custom-call | tf_op jit(solution)/shard_map/pallas_call | solution.py:396
  42.9 12.2 %all_to_all.11.nd_ref = f32[16,8,4,128]{3,2,1,0:T(4,128)S(1)} all-to-all(f32[16,8,4,128]{3,2,1,0:T(4,128)S(1)} %get-tuple-element.21), channel_id=1, replica_groups=mesh['plane'=8,'tile'=16] {'tile'}, dimensions={0} | all-to-all | bytes 524288 | tf_op jit(solution)/shard_map/all_to_all | solution.py:403
  55.2 0.0 copy-start.6
  55.2 0.0 copy-start.11
  55.2 0.0 copy-start.13
  55.3 9.0 %back.1 = (f32[64,128]{1,0:T(8,128)S(1)}, f32[16,128]{1,0:T(8,128)S(1)}, f32[16,128]{1,0:T(8,128)S(1)}) custom-call(s32[12,1,16]{2,1,0:T(1,128)S(1)} %bitcast.9, s32[12,16,16]{2,1,0:T(8,128)S(1)} %bitcast.5, s32[1,16]{1,0:T(1,128)S(1)} %copy-done.7, f32[16,8,4,128]{3,2,1,0:T(4,128)S(1)} %all_to_all.11.nd_ref, ...), custom_call_target="tpu_custom_call" | custom-call | tf_op jit(solution)/shard_map/back/pallas_call | solution.py:405
  64.3 0.5 collective-permute-start.4
  64.8 4.9 %collective-permute-start.5 = (f32[16,128]{1,0:T(8,128)S(1)}, f32[16,128]{1,0:T(8,128)S(1)}, u32[]{:S(2)}, u32[]{:S(2)}) collective-permute-start(f32[16,128]{1,0:T(8,128)S(1)} %get-tuple-element.26), channel_id=1, source_target_pairs={{0,15},{1,0},{2,1},{3,2},{4,3},{5,4},{6,5},{7,6},{8,7},{9,8},{10,9... | collective-permute-start | bytes 24584 | tf_op jit(solution)/shard_map/ppermute | solution.py:342
  69.7 1.6 %collective-permute-done.4.above_ref = f32[16,128]{1,0:T(8,128)S(1)} collective-permute-done((f32[16,128]{1,0:T(8,128)S(1)}, f32[16,128]{1,0:T(8,128)S(1)}, u32[]{:S(2)}, u32[]{:S(2)}) %collective-permute-start.4) | collective-permute-done | bytes 8224 | tf_op jit(solution)/shard_map/ppermute | solution.py:342
  71.4 3.5 %shard_map.179 = f32[5,2,4,512]{3,2,1,0:T(4,128)} custom-call(f32[64,1024]{1,0:T(8,128)S(1)} %get-tuple-element.19.own_ref.sp_ref, f32[64,1024]{1,0:T(8,128)S(1)} %get-tuple-element.20.sm_ref, f32[64,1024]{1,0:T(8,128)S(1)} %collective-permute-done.2.prev_ref, f32[64,1024]{1,0:T(8,128)S(1)} %collective-permute-done.3.next_ref, ...), custom_call_target="tpu_custom_call" | custom-call | tf_op jit(solution)/shard_map/pallas_call | solution.py:428
  (24 shorter events, 0.1 us)
Async XLA Ops:
  1.6 15.3 %collective-permute-start.1 = (f32[32,1024]{1,0:T(8,128)S(1)}, f32[32,1024]{1,0:T(8,128)S(1)}, u32[]{:S(2)}, u32[]{:S(2)}) collective-permute-start(f32[32,1024]{1,0:T(8,128)S(1)} %shard_map.176.after_ref.own_ref), channel_id=1, source_target_pairs={{0,15},{1,0},{2,1},{3,2},{4,3},{5,4},{6,5},{7,6},{8,7},{9,8},{10,9... | collective-permute-start | bytes 393224 | tf_op jit(solution)/shard_map/ppermute | solution.py:342
  8.3 8.6 %collective-permute-start = (f32[32,1024]{1,0:T(8,128)S(1)}, f32[32,1024]{1,0:T(8,128)S(1)}, u32[]{:S(2)}, u32[]{:S(2)}) collective-permute-start(f32[32,1024]{1,0:T(8,128)S(1)} %shard_map.176.after_ref.own_ref), channel_id=1, source_target_pairs={{0,1},{1,2},{2,3},{3,4},{4,5},{5,6},{6,7},{7,8},{8,9},{9,10},{10,1... | collective-permute-start | bytes 393224 | tf_op jit(solution)/shard_map/ppermute | solution.py:342
  8.3 24.4 %copy-start = (f32[5,2,4,512]{3,2,1,0:T(4,128)S(1)}, f32[5,2,4,512]{3,2,1,0:T(4,128)}, u32[]{:S(2)}) copy-start(f32[5,2,4,512]{3,2,1,0:T(4,128)} %primal_ref.3) | copy-start | bytes 245764
  8.3 31.7 %copy-start.3 = (f32[32,7,3,3,3]{0,1,4,3,2:T(8,128)S(1)}, f32[32,7,3,3,3]{0,1,4,3,2:T(8,128)}, u32[]{:S(2)}) copy-start(f32[32,7,3,3,3]{0,1,4,3,2:T(8,128)} %param.24) | copy-start | bytes 72580
  8.3 31.7 %copy-start.5 = (f32[5,32]{1,0:T(8,128)S(1)}, f32[5,32]{1,0:T(8,128)}, u32[]{:S(2)}) copy-start(f32[5,32]{1,0:T(8,128)} %mix_ref.2) | copy-start | bytes 1924
  8.3 31.7 %copy-start.8 = (f32[32]{0:T(128)S(1)}, f32[32]{0:T(128)}, u32[]{:S(2)}) copy-start(f32[32]{0:T(128)} %bias_ref.2) | copy-start | bytes 388
  8.3 31.7 %copy-start.9 = (f32[32]{0:T(128)S(1)}, f32[32]{0:T(128)}, u32[]{:S(2)}) copy-start(f32[32]{0:T(128)} %slope_ref.2) | copy-start | bytes 388
  8.3 31.7 %copy-start.10 = (f32[5]{0:T(128)S(1)}, f32[5]{0:T(128)}, u32[]{:S(2)}) copy-start(f32[5]{0:T(128)} %shift_ref.2) | copy-start | bytes 64
  8.3 46.9 %copy-start.1 = (s32[16,16,12]{1,0,2:T(8,128)S(1)}, s32[16,16,12]{1,0,2:T(8,128)}, u32[]{:S(2)}) copy-start(s32[16,16,12]{1,0,2:T(8,128)} %param.22) | copy-start | bytes 36868
  8.3 46.8 %copy-start.4 = (s32[1,16,12]{1,0,2:T(1,128)S(1)}, s32[1,16,12]{1,0,2:T(1,128)}, u32[]{:S(2)}) copy-start(s32[1,16,12]{1,0,2:T(1,128)} %param.21) | copy-start | bytes 2308
  8.4 46.8 %copy-start.7 = (s32[1,16]{1,0:T(1,128)S(1)}, s32[1,16]{1,0:T(1,128)}, u32[]{:S(2)}) copy-start(s32[1,16]{1,0:T(1,128)} %cnt_ref.1) | copy-start | bytes 196
  32.8 4.1 %collective-permute-start.3 = (f32[64,1024]{1,0:T(8,128)S(1)}, f32[64,1024]{1,0:T(8,128)S(1)}, u32[]{:S(2)}, u32[]{:S(2)}) collective-permute-start(f32[64,1024]{1,0:T(8,128)S(1)} %get-tuple-element.20.sm_ref), channel_id=1, source_target_pairs={{0,112},{16,0},{32,16},{48,32},{64,48},{80,64},{96,80},{112,96},{1... | collective-permute-start | bytes 786440 | tf_op jit(solution)/shard_map/ppermute | solution.py:342
  33.0 7.0 %collective-permute-start.2 = (f32[64,1024]{1,0:T(8,128)S(1)}, f32[64,1024]{1,0:T(8,128)S(1)}, u32[]{:S(2)}, u32[]{:S(2)}) collective-permute-start(f32[64,1024]{1,0:T(8,128)S(1)} %get-tuple-element.19.own_ref.sp_ref), channel_id=1, source_target_pairs={{0,16},{16,32},{32,48},{48,64},{64,80},{80,96},{96,112},{112,0},{1... | collective-permute-start | bytes 786440 | tf_op jit(solution)/shard_map/ppermute | solution.py:342
  55.2 16.2 %copy-start.2 = (f32[32,6,3,3,3]{0,4,3,2,1:T(4,128)S(1)}, f32[32,6,3,3,3]{0,4,3,2,1:T(4,128)}, u32[]{:S(2)}) copy-start(f32[32,6,3,3,3]{0,4,3,2,1:T(4,128)} %param.29) | copy-start | bytes 62212
  55.2 16.1 %copy-start.6 = (f32[5,32]{1,0:T(8,128)S(1)}, f32[5,32]{1,0:T(8,128)}, u32[]{:S(2)}) copy-start(f32[5,32]{1,0:T(8,128)} %mix_ref.3) | copy-start | bytes 1924
  55.2 16.1 %copy-start.11 = (f32[32]{0:T(128)S(1)}, f32[32]{0:T(128)}, u32[]{:S(2)}) copy-start(f32[32]{0:T(128)} %bias_ref.3) | copy-start | bytes 388
  55.2 16.1 %copy-start.12 = (f32[32]{0:T(128)S(1)}, f32[32]{0:T(128)}, u32[]{:S(2)}) copy-start(f32[32]{0:T(128)} %slope_ref.3) | copy-start | bytes 388
  55.2 16.1 %copy-start.13 = (f32[5]{0:T(128)S(1)}, f32[5]{0:T(128)}, u32[]{:S(2)}) copy-start(f32[5]{0:T(128)} %shift_ref.3) | copy-start | bytes 64
  64.3 7.0 %collective-permute-start.4 = (f32[16,128]{1,0:T(8,128)S(1)}, f32[16,128]{1,0:T(8,128)S(1)}, u32[]{:S(2)}, u32[]{:S(2)}) collective-permute-start(f32[16,128]{1,0:T(8,128)S(1)} %get-tuple-element.25), channel_id=1, source_target_pairs={{0,1},{1,2},{2,3},{3,4},{4,5},{5,6},{6,7},{7,8},{8,9},{9,10},{10,1... | collective-permute-start | bytes 24584 | tf_op jit(solution)/shard_map/ppermute | solution.py:342
  64.8 6.6 %collective-permute-start.5 = (f32[16,128]{1,0:T(8,128)S(1)}, f32[16,128]{1,0:T(8,128)S(1)}, u32[]{:S(2)}, u32[]{:S(2)}) collective-permute-start(f32[16,128]{1,0:T(8,128)S(1)} %get-tuple-element.26), channel_id=1, source_target_pairs={{0,15},{1,0},{2,1},{3,2},{4,3},{5,4},{6,5},{7,6},{8,7},{9,8},{10,9... | collective-permute-start | bytes 24584 | tf_op jit(solution)/shard_map/ppermute | solution.py:342

commit v3 on v2

--- a/solution.py
+++ b/solution.py
@@ -1,5 +1,3 @@
-import functools
-
 import jax
 import jax.numpy as jnp
 from jax import lax
@@ -20,12 +18,14 @@
     return hi, (x - hi.astype(F32)).astype(BF16)
 
 
-def dot3(a, b, dims):
-    (a_hi, a_lo), (b_hi, b_lo) = a, b
-    dot = functools.partial(
-        lax.dot_general, dimension_numbers=(dims, ((), ())), preferred_element_type=F32
-    )
-    return dot(a_hi, b_hi) + dot(a_lo, b_hi) + dot(a_hi, b_lo)
+def joined(a):
+    hi, lo = split(a)
+    return jnp.concatenate([hi, lo, hi], 1)
+
+
+def dot3(left, b):
+    hi, lo = split(b)
+    return jnp.dot(left, jnp.concatenate([hi, hi, lo], 0), preferred_element_type=F32)
 
 
 def column(ref, count):
@@ -74,8 +74,8 @@
 
 def project_kernel(
     pix_hbm, bin_hbm, cnt_hbm, primal_hbm, w_hbm, after_ref,
-    out_ref, wh_ref, wl_ref,
-    hi_ref, lo_ref, hot_ref, pix_ref, bin_ref, cnt_ref, primal_ref, w_ref, sem, w_sem,
+    final_ref, wh_ref, wl_ref,
+    out_ref, hi_ref, lo_ref, hot_ref, pix_ref, bin_ref, cnt_ref, primal_ref, w_ref, sem, w_sem,
 ):
     del after_ref
     t = lax.axis_index("tile")
@@ -93,16 +93,17 @@
     for copy in copies:
         copy.start()
 
-    def fetch(a):
-        return pltpu.make_async_copy(w_hbm.at[0, a], w_ref.at[a], w_sem.at[a])
-
-    for a in range(16):
-        fetch(a).start()
+    def fetch(i):
+        part = pl.ds(i * 2, 2)
+        return pltpu.make_async_copy(w_hbm.at[0, part], w_ref.at[part], w_sem.at[i])
+
+    for i in range(8):
+        fetch(i).start()
     row = lax.broadcasted_iota(jnp.int32, (16, 128), 0)
     for b in range(9):
         hot_ref[b] = jnp.where((row & 7) == b, 1.0, 0.0).astype(BF16)
-    out_ref[0, 0] = jnp.zeros((16, 128), F32)
-    out_ref[15, 2] = jnp.zeros((16, 128), F32)
+    out_ref[1, 0] = jnp.zeros((16, 128), F32)
+    out_ref[16, 2] = jnp.zeros((16, 128), F32)
     for copy in copies:
         copy.wait()
     for q in range(16):
@@ -116,7 +117,7 @@
         )
         hi_ref[q], lo_ref[q] = split(v)
 
-    def angle(a, carry):
+    def angle(a):
         count = cnt_ref[0, a]
         parts = []
         for s in range(12):
@@ -125,25 +126,23 @@
             hot = hot_ref[b]
             parts.append(jnp.concatenate([hi_ref[q] * hot, lo_ref[q] * hot], 0))
         left = jnp.concatenate(parts, 1)
-        fetch(a).wait()
         w_hi, w_lo = split(w_ref[a].reshape(12 * 128, 128))
         wh_ref[a], wl_ref[a] = w_hi, w_lo
         right = jnp.concatenate([w_hi, w_lo], 1)
         d = jnp.dot(left, right, preferred_element_type=F32)
         res = d[0:16, 0:128] + (d[0:16, 128:256] + d[16:32, 0:128])
-        out_ref[a, 1] = res
-
-        @pl.when(a > 0)
-        def _():
-            out_ref[jnp.maximum(a - 1, 0), 2] = res
-
-        @pl.when(a < 15)
-        def _():
-            out_ref[jnp.minimum(a + 1, 15), 0] = res
-
+        out_ref[a + 1, 1] = res
+        out_ref[a, 2] = res
+        out_ref[a + 2, 0] = res
+
+    def chunk(i, carry):
+        fetch(i).wait()
+        angle(i * 2)
+        angle(i * 2 + 1)
         return carry
 
-    lax.fori_loop(0, 16, angle, 0)
+    lax.fori_loop(0, 8, chunk, 0)
+    final_ref[...] = out_ref[1:17]
 
 
 def assemble_kernel(got_ref, own_ref, left_ref, right_ref, primal_ref, sp_ref, sm_ref):
@@ -182,7 +181,7 @@
     new_ref, send_ref, tt_ref,
 ):
     p = lax.axis_index("plane")
-    tt_ref[...] = jnp.zeros((72, 96), F32)
+    tt_ref[...] = jnp.zeros((80, 96), F32)
     for dz in range(3):
         for da in range(3):
             base = dz * 24 + da * 8
@@ -194,19 +193,18 @@
             jnp.where(p > 0, prev_ref[0:48, :], 0.0),
             own_ref[0:48, :],
             jnp.where(p < 7, next_ref[0:48, :], 0.0),
+            jnp.zeros((8, 1024), F32),
         ],
         0,
     )
-    x_hi, x_lo = split(x)
-    tt = split(tt_ref[...].T)
+    tt = joined(tt_ref[...].T)
     bias, slope, shift = column(bias_ref, 32), column(slope_ref, 32), column(shift_ref, 5)
-    mix = split(jnp.concatenate([mix_ref[...], jnp.zeros((3, 32), F32)], 0))
+    mix = joined(jnp.concatenate([mix_ref[...], jnp.zeros((3, 32), F32)], 0))
     for z in range(4):
-        rows = slice(z * 24, z * 24 + 72)
-        h = dot3(tt, (x_hi[rows], x_lo[rows]), ((1,), (0,)))
+        h = dot3(tt, x[z * 24 : z * 24 + 80])
         h = shifted_sum([h[i * 32 : (i + 1) * 32] for i in range(3)]) + bias
         h = jnp.where(h > 0, h, slope * h)
-        out = dot3(mix, split(h), ((1,), (0,))) + shift
+        out = dot3(mix, h) + shift
         out = out + x[(z + 1) * 24 + 8 : (z + 1) * 24 + 16]
         if z in (1, 2):
             for c in range(5):
@@ -218,52 +216,55 @@
 
 def back_kernel(
     pix_ref, bin_ref, cnt_ref, nd_ref, wh_ref, wl_ref,
-    out_ref, up_ref, down_ref, tab_ref, hot_ref, acc_ref,
+    out_ref, up_ref, down_ref, tab_ref, acc_ref,
 ):
-    a = pl.program_id(0)
     t = lax.axis_index("tile")
-
-    @pl.when(a == 0)
-    def _():
-        row = lax.broadcasted_iota(jnp.int32, (16, 128), 0)
-        for q in range(17):
-            hot_ref[q] = jnp.where(row == q, 1.0, 0.0).astype(BF16)
-        acc_ref[...] = jnp.zeros_like(acc_ref)
-
-    for b in range(8):
-        hi, lo = split(
-            jnp.concatenate(
-                [jnp.broadcast_to(nd_ref[a, b, z : z + 1, :], (16, 128)) for z in range(4)], 0
+    for a in range(16):
+        for b in range(8):
+            v = nd_ref[a, b]
+            hi = v.astype(BF16).astype(F32)
+            tab_ref[a, b, 0:4] = hi
+            tab_ref[a, b, 4:8] = v - hi
+    acc_ref[...] = jnp.zeros_like(acc_ref)
+    zero = jnp.zeros((8, 128), F32)
+
+    def angle(a):
+        count = cnt_ref[0, a]
+        for s in range(0, 12, 2):
+            one, two = (tab_ref[a, bin_ref[s + i, t, a]] for i in range(2))
+            left = jnp.concatenate(
+                [jnp.concatenate([one, zero], 1), jnp.concatenate([zero, two], 1)], 0
+            ).astype(BF16)
+            right = jnp.concatenate(
+                [
+                    jnp.concatenate(
+                        [w[a, (s + i) * 128 : (s + i + 1) * 128, :] for i in range(2)], 1
+                    )
+                    for w in (wh_ref, wl_ref)
+                ],
+                0,
             )
-        )
-        tab_ref[b, 0:64] = hi
-        tab_ref[b, 64:128] = lo
-    count = cnt_ref[0, a]
-    parts = []
-    for s in range(12):
-        q = jnp.where(s < count, pix_ref[s, 0, a], 16)
-        hot = hot_ref[q]
-        parts.append(tab_ref[bin_ref[s, t, a]] * jnp.concatenate([hot] * 8, 0))
-    left = jnp.concatenate(parts, 1)
-    right = jnp.concatenate(
-        [
-            jnp.concatenate([w[a, s * 128 : (s + 1) * 128, :] for s in range(12)], 1)
-            for w in (wh_ref, wl_ref)
-        ],
-        0,
-    )
-    acc_ref[...] += lax.dot_general(
-        left, right, (((1,), (1,)), ((), ())), preferred_element_type=F32
-    )
-
-    @pl.when(a == 15)
-    def _():
-        d = acc_ref[...]
-        res = d[0:64, 0:128] + (d[0:64, 128:256] + d[64:128, 0:128])
-        out_ref[...] = res
-        for z in range(4):
-            up_ref[z * 4 : z * 4 + 4, :] = res[z * 16 : z * 16 + 4]
-            down_ref[z * 4 : z * 4 + 4, :] = res[z * 16 + 12 : z * 16 + 16]
+            d = lax.dot_general(
+                left, right, (((1,), (1,)), ((), ())), preferred_element_type=F32
+            )
+            d = d[:, 0:128] + d[:, 128:256]
+            for i in range(2):
+                q = jnp.where(s + i < count, pix_ref[s + i, 0, a], 16)
+                acc_ref[q] += d[i * 8 : i * 8 + 8]
+
+    def chunk(i, carry):
+        for k in range(4):
+            angle(i * 4 + k)
+        return carry
+
+    lax.fori_loop(0, 4, chunk, 0)
+    for q in range(16):
+        v = acc_ref[q, 0:4] + acc_ref[q, 4:8]
+        out_ref[q * 4 : q * 4 + 4, :] = v
+        if q < 4:
+            up_ref[q * 4 : q * 4 + 4, :] = v
+        if q >= 12:
+            down_ref[q * 4 - 48 : q * 4 - 44, :] = v
 
 
 def primal_kernel_body(
@@ -279,22 +280,22 @@
             if keeps[plane] is not None:
                 v = jnp.where(keeps[plane], v, 0.0)
             x_ref[plane * 32 + half * 16 : plane * 32 + half * 16 + 16, :] = v
-    y_ref[...] = jnp.zeros((32, 512), F32)
+    y_ref[...] = jnp.zeros((40, 512), F32)
     for plane in range(4):
         for row in range(6):
             for col in range(4):
                 if row == 0:
-                    v = jnp.where(t > 0, above_ref[plane * 4 + col : plane * 4 + col + 1, :], 0.0)
+                    v = jnp.where(t > 0, above_ref[col * 4 + plane : col * 4 + plane + 1, :], 0.0)
                 elif row == 5:
-                    v = jnp.where(t < 15, below_ref[plane * 4 + col : plane * 4 + col + 1, :], 0.0)
+                    v = jnp.where(t < 15, below_ref[col * 4 + plane : col * 4 + plane + 1, :], 0.0)
                 else:
-                    i = plane * 16 + (row - 1) * 4 + col
+                    i = (row * 4 - 4 + col) * 4 + plane
                     v = back_ref[i : i + 1, :]
                 if keeps[plane] is not None:
                     v = jnp.where(keeps[plane], v, 0.0)
                 y_ref[plane * 8 + row : plane * 8 + row + 1, col * 128 : (col + 1) * 128] = v
     tt_ref[...] = jnp.zeros((96, 384), F32)
-    tb_ref[...] = jnp.zeros((24, 384), F32)
+    tb_ref[...] = jnp.zeros((32, 384), F32)
     for dz in range(3):
         for dr in range(3):
             rows = [
@@ -307,21 +308,16 @@
                 tt_ref[i : i + 5, r * 96 : (r + 1) * 96] = block[0:5]
                 i = dz * 8 + r + dr
                 tb_ref[i : i + 1, r * 96 : (r + 1) * 96] = block[5:6]
-    tt = split(tt_ref[...].T)
-    tb = split(tb_ref[...].T)
-    x_hi, x_lo = split(x_ref[...])
-    y_hi, y_lo = split(y_ref[...])
+    tt = joined(jnp.concatenate([tt_ref[...], tb_ref[...]], 0).T)
     bias, slope, shift = column(bias_ref, 32), column(slope_ref, 32), column(shift_ref, 5)
-    mix = split(jnp.concatenate([mix_ref[...], jnp.zeros((3, 32), F32)], 0))
+    mix = joined(jnp.concatenate([mix_ref[...], jnp.zeros((3, 32), F32)], 0))
     for z in range(2):
-        rows = slice(z * 32, z * 32 + 96)
-        h = dot3(tt, (x_hi[rows], x_lo[rows]), ((1,), (0,)))
-        rows = slice(z * 8, z * 8 + 24)
-        h = h + dot3(tb, (y_hi[rows], y_lo[rows]), ((1,), (0,)))
+        rows = [x_ref[z * 32 : z * 32 + 96], y_ref[z * 8 : z * 8 + 32]]
+        h = dot3(tt, jnp.concatenate(rows, 0))
         for r in range(4):
             g = shifted_sum([h[r * 96 + i * 32 : r * 96 + (i + 1) * 32] for i in range(3)]) + bias
             g = jnp.where(g > 0, g, slope * g)
-            out = dot3(mix, split(g), ((1,), (0,))) + shift
+            out = dot3(mix, g) + shift
             for c in range(5):
                 new_ref[c, z, r : r + 1, :] = out[c : c + 1, :] + primal_ref[c, z, r : r + 1, :]
 
@@ -373,7 +369,8 @@
         ),
         in_specs=[HBM] * 5 + [VMEM],
         out_specs=(VMEM, VMEM, VMEM),
-        scratch_shapes=[pltpu.VMEM((16, 16, 128), BF16)] * 3
+        scratch_shapes=[pltpu.VMEM((18, 3, 16, 128), F32)]
+        + [pltpu.VMEM((16, 16, 128), BF16)] * 3
         + [
             pltpu.SMEM((12, 1, 16), jnp.int32),
             pltpu.SMEM((12, 1, 16), jnp.int32),
@@ -381,7 +378,7 @@
             pltpu.VMEM((2, 4, 512), F32),
             pltpu.VMEM((16, 12, 128, 128), F32),
             pltpu.SemaphoreType.DMA((4,)),
-            pltpu.SemaphoreType.DMA((16,)),
+            pltpu.SemaphoreType.DMA((8,)),
         ],
         compiler_params=pltpu.CompilerParams(vmem_limit_bytes=18 << 20),
         cost_estimate=pl.CostEstimate(flops=1 << 31, bytes_accessed=25 << 20, transcendentals=0),
@@ -395,7 +392,7 @@
 
     new_dual, send = call(
         dual_kernel_body, [(5, 2, 1, 1024), (16, 8, 4, 128)],
-        [VMEM] * 5 + [SMEM] * 3, [pltpu.VMEM((72, 96), F32)],
+        [VMEM] * 5 + [SMEM] * 3, [pltpu.VMEM((80, 96), F32)],
     )(
         sp, prev, after, jnp.transpose(dual_kernel, (2, 3, 4, 1, 0)), dual_mixing,
         dual_bias, dual_slope, dual_shift,
@@ -405,7 +402,6 @@
     back, up, down = pl.pallas_call(
         back_kernel,
         name="back",
-        grid=(16,),
         out_shape=(
             jax.ShapeDtypeStruct((64, 128), F32),
             jax.ShapeDtypeStruct((16, 128), F32),
@@ -413,14 +409,8 @@
         ),
         in_specs=[SMEM, SMEM, SMEM, VMEM, VMEM, VMEM],
         out_specs=(VMEM, VMEM, VMEM),
-        scratch_shapes=[
-            pltpu.VMEM((8, 128, 128), BF16),
-            pltpu.VMEM((17, 16, 128), BF16),
-            pltpu.VMEM((128, 256), F32),
-        ],
-        compiler_params=pltpu.CompilerParams(
-            vmem_limit_bytes=4 << 20, dimension_semantics=("arbitrary",)
-        ),
+        scratch_shapes=[pltpu.VMEM((16, 8, 8, 128), F32), pltpu.VMEM((17, 8, 128), F32)],
+        compiler_params=pltpu.CompilerParams(vmem_limit_bytes=4 << 20),
     )(pix, bins, slot_count, leading, w_hi, w_lo)
     above = ring(down, "tile", 1)
     below = ring(up, "tile", -1)
@@ -429,9 +419,9 @@
         primal_kernel_body, [(5, 2, 4, 512)], [VMEM] * 10 + [SMEM] * 3,
         [
             pltpu.VMEM((96, 384), F32),
-            pltpu.VMEM((24, 384), F32),
+            pltpu.VMEM((32, 384), F32),
             pltpu.VMEM((128, 512), F32),
-            pltpu.VMEM((32, 512), F32),
+            pltpu.VMEM((40, 512), F32),
         ],
     )(
         sp, sm, prev, after, back, above, below, primal,

time: 75.1 us -> 68.4 us (0.911)
  Pallas kernels: 25 us -> 18.3 us
  waiting for transfers between devices: 8.36 us -> 10.6 us
  blocking collectives: 28 us -> 25.8 us
    pallas_call x1, Pallas kernels: 9.04 us -> 6.16 us  [per_device(): pl.pallas_call(back_kernel, name='back', out_shape=(jax.ShapeDtypeStruct(...]
    pallas_call x1, Pallas kernels: 8.49 us -> 5.95 us  [per_device(): pl.pallas_call(project_kernel, name='project', out_shape=(jax.ShapeDtypeS...]
    ppermute x6, waiting for transfers between devices: 8.36 us -> 10.6 us  [ring(): lax.ppermute(array, axis, [(i, (i + step) % count) for i in range(count)])]
    all_to_all x1, blocking collectives: 15.8 us -> 13.6 us  [per_device(): got = lax.all_to_all(terms, 'tile', 0, 0, tiled=True)]
    pallas_call x1, Pallas kernels: 3.48 us -> 2.61 us  [per_device(): call(primal_kernel_body, [(5, 2, 4, 512)], [VMEM] * 10 + [SMEM] * 3, [plt...]
  transfers between devices with their start and end apart: 6 -> 6, of which waited for: 3 -> 4; matrix products, arithmetic and copies ran while one was open for 0% -> 0% of each run, Pallas kernels for 11% -> 9%
where the time goes in v3:
time: 68.4 us; the launch traced here: 68.2 us
  blocking collectives  25.8 us (38%)
  Pallas kernels  18.3 us (27%)
  starting transfers between devices  12.6 us (18%)
  waiting for transfers between devices  10.6 us (15%)
  between operations  0.82 us (1%)
    all_to_all x1, blocking collectives, per_device(): got = lax.all_to_all(terms, 'tile', 0, 0, tiled=True)  13.6 us
    ppermute x6, starting transfers between devices, ring(): lax.ppermute(array, axis, [(i, (i + step) % count) for i in range(count)])  12.6 us
    all_to_all x1, blocking collectives, per_device(): leading = lax.all_to_all(send, 'tile', 0, 0, tiled=True)  12.2 us
    ppermute x6, waiting for transfers between devices, ring(): lax.ppermute(array, axis, [(i, (i + step) % count) for i in range(count)])  10.6 us
    pallas_call x1, Pallas kernels, per_device(): pl.pallas_call(back_kernel, name='back', out_shape=(jax.ShapeDtypeStruct(...  6.16 us
    pallas_call x1, Pallas kernels, per_device(): pl.pallas_call(project_kernel, name='project', out_shape=(jax.ShapeDtypeS...  5.95 us
    pallas_call x1, Pallas kernels, per_device(): call(primal_kernel_body, [(5, 2, 4, 512)], [VMEM] * 10 + [SMEM] * 3, [plt...  2.61 us
    pallas_call x1, Pallas kernels, per_device(): call(dual_kernel_body, [(5, 2, 1, 1024), (16, 8, 4, 128)], [VMEM] * 5 + [...  2.54 us
  transfers between devices with their start and end apart: 6, of which 4 were waited for; matrix products, arithmetic and copies ran while one was open for 0% of the time, Pallas kernels for 9%

profile of v3, /device:TPU:0, one launch (start us, length us, event | category | flops | bytes accessed | tf_op | source)
XLA Modules:
  0.0 68.2 jit_solution(4540439055388443746)
XLA Ops:
  0.6 1.0 %shard_map.176.after_ref.own_ref = f32[32,1024]{1,0:T(8,128)S(1)} custom-call(f32[5,2,1,1024]{3,2,1,0:T(1,128)} %dual_hbm.1, f32[2,1,1024]{2,1,0:T(1,128)} %measured_hbm.1, f32[5,2,4,512]{3,2,1,0:T(4,128)} %primal_ref.3), custom_call_target="tpu_custom_call" | custom-call | tf_op jit(solution)/shard_map/pallas_call | solution.py:350
  1.6 6.7 %collective-permute-start.1 = (f32[32,1024]{1,0:T(8,128)S(1)}, f32[32,1024]{1,0:T(8,128)S(1)}, u32[]{:S(2)}, u32[]{:S(2)}) collective-permute-start(f32[32,1024]{1,0:T(8,128)S(1)} %shard_map.176.after_ref.own_ref), channel_id=1, source_target_pairs={{0,15},{1,0},{2,1},{3,2},{4,3},{5,4},{6,5},{7,6},{8,7},{9,8},{10,9... | collective-permute-start | bytes 393224 | tf_op jit(solution)/shard_map/ppermute | solution.py:338
  8.3 0.0 copy-start.8
  8.3 0.0 copy-start.9
  8.3 0.0 copy-start.10
  8.3 0.0 copy-start.1
  8.3 0.0 copy-start.4
  8.4 6.0 %project.1 = (f32[16,3,16,128]{3,2,1,0:T(8,128)S(1)}, bf16[16,1536,128]{2,1,0:T(8,128)(2,1)S(1)}, bf16[16,1536,128]{2,1,0:T(8,128)(2,1)S(1)}) custom-call(s32[12,1,16]{2,1,0:T(1,128)} %bitcast.8, s32[12,16,16]{2,1,0:T(8,128)} %bitcast.4, s32[1,16]{1,0:T(1,128)} %cnt_ref.1, f32[5,2,4,512]{3,2,1,0:T(4,128)} %primal_ref.3, f32[1,16,12,128,128]{4,3,2,1,0:T(8,128)} %w_hbm.1, ...), custom_call_target="tpu_custom_call" | custom-call | flops 2147483648 | bytes 26214400 | tf_op jit(solution)/shard_map/project/pallas_call | solution.py:362
  14.3 2.2 %collective-permute-done.left_ref = f32[32,1024]{1,0:T(8,128)S(1)} collective-permute-done((f32[32,1024]{1,0:T(8,128)S(1)}, f32[32,1024]{1,0:T(8,128)S(1)}, u32[]{:S(2)}, u32[]{:S(2)}) %collective-permute-start) | collective-permute-done | bytes 131104 | tf_op jit(solution)/shard_map/ppermute | solution.py:338
  16.6 13.6 %all_to_all.10.got_ref = f32[16,3,16,128]{3,2,1,0:T(8,128)S(1)} all-to-all(f32[16,3,16,128]{3,2,1,0:T(8,128)S(1)} %get-tuple-element.16), channel_id=1, replica_groups=mesh['plane'=8,'tile'=16] {'tile'}, dimensions={0} | all-to-all | bytes 786432 | tf_op jit(solution)/shard_map/all_to_all | solution.py:387
  30.1 0.1 shard_map.177
  30.2 0.2 collective-permute-start.3
  30.5 0.3 collective-permute-start.2
  30.8 3.6 %collective-permute-done.3.next_ref = f32[64,1024]{1,0:T(8,128)S(1)} collective-permute-done((f32[64,1024]{1,0:T(8,128)S(1)}, f32[64,1024]{1,0:T(8,128)S(1)}, u32[]{:S(2)}, u32[]{:S(2)}) %collective-permute-start.3) | collective-permute-done | bytes 262176 | tf_op jit(solution)/shard_map/ppermute | solution.py:338
  34.4 3.1 %collective-permute-done.2.prev_ref = f32[64,1024]{1,0:T(8,128)S(1)} collective-permute-done((f32[64,1024]{1,0:T(8,128)S(1)}, f32[64,1024]{1,0:T(8,128)S(1)}, u32[]{:S(2)}, u32[]{:S(2)}) %collective-permute-start.2) | collective-permute-done | bytes 262176 | tf_op jit(solution)/shard_map/ppermute | solution.py:338
  37.5 2.5 %shard_map.178 = (f32[5,2,1,1024]{3,2,1,0:T(1,128)}, f32[16,8,4,128]{3,2,1,0:T(4,128)S(1)}) custom-call(f32[64,1024]{1,0:T(8,128)S(1)} %get-tuple-element.19.own_ref.sp_ref, f32[64,1024]{1,0:T(8,128)S(1)} %collective-permute-done.2.prev_ref, f32[64,1024]{1,0:T(8,128)S(1)} %collective-permute-done.3.next_ref, f32[3,3,3,7,32]{4,3,2,1,0:T(8,128)S(1)} %bitcast.7, ...), custom_call_target="tpu_custom_call" | custom-call | tf_op jit(solution)/shard_map/pallas_call | solution.py:393
  40.1 12.2 %all_to_all.11.nd_ref = f32[16,8,4,128]{3,2,1,0:T(4,128)S(1)} all-to-all(f32[16,8,4,128]{3,2,1,0:T(4,128)S(1)} %get-tuple-element.21), channel_id=1, replica_groups=mesh['plane'=8,'tile'=16] {'tile'}, dimensions={0} | all-to-all | bytes 524288 | tf_op jit(solution)/shard_map/all_to_all | solution.py:400
  52.3 0.0 copy-start.11
  52.3 0.0 copy-start.12
  52.4 6.2 %back.1 = (f32[64,128]{1,0:T(8,128)S(1)}, f32[16,128]{1,0:T(8,128)S(1)}, f32[16,128]{1,0:T(8,128)S(1)}) custom-call(s32[12,1,16]{2,1,0:T(1,128)S(1)} %bitcast.9, s32[12,16,16]{2,1,0:T(8,128)S(1)} %bitcast.5, s32[1,16]{1,0:T(1,128)S(1)} %copy-done.7, f32[16,8,4,128]{3,2,1,0:T(4,128)S(1)} %all_to_all.11.nd_ref, ...), custom_call_target="tpu_custom_call" | custom-call | tf_op jit(solution)/shard_map/back/pallas_call | solution.py:402
  58.5 0.5 collective-permute-start.4
  59.1 4.9 %collective-permute-start.5 = (f32[16,128]{1,0:T(8,128)S(1)}, f32[16,128]{1,0:T(8,128)S(1)}, u32[]{:S(2)}, u32[]{:S(2)}) collective-permute-start(f32[16,128]{1,0:T(8,128)S(1)} %get-tuple-element.26), channel_id=1, source_target_pairs={{0,15},{1,0},{2,1},{3,2},{4,3},{5,4},{6,5},{7,6},{8,7},{9,8},{10,9... | collective-permute-start | bytes 24584 | tf_op jit(solution)/shard_map/ppermute | solution.py:338
  63.9 1.6 %collective-permute-done.4.above_ref = f32[16,128]{1,0:T(8,128)S(1)} collective-permute-done((f32[16,128]{1,0:T(8,128)S(1)}, f32[16,128]{1,0:T(8,128)S(1)}, u32[]{:S(2)}, u32[]{:S(2)}) %collective-permute-start.4) | collective-permute-done | bytes 8224 | tf_op jit(solution)/shard_map/ppermute | solution.py:338
  65.6 2.6 %shard_map.179 = f32[5,2,4,512]{3,2,1,0:T(4,128)} custom-call(f32[64,1024]{1,0:T(8,128)S(1)} %get-tuple-element.19.own_ref.sp_ref, f32[64,1024]{1,0:T(8,128)S(1)} %get-tuple-element.20.sm_ref, f32[64,1024]{1,0:T(8,128)S(1)} %collective-permute-done.2.prev_ref, f32[64,1024]{1,0:T(8,128)S(1)} %collective-permute-done.3.next_ref, ...), custom_call_target="tpu_custom_call" | custom-call | tf_op jit(solution)/shard_map/pallas_call | solution.py:418
  (24 shorter events, 0.1 us)
Async XLA Ops:
  1.6 12.7 %collective-permute-start.1 = (f32[32,1024]{1,0:T(8,128)S(1)}, f32[32,1024]{1,0:T(8,128)S(1)}, u32[]{:S(2)}, u32[]{:S(2)}) collective-permute-start(f32[32,1024]{1,0:T(8,128)S(1)} %shard_map.176.after_ref.own_ref), channel_id=1, source_target_pairs={{0,15},{1,0},{2,1},{3,2},{4,3},{5,4},{6,5},{7,6},{8,7},{9,8},{10,9... | collective-permute-start | bytes 393224 | tf_op jit(solution)/shard_map/ppermute | solution.py:338
  8.3 8.3 %collective-permute-start = (f32[32,1024]{1,0:T(8,128)S(1)}, f32[32,1024]{1,0:T(8,128)S(1)}, u32[]{:S(2)}, u32[]{:S(2)}) collective-permute-start(f32[32,1024]{1,0:T(8,128)S(1)} %shard_map.176.after_ref.own_ref), channel_id=1, source_target_pairs={{0,1},{1,2},{2,3},{3,4},{4,5},{5,6},{6,7},{7,8},{8,9},{9,10},{10,1... | collective-permute-start | bytes 393224 | tf_op jit(solution)/shard_map/ppermute | solution.py:338
  8.3 21.9 %copy-start = (f32[5,2,4,512]{3,2,1,0:T(4,128)S(1)}, f32[5,2,4,512]{3,2,1,0:T(4,128)}, u32[]{:S(2)}) copy-start(f32[5,2,4,512]{3,2,1,0:T(4,128)} %primal_ref.3) | copy-start | bytes 245764
  8.3 29.2 %copy-start.3 = (f32[32,7,3,3,3]{0,1,4,3,2:T(8,128)S(1)}, f32[32,7,3,3,3]{0,1,4,3,2:T(8,128)}, u32[]{:S(2)}) copy-start(f32[32,7,3,3,3]{0,1,4,3,2:T(8,128)} %param.24) | copy-start | bytes 72580
  8.3 29.2 %copy-start.5 = (f32[5,32]{1,0:T(8,128)S(1)}, f32[5,32]{1,0:T(8,128)}, u32[]{:S(2)}) copy-start(f32[5,32]{1,0:T(8,128)} %mix_ref.2) | copy-start | bytes 1924
  8.3 29.2 %copy-start.8 = (f32[32]{0:T(128)S(1)}, f32[32]{0:T(128)}, u32[]{:S(2)}) copy-start(f32[32]{0:T(128)} %bias_ref.2) | copy-start | bytes 388
  8.3 29.2 %copy-start.9 = (f32[32]{0:T(128)S(1)}, f32[32]{0:T(128)}, u32[]{:S(2)}) copy-start(f32[32]{0:T(128)} %slope_ref.2) | copy-start | bytes 388
  8.3 29.2 %copy-start.10 = (f32[5]{0:T(128)S(1)}, f32[5]{0:T(128)}, u32[]{:S(2)}) copy-start(f32[5]{0:T(128)} %shift_ref.2) | copy-start | bytes 64
  8.3 44.0 %copy-start.1 = (s32[16,16,12]{1,0,2:T(8,128)S(1)}, s32[16,16,12]{1,0,2:T(8,128)}, u32[]{:S(2)}) copy-start(s32[16,16,12]{1,0,2:T(8,128)} %param.22) | copy-start | bytes 36868
  8.3 44.0 %copy-start.4 = (s32[1,16,12]{1,0,2:T(1,128)S(1)}, s32[1,16,12]{1,0,2:T(1,128)}, u32[]{:S(2)}) copy-start(s32[1,16,12]{1,0,2:T(1,128)} %param.21) | copy-start | bytes 2308
  8.4 43.9 %copy-start.7 = (s32[1,16]{1,0:T(1,128)S(1)}, s32[1,16]{1,0:T(1,128)}, u32[]{:S(2)}) copy-start(s32[1,16]{1,0:T(1,128)} %cnt_ref.1) | copy-start | bytes 196
  30.2 4.1 %collective-permute-start.3 = (f32[64,1024]{1,0:T(8,128)S(1)}, f32[64,1024]{1,0:T(8,128)S(1)}, u32[]{:S(2)}, u32[]{:S(2)}) collective-permute-start(f32[64,1024]{1,0:T(8,128)S(1)} %get-tuple-element.20.sm_ref), channel_id=1, source_target_pairs={{0,112},{16,0},{32,16},{48,32},{64,48},{80,64},{96,80},{112,96},{1... | collective-permute-start | bytes 786440 | tf_op jit(solution)/shard_map/ppermute | solution.py:338
  30.5 7.0 %collective-permute-start.2 = (f32[64,1024]{1,0:T(8,128)S(1)}, f32[64,1024]{1,0:T(8,128)S(1)}, u32[]{:S(2)}, u32[]{:S(2)}) collective-permute-start(f32[64,1024]{1,0:T(8,128)S(1)} %get-tuple-element.19.own_ref.sp_ref), channel_id=1, source_target_pairs={{0,16},{16,32},{32,48},{48,64},{64,80},{80,96},{96,112},{112,0},{1... | collective-permute-start | bytes 786440 | tf_op jit(solution)/shard_map/ppermute | solution.py:338
  52.3 13.3 %copy-start.2 = (f32[32,6,3,3,3]{0,4,3,2,1:T(4,128)S(1)}, f32[32,6,3,3,3]{0,4,3,2,1:T(4,128)}, u32[]{:S(2)}) copy-start(f32[32,6,3,3,3]{0,4,3,2,1:T(4,128)} %param.29) | copy-start | bytes 62212
  52.3 13.3 %copy-start.6 = (f32[5,32]{1,0:T(8,128)S(1)}, f32[5,32]{1,0:T(8,128)}, u32[]{:S(2)}) copy-start(f32[5,32]{1,0:T(8,128)} %mix_ref.3) | copy-start | bytes 1924
  52.3 13.3 %copy-start.11 = (f32[32]{0:T(128)S(1)}, f32[32]{0:T(128)}, u32[]{:S(2)}) copy-start(f32[32]{0:T(128)} %bias_ref.3) | copy-start | bytes 388
  52.3 13.3 %copy-start.12 = (f32[32]{0:T(128)S(1)}, f32[32]{0:T(128)}, u32[]{:S(2)}) copy-start(f32[32]{0:T(128)} %slope_ref.3) | copy-start | bytes 388
  52.4 13.3 %copy-start.13 = (f32[5]{0:T(128)S(1)}, f32[5]{0:T(128)}, u32[]{:S(2)}) copy-start(f32[5]{0:T(128)} %shift_ref.3) | copy-start | bytes 64
  58.5 7.0 %collective-permute-start.4 = (f32[16,128]{1,0:T(8,128)S(1)}, f32[16,128]{1,0:T(8,128)S(1)}, u32[]{:S(2)}, u32[]{:S(2)}) collective-permute-start(f32[16,128]{1,0:T(8,128)S(1)} %get-tuple-element.25), channel_id=1, source_target_pairs={{0,1},{1,2},{2,3},{3,4},{4,5},{5,6},{6,7},{7,8},{8,9},{9,10},{10,1... | collective-permute-start | bytes 24584 | tf_op jit(solution)/shard_map/ppermute | solution.py:338
  59.1 6.5 %collective-permute-start.5 = (f32[16,128]{1,0:T(8,128)S(1)}, f32[16,128]{1,0:T(8,128)S(1)}, u32[]{:S(2)}, u32[]{:S(2)}) collective-permute-start(f32[16,128]{1,0:T(8,128)S(1)} %get-tuple-element.26), channel_id=1, source_target_pairs={{0,15},{1,0},{2,1},{3,2},{4,3},{5,4},{6,5},{7,6},{8,7},{9,8},{10,9... | collective-permute-start | bytes 24584 | tf_op jit(solution)/shard_map/ppermute | solution.py:338

commit v4 on v3

--- a/solution.py
+++ b/solution.py
@@ -145,22 +145,17 @@
     final_ref[...] = out_ref[1:17]
 
 
-def assemble_kernel(got_ref, own_ref, left_ref, right_ref, primal_ref, sp_ref, sm_ref):
+def rims_kernel(own_ref, left_ref, right_ref, primal_ref, sp_ref, sm_ref):
     t = lax.axis_index("tile")
-    total = got_ref[0]
-    for i in range(1, 16):
-        total = total + got_ref[i]
     ok = (t > 0, None, t < 15)
     for k, src in enumerate((left_ref, own_ref, right_ref)):
-        keep = (lambda v: v) if ok[k] is None else (lambda v, m=ok[k]: jnp.where(m, v, 0.0))
         for z in range(2):
             base = z * 24 + k * 8
-            block = keep(src[z * 8 : z * 8 + 8, :])
+            block = src[z * 8 : z * 8 + 8, :]
+            if ok[k] is not None:
+                block = jnp.where(ok[k], block, 0.0)
             for out in (sp_ref, sm_ref):
                 out[base : base + 8, :] = block
-                for b in range(8):
-                    i = z * 8 + b
-                    out[base + 5 : base + 6, b * 128 : (b + 1) * 128] = keep(total[k, i : i + 1, :])
     for z, out in ((0, sm_ref), (1, sp_ref)):
         for row in range(6):
             for c in range(5):
@@ -176,19 +171,20 @@
         out[62:64, 512:1024] = jnp.zeros((2, 512), F32)
 
 
-def dual_kernel_body(
-    own_ref, prev_ref, next_ref, kern_ref, mix_ref, bias_ref, slope_ref, shift_ref,
-    new_ref, send_ref, tt_ref,
-):
+def total_kernel(got_ref, out_ref):
+    t = lax.axis_index("tile")
+    for k, ok in enumerate((t > 0, None, t < 15)):
+        total = got_ref[0, k]
+        for i in range(1, 16):
+            total = total + got_ref[i, k]
+        if ok is not None:
+            total = jnp.where(ok, total, 0.0)
+        out_ref[k * 16 : k * 16 + 16, :] = total
+
+
+def dual_inputs(own_ref, prev_ref, next_ref):
     p = lax.axis_index("plane")
-    tt_ref[...] = jnp.zeros((80, 96), F32)
-    for dz in range(3):
-        for da in range(3):
-            base = dz * 24 + da * 8
-            tt_ref[base : base + 7, :] = jnp.concatenate(
-                [kern_ref[dz, da, db] for db in range(3)], 1
-            )
-    x = jnp.concatenate(
+    return jnp.concatenate(
         [
             jnp.where(p > 0, prev_ref[0:48, :], 0.0),
             own_ref[0:48, :],
@@ -197,15 +193,68 @@
         ],
         0,
     )
+
+
+def dual_known_kernel(
+    own_ref, prev_ref, next_ref, kern_ref, bias_ref, known_ref, last_ref, tt_ref, lt_ref
+):
+    tt_ref[...] = jnp.zeros((80, 96), F32)
+    lt_ref[...] = jnp.zeros((80, 128), F32)
+    for dz in range(3):
+        for da in range(3):
+            tiles = [kern_ref[dz, da, db] for db in range(3)]
+            base = dz * 24 + da * 8
+            tt_ref[base : base + 7, :] = jnp.concatenate(tiles, 1)
+            for db in range(3):
+                four = jnp.concatenate([tiles[db][5:6]] * 4, 1)
+                for z in range(4):
+                    i = db * 24 + (z + dz) * 3 + da
+                    lt_ref[i : i + 1, z * 32 : (z + 1) * 32] = four[:, z * 32 : (z + 1) * 32]
+    last_ref[...] = joined(lt_ref[...].T)
+    x = dual_inputs(own_ref, prev_ref, next_ref)
     tt = joined(tt_ref[...].T)
-    bias, slope, shift = column(bias_ref, 32), column(slope_ref, 32), column(shift_ref, 5)
-    mix = joined(jnp.concatenate([mix_ref[...], jnp.zeros((3, 32), F32)], 0))
+    bias = column(bias_ref, 32)
     for z in range(4):
         h = dot3(tt, x[z * 24 : z * 24 + 80])
         h = shifted_sum([h[i * 32 : (i + 1) * 32] for i in range(3)]) + bias
-        h = jnp.where(h > 0, h, slope * h)
-        out = dot3(mix, h) + shift
-        out = out + x[(z + 1) * 24 + 8 : (z + 1) * 24 + 16]
+        known_ref[z * 32 : (z + 1) * 32, :] = h
+
+
+def spread_columns(y_ref, width):
+    mid = y_ref[24:48, :]
+    lane = lax.broadcasted_iota(jnp.int32, mid.shape, 1)
+    y_ref[0:24, :] = jnp.where(lane == 0, 0.0, pltpu.roll(mid, 1, 1))
+    y_ref[48:72, :] = jnp.where(lane == width - 1, 0.0, pltpu.roll(mid, width - 1, 1))
+
+
+def dual_kernel_body(
+    total_ref, tprev_ref, tnext_ref, own_ref, prev_ref, next_ref, known_ref, last_ref,
+    mix_ref, slope_ref, shift_ref, new_ref, send_ref, y_ref,
+):
+    p = lax.axis_index("plane")
+    y_ref[...] = jnp.zeros((80, 1024), F32)
+    for first, src, keep in ((0, tprev_ref, p > 0), (2, total_ref, None), (4, tnext_ref, p < 7)):
+        v = src[...]
+        if keep is not None:
+            v = jnp.where(keep, v, 0.0)
+        for k in range(3):
+            for z in range(2):
+                row = 24 + (first + z) * 3 + k
+                for b in range(8):
+                    i = k * 16 + z * 8 + b
+                    y_ref[row : row + 1, b * 128 : (b + 1) * 128] = v[i : i + 1]
+    spread_columns(y_ref, 1024)
+    slope, shift = column(slope_ref, 32), column(shift_ref, 5)
+    mix = joined(jnp.concatenate([mix_ref[...], jnp.zeros((3, 32), F32)], 0))
+    h = dot3(last_ref[...], y_ref[...]) + known_ref[...]
+    dual_rows = (
+        jnp.where(p > 0, prev_ref[32:40, :], 0.0), own_ref[8:16, :], own_ref[32:40, :],
+        jnp.where(p < 7, next_ref[8:16, :], 0.0),
+    )
+    for z in range(4):
+        g = h[z * 32 : (z + 1) * 32]
+        g = jnp.where(g > 0, g, slope * g)
+        out = dot3(mix, g) + shift + dual_rows[z]
         if z in (1, 2):
             for c in range(5):
                 new_ref[c, z - 1] = out[c : c + 1, :]
@@ -267,12 +316,11 @@
             down_ref[q * 4 - 48 : q * 4 - 44, :] = v
 
 
-def primal_kernel_body(
-    sp_ref, sm_ref, prev_ref, next_ref, back_ref, above_ref, below_ref, primal_ref, kern_ref,
-    mix_ref, bias_ref, slope_ref, shift_ref, new_ref, tt_ref, tb_ref, x_ref, y_ref,
+def primal_known_kernel(
+    sp_ref, sm_ref, prev_ref, next_ref, kern_ref, bias_ref, known_ref, last_ref,
+    tt_ref, lt_ref, x_ref,
 ):
     p = lax.axis_index("plane")
-    t = lax.axis_index("tile")
     keeps = (p > 0, None, None, p < 7)
     for plane, src in enumerate((prev_ref, sm_ref, sp_ref, next_ref)):
         for half in range(2):
@@ -280,42 +328,70 @@
             if keeps[plane] is not None:
                 v = jnp.where(keeps[plane], v, 0.0)
             x_ref[plane * 32 + half * 16 : plane * 32 + half * 16 + 16, :] = v
-    y_ref[...] = jnp.zeros((40, 512), F32)
+    tt_ref[...] = jnp.zeros((96, 384), F32)
+    lt_ref[...] = jnp.zeros((80, 256), F32)
+    for dz in range(3):
+        for dr in range(3):
+            block = jnp.concatenate(
+                [
+                    jnp.concatenate([kern_ref[c, dz, dr, db : db + 1, :] for db in range(3)], 1)
+                    for c in range(5)
+                ],
+                0,
+            )
+            for r in range(4):
+                i = dz * 32 + (r + dr) * 5
+                tt_ref[i : i + 5, r * 96 : (r + 1) * 96] = block
+            for db in range(3):
+                four = jnp.concatenate([kern_ref[5, dz, dr, db : db + 1, :]] * 4, 1)
+                for z in range(2):
+                    for r in range(4):
+                        i = db * 24 + (z + dz) * 6 + r + dr
+                        lane = z * 128 + r * 32
+                        lt_ref[i : i + 1, lane : lane + 32] = four[:, r * 32 : (r + 1) * 32]
+    last_ref[...] = joined(lt_ref[...].T)
+    tt = joined(tt_ref[...].T)
+    bias = column(bias_ref, 32)
+    for z in range(2):
+        h = dot3(tt, x_ref[z * 32 : z * 32 + 96])
+        for r in range(4):
+            g = shifted_sum([h[r * 96 + i * 32 : r * 96 + (i + 1) * 32] for i in range(3)]) + bias
+            i = (z * 4 + r) * 32
+            known_ref[i : i + 32, :] = g
+
+
+def primal_kernel_body(
+    back_ref, above_ref, below_ref, known_ref, last_ref, primal_ref,
+    mix_ref, slope_ref, shift_ref, new_ref, y_ref,
+):
+    p = lax.axis_index("plane")
+    t = lax.axis_index("tile")
+    keeps = (p > 0, None, None, p < 7)
+    y_ref[...] = jnp.zeros((80, 512), F32)
     for plane in range(4):
         for row in range(6):
             for col in range(4):
                 if row == 0:
-                    v = jnp.where(t > 0, above_ref[col * 4 + plane : col * 4 + plane + 1, :], 0.0)
+                    i = col * 4 + plane
+                    v = jnp.where(t > 0, above_ref[i : i + 1, :], 0.0)
                 elif row == 5:
-                    v = jnp.where(t < 15, below_ref[col * 4 + plane : col * 4 + plane + 1, :], 0.0)
+                    i = col * 4 + plane
+                    v = jnp.where(t < 15, below_ref[i : i + 1, :], 0.0)
                 else:
                     i = (row * 4 - 4 + col) * 4 + plane
                     v = back_ref[i : i + 1, :]
                 if keeps[plane] is not None:
                     v = jnp.where(keeps[plane], v, 0.0)
-                y_ref[plane * 8 + row : plane * 8 + row + 1, col * 128 : (col + 1) * 128] = v
-    tt_ref[...] = jnp.zeros((96, 384), F32)
-    tb_ref[...] = jnp.zeros((32, 384), F32)
-    for dz in range(3):
-        for dr in range(3):
-            rows = [
-                jnp.concatenate([kern_ref[c, dz, dr, db : db + 1, :] for db in range(3)], 1)
-                for c in range(6)
-            ]
-            block = jnp.concatenate(rows, 0)
-            for r in range(4):
-                i = dz * 32 + (r + dr) * 5
-                tt_ref[i : i + 5, r * 96 : (r + 1) * 96] = block[0:5]
-                i = dz * 8 + r + dr
-                tb_ref[i : i + 1, r * 96 : (r + 1) * 96] = block[5:6]
-    tt = joined(jnp.concatenate([tt_ref[...], tb_ref[...]], 0).T)
-    bias, slope, shift = column(bias_ref, 32), column(slope_ref, 32), column(shift_ref, 5)
+                i = 24 + plane * 6 + row
+                y_ref[i : i + 1, col * 128 : (col + 1) * 128] = v
+    spread_columns(y_ref, 512)
+    slope, shift = column(slope_ref, 32), column(shift_ref, 5)
     mix = joined(jnp.concatenate([mix_ref[...], jnp.zeros((3, 32), F32)], 0))
+    h = dot3(last_ref[...], y_ref[...]) + known_ref[...]
     for z in range(2):
-        rows = [x_ref[z * 32 : z * 32 + 96], y_ref[z * 8 : z * 8 + 32]]
-        h = dot3(tt, jnp.concatenate(rows, 0))
         for r in range(4):
-            g = shifted_sum([h[r * 96 + i * 32 : r * 96 + (i + 1) * 32] for i in range(3)]) + bias
+            i = (z * 4 + r) * 32
+            g = h[i : i + 32]
             g = jnp.where(g > 0, g, slope * g)
             out = dot3(mix, g) + shift
             for c in range(5):
@@ -325,7 +401,7 @@
 def call(body, outs, in_specs, scratch=(), limit=8 << 20):
     return pl.pallas_call(
         body,
-        out_shape=tuple(jax.ShapeDtypeStruct(s, F32) for s in outs),
+        out_shape=tuple(jax.ShapeDtypeStruct(s[0], s[1]) for s in outs),
         in_specs=in_specs,
         out_specs=tuple(VMEM for _ in outs),
         scratch_shapes=list(scratch),
@@ -348,7 +424,7 @@
     hbm = lambda x: pltpu.with_memory_space_constraint(x, pltpu.HBM)
 
     own = call(
-        pack_kernel, [(32, 1024)], [HBM] * 3,
+        pack_kernel, [((32, 1024), F32)], [HBM] * 3,
         [
             pltpu.VMEM((5, 2, 1, 1024), F32),
             pltpu.VMEM((2, 1, 1024), F32),
@@ -383,19 +459,26 @@
         compiler_params=pltpu.CompilerParams(vmem_limit_bytes=18 << 20),
         cost_estimate=pl.CostEstimate(flops=1 << 31, bytes_accessed=25 << 20, transcendentals=0),
     )(hbm(pix), hbm(bins), hbm(slot_count), hbm(primal), hbm(footprint_weights), own)
-    terms, left, right = lax.optimization_barrier((terms, left, right))
-    got = lax.all_to_all(terms, "tile", 0, 0, tiled=True)
-
-    sp, sm = call(assemble_kernel, [(64, 1024)] * 2, [VMEM] * 5)(got, own, left, right, primal)
+    sp, sm = call(rims_kernel, [((64, 1024), F32)] * 2, [VMEM] * 4)(own, left, right, primal)
     prev = ring(sp, "plane", 1)
     after = ring(sm, "plane", -1)
+    got = lax.all_to_all(terms, "tile", 0, 0, tiled=True)
+    total = call(total_kernel, [((48, 128), F32)], [VMEM])(got)[0]
+    tprev = ring(total, "plane", 1)
+    tnext = ring(total, "plane", -1)
+
+    known, last = call(
+        dual_known_kernel, [((128, 1024), F32), ((128, 240), BF16)],
+        [VMEM] * 4 + [SMEM],
+        [pltpu.VMEM((80, 96), F32), pltpu.VMEM((80, 128), F32)],
+    )(sp, prev, after, jnp.transpose(dual_kernel, (2, 3, 4, 1, 0)), dual_bias)
 
     new_dual, send = call(
-        dual_kernel_body, [(5, 2, 1, 1024), (16, 8, 4, 128)],
-        [VMEM] * 5 + [SMEM] * 3, [pltpu.VMEM((80, 96), F32)],
+        dual_kernel_body, [((5, 2, 1, 1024), F32), ((16, 8, 4, 128), F32)],
+        [VMEM] * 9 + [SMEM] * 2, [pltpu.VMEM((80, 1024), F32)],
     )(
-        sp, prev, after, jnp.transpose(dual_kernel, (2, 3, 4, 1, 0)), dual_mixing,
-        dual_bias, dual_slope, dual_shift,
+        total, tprev, tnext, sp, prev, after, known, last, dual_mixing,
+        dual_slope, dual_shift,
     )
     leading = lax.all_to_all(send, "tile", 0, 0, tiled=True)
 
@@ -415,18 +498,17 @@
     above = ring(down, "tile", 1)
     below = ring(up, "tile", -1)
 
+    known, last = call(
+        primal_known_kernel, [((256, 512), F32), ((256, 240), BF16)],
+        [VMEM] * 5 + [SMEM],
+        [pltpu.VMEM((96, 384), F32), pltpu.VMEM((80, 256), F32), pltpu.VMEM((128, 512), F32)],
+    )(sp, sm, prev, after, jnp.transpose(primal_kernel, (1, 2, 3, 4, 0)), primal_bias)
+
     new_primal = call(
-        primal_kernel_body, [(5, 2, 4, 512)], [VMEM] * 10 + [SMEM] * 3,
-        [
-            pltpu.VMEM((96, 384), F32),
-            pltpu.VMEM((32, 384), F32),
-            pltpu.VMEM((128, 512), F32),
-            pltpu.VMEM((40, 512), F32),
-        ],
+        primal_kernel_body, [((5, 2, 4, 512), F32)], [VMEM] * 7 + [SMEM] * 2,
+        [pltpu.VMEM((80, 512), F32)],
     )(
-        sp, sm, prev, after, back, above, below, primal,
-        jnp.transpose(primal_kernel, (1, 2, 3, 4, 0)), primal_mixing,
-        primal_bias, primal_slope, primal_shift,
+        back, above, below, known, last, primal, primal_mixing, primal_slope, primal_shift,
     )[0]
     return new_primal, new_dual
 

time: 68.4 us -> 73.8 us (1.079)
  blocking collectives: 25.8 us -> 12.6 us
  local copies, waits for them, and re-layouts: 0.08 us -> 10.9 us
  starting transfers between devices: 12.6 us -> 21.6 us
  waiting for transfers between devices: 10.6 us -> 6.83 us
  Pallas kernels: 18.3 us -> 20.6 us
    all_to_all x1 -> x0, blocking collectives: 13.6 us -> none  [per_device(): got = lax.all_to_all(terms, 'tile', 0, 0, tiled=True)]
    unnamed x28 -> x36, local copies, waits for them, and re-layouts: 0.08 us -> 10.9 us
    ppermute x6 -> x8, waiting for transfers between devices: 10.6 us -> 0.13 us  [ring(): lax.ppermute(array, axis, [(i, (i + step) % count) for i in range(count)])]
    all_to_all x0 -> x1, waiting for transfers between devices: none -> 6.69 us  [per_device(): got = lax.all_to_all(terms, 'tile', 0, 0, tiled=True)]
    ppermute x6 -> x8, starting transfers between devices: 12.6 us -> 18.1 us  [ring(): lax.ppermute(array, axis, [(i, (i + step) % count) for i in range(count)])]
    all_to_all x0 -> x1, starting transfers between devices: none -> 3.55 us  [per_device(): got = lax.all_to_all(terms, 'tile', 0, 0, tiled=True)]
    pallas_call x4 -> x7, Pallas kernels: 6.21 us -> 7.71 us  [the longest x1 1.78 us: per_device(): call(dual_kernel_body, [((5, 2, 1, 1024), F32), ((16, 8, 4, 128), F32)],...]
    pallas_call x1, Pallas kernels: 5.95 us -> 6.76 us  [per_device(): pl.pallas_call(project_kernel, name='project', out_shape=(jax.ShapeDtypeS...]
  transfers between devices with their start and end apart: 6 -> 9, of which waited for: 4 -> 2; matrix products, arithmetic and copies ran while one was open for 0% -> 0% of each run, Pallas kernels for 9% -> 14%
where the time goes in v4:
time: 73.8 us; the launch traced here: 73.4 us
  starting transfers between devices  21.6 us (29%)
  Pallas kernels  20.6 us (28%)
  blocking collectives  12.6 us (17%)
  local copies, waits for them, and re-layouts  10.9 us (15%)
  waiting for transfers between devices  6.83 us (9%)
  between operations  0.87 us (1%)
    ppermute x8, starting transfers between devices, ring(): lax.ppermute(array, axis, [(i, (i + step) % count) for i in range(count)])  18.1 us
    all_to_all x1, blocking collectives, per_device(): leading = lax.all_to_all(send, 'tile', 0, 0, tiled=True)  12.6 us
    unnamed x36, local copies, waits for them, and re-layouts  10.9 us
    pallas_call x1, Pallas kernels, per_device(): pl.pallas_call(project_kernel, name='project', out_shape=(jax.ShapeDtypeS...  6.76 us
    all_to_all x1, waiting for transfers between devices, per_device(): got = lax.all_to_all(terms, 'tile', 0, 0, tiled=True)  6.69 us
    pallas_call x1, Pallas kernels, per_device(): pl.pallas_call(back_kernel, name='back', out_shape=(jax.ShapeDtypeStruct(...  6.16 us
    all_to_all x1, starting transfers between devices, per_device(): got = lax.all_to_all(terms, 'tile', 0, 0, tiled=True)  3.55 us
    pallas_call x1, Pallas kernels, per_device(): call(dual_kernel_body, [((5, 2, 1, 1024), F32), ((16, 8, 4, 128), F32)],...  1.78 us
  transfers between devices with their start and end apart: 9, of which 2 were waited for; matrix products, arithmetic and copies ran while one was open for 0% of the time, Pallas kernels for 14%

profile of v4, /device:TPU:0, one launch (start us, length us, event | category | flops | bytes accessed | tf_op | source)
XLA Modules:
  0.0 73.4 jit_solution(1534931526547032126)
XLA Ops:
  0.6 1.0 %shard_map.176.after_ref.own_ref = f32[32,1024]{1,0:T(8,128)S(1)} custom-call(f32[5,2,1,1024]{3,2,1,0:T(1,128)} %dual_hbm.1, f32[2,1,1024]{2,1,0:T(1,128)} %measured_hbm.1, f32[5,2,4,512]{3,2,1,0:T(4,128)} %primal_ref.3), custom_call_target="tpu_custom_call" | custom-call | tf_op jit(solution)/shard_map/pallas_call | solution.py:426
  1.6 2.1 %collective-permute-start.2 = (f32[32,1024]{1,0:T(8,128)S(1)}, f32[32,1024]{1,0:T(8,128)S(1)}, u32[]{:S(2)}, u32[]{:S(2)}) collective-permute-start(f32[32,1024]{1,0:T(8,128)S(1)} %shard_map.176.after_ref.own_ref), channel_id=1, source_target_pairs={{0,1},{1,2},{2,3},{3,4},{4,5},{5,6},{6,7},{7,8},{8,9},{9,10},{10,1... | collective-permute-start | bytes 393224 | tf_op jit(solution)/shard_map/ppermute | solution.py:414
  3.7 4.7 %collective-permute-start.3 = (f32[32,1024]{1,0:T(8,128)S(1)}, f32[32,1024]{1,0:T(8,128)S(1)}, u32[]{:S(2)}, u32[]{:S(2)}) collective-permute-start(f32[32,1024]{1,0:T(8,128)S(1)} %shard_map.176.after_ref.own_ref), channel_id=1, source_target_pairs={{0,15},{1,0},{2,1},{3,2},{4,3},{5,4},{6,5},{7,6},{8,7},{9,8},{10,9... | collective-permute-start | bytes 393224 | tf_op jit(solution)/shard_map/ppermute | solution.py:414
  8.4 6.8 %project.1 = (f32[16,3,16,128]{3,2,1,0:T(8,128)}, bf16[16,1536,128]{2,1,0:T(8,128)(2,1)S(1)}, bf16[16,1536,128]{2,1,0:T(8,128)(2,1)S(1)}) custom-call(s32[12,1,16]{2,1,0:T(1,128)} %bitcast.8, s32[12,16,16]{2,1,0:T(8,128)} %bitcast.4, s32[1,16]{1,0:T(1,128)} %cnt_ref.1, f32[5,2,4,512]{3,2,1,0:T(4,128)} %primal_ref.3, f32[1,16,12,128,128]{4,3,2,1,0:T(8,128)} %w_hbm.1, ...), custom_call_target="tpu_custom_call" | custom-call | flops 2147483648 | bytes 26214400 | tf_op jit(solution)/shard_map/project/pallas_call | solution.py:438
  15.2 2.6 %copy-done = bf16[16,1536,128]{2,1,0:T(8,128)(2,1)} copy-done((bf16[16,1536,128]{2,1,0:T(8,128)(2,1)}, bf16[16,1536,128]{2,1,0:T(8,128)(2,1)S(1)}, u32[]{:S(2)}) %copy-start) | copy-done | bytes 6291480
  17.8 2.6 %copy-done.2 = bf16[16,1536,128]{2,1,0:T(8,128)(2,1)} copy-done((bf16[16,1536,128]{2,1,0:T(8,128)(2,1)}, bf16[16,1536,128]{2,1,0:T(8,128)(2,1)S(1)}, u32[]{:S(2)}) %copy-start.2) | copy-done | bytes 6291480
  20.5 3.6 %all-to-all-start = ((f32[16,3,16,128]{3,2,1,0:T(8,128)}), f32[16,3,16,128]{3,2,1,0:T(8,128)S(1)}, u32[]{:S(2)}, u32[]{:S(2)}) async-start(f32[16,3,16,128]{3,2,1,0:T(8,128)} %get-tuple-element.16), calls=%async_computation | async-start | bytes 786432 | tf_op jit(solution)/shard_map/all_to_all | solution.py:465
  24.1 0.1 shard_map.178
  24.1 0.0 collective-permute-start.4
  24.1 2.9 %collective-permute-start.5 = (f32[64,1024]{1,0:T(8,128)S(1)}, f32[64,1024]{1,0:T(8,128)S(1)}, u32[]{:S(2)}, u32[]{:S(2)}) collective-permute-start(f32[64,1024]{1,0:T(8,128)S(1)} %get-tuple-element.18.sm_ref), channel_id=1, source_target_pairs={{0,112},{16,0},{32,16},{48,32},{64,48},{80,64},{96,80},{112,96},{1... | collective-permute-start | bytes 786440 | tf_op jit(solution)/shard_map/ppermute | solution.py:414
  27.1 6.7 %all-to-all-done.got_ref = f32[16,3,16,128]{3,2,1,0:T(8,128)S(1)} async-done(((f32[16,3,16,128]{3,2,1,0:T(8,128)}), f32[16,3,16,128]{3,2,1,0:T(8,128)S(1)}, u32[]{:S(2)}, u32[]{:S(2)}) %all-to-all-start) | async-done | bytes 393248 | tf_op jit(solution)/shard_map/all_to_all | solution.py:465
  33.8 0.0 collective-permute-start
  33.8 2.9 %collective-permute-start.1 = (f32[48,128]{1,0:T(8,128)S(1)}, f32[48,128]{1,0:T(8,128)S(1)}, u32[]{:S(2)}, u32[]{:S(2)}) collective-permute-start(f32[48,128]{1,0:T(8,128)S(1)} %shard_map.177.total_ref), channel_id=1, source_target_pairs={{0,112},{16,0},{32,16},{48,32},{64,48},{80,64},{96,80},{112,96},{1... | collective-permute-start | bytes 73736 | tf_op jit(solution)/shard_map/ppermute | solution.py:414
  36.8 1.4 %shard_map.179 = (f32[128,1024]{1,0:T(8,128)S(1)}, bf16[128,240]{1,0:T(8,128)(2,1)S(1)}) custom-call(f32[64,1024]{1,0:T(8,128)S(1)} %get-tuple-element.17.own_ref.sp_ref, f32[64,1024]{1,0:T(8,128)S(1)} %collective-permute-done.4.prev_ref, f32[64,1024]{1,0:T(8,128)S(1)} %collective-permute-done.5.next_ref, f32[3,3,3,7,32]{4,3,2,1,0:T(8,128)S(1)} %bitcast.7, ...), custom_call_target="tpu_custom_call" | custom-call | tf_op jit(solution)/shard_map/pallas_call | solution.py:470
  38.2 0.1 collective-permute-done.tprev_ref
  38.3 1.8 %shard_map.180 = (f32[5,2,1,1024]{3,2,1,0:T(1,128)}, f32[16,8,4,128]{3,2,1,0:T(4,128)S(1)}) custom-call(f32[48,128]{1,0:T(8,128)S(1)} %shard_map.177.total_ref, f32[48,128]{1,0:T(8,128)S(1)} %collective-permute-done.tprev_ref, f32[48,128]{1,0:T(8,128)S(1)} %collective-permute-done.1.tnext_ref, f32[64,1024]{1,0:T(8,128)S(1)} %get-tuple-element.17.own_ref.sp_ref, ...), custom_call_target="tpu_custom_call" | custom-call | tf_op jit(solution)/shard_map/pallas_call | solution.py:476
  40.1 12.6 %all_to_all.10.nd_ref = f32[16,8,4,128]{3,2,1,0:T(4,128)S(1)} all-to-all(f32[16,8,4,128]{3,2,1,0:T(4,128)S(1)} %get-tuple-element.21), channel_id=1, replica_groups=mesh['plane'=8,'tile'=16] {'tile'}, dimensions={0} | all-to-all | bytes 524288 | tf_op jit(solution)/shard_map/all_to_all | solution.py:483
  52.7 2.8 %copy-done.1 = bf16[16,1536,128]{2,1,0:T(8,128)(2,1)S(1)} copy-done((bf16[16,1536,128]{2,1,0:T(8,128)(2,1)S(1)}, bf16[16,1536,128]{2,1,0:T(8,128)(2,1)}, u32[]{:S(2)}) %copy-start.1) | copy-done | bytes 6291480
  55.5 2.8 %copy-done.3 = bf16[16,1536,128]{2,1,0:T(8,128)(2,1)S(1)} copy-done((bf16[16,1536,128]{2,1,0:T(8,128)(2,1)S(1)}, bf16[16,1536,128]{2,1,0:T(8,128)(2,1)}, u32[]{:S(2)}) %copy-start.3) | copy-done | bytes 6291480
  58.3 6.2 %back.1 = (f32[64,128]{1,0:T(8,128)S(1)}, f32[16,128]{1,0:T(8,128)S(1)}, f32[16,128]{1,0:T(8,128)S(1)}) custom-call(s32[12,1,16]{2,1,0:T(1,128)S(1)} %bitcast.9, s32[12,16,16]{2,1,0:T(8,128)S(1)} %bitcast.5, s32[1,16]{1,0:T(1,128)S(1)} %copy-done.11, f32[16,8,4,128]{3,2,1,0:T(4,128)S(1)} %all_to_all.10.nd_ref, bf16[16,1536,128]{2,1,0:T(8,128)(2,1)S(1)} %copy-done.1, ...), custom_call_target="tpu_custom_call" | custom-call | tf_op jit(solution)/shard_map/back/pallas_call | solution.py:485
  64.4 0.5 collective-permute-start.6
  64.9 4.9 %collective-permute-start.7 = (f32[16,128]{1,0:T(8,128)S(1)}, f32[16,128]{1,0:T(8,128)S(1)}, u32[]{:S(2)}, u32[]{:S(2)}) collective-permute-start(f32[16,128]{1,0:T(8,128)S(1)} %get-tuple-element.26), channel_id=1, source_target_pairs={{0,15},{1,0},{2,1},{3,2},{4,3},{5,4},{6,5},{7,6},{8,7},{9,8},{10,9... | collective-permute-start | bytes 24584 | tf_op jit(solution)/shard_map/ppermute | solution.py:414
  69.9 1.8 %shard_map.181 = (f32[256,512]{1,0:T(8,128)S(1)}, bf16[256,240]{1,0:T(8,128)(2,1)S(1)}) custom-call(f32[64,1024]{1,0:T(8,128)S(1)} %get-tuple-element.17.own_ref.sp_ref, f32[64,1024]{1,0:T(8,128)S(1)} %get-tuple-element.18.sm_ref, f32[64,1024]{1,0:T(8,128)S(1)} %collective-permute-done.4.prev_ref, f32[64,1024]{1,0:T(8,128)S(1)} %collective-permute-done.5.next_ref, ...), custom_call_target="tpu_custom_call" | custom-call | tf_op jit(solution)/shard_map/pallas_call | solution.py:501
  71.7 1.7 %shard_map.182 = f32[5,2,4,512]{3,2,1,0:T(4,128)} custom-call(f32[64,128]{1,0:T(8,128)S(1)} %get-tuple-element.24.back_ref, f32[16,128]{1,0:T(8,128)S(1)} %collective-permute-done.6.above_ref, f32[16,128]{1,0:T(8,128)S(1)} %collective-permute-done.7.below_ref, f32[256,512]{1,0:T(8,128)S(1)} %get-tuple-element.27.known_ref, ...), custom_call_target="tpu_custom_call" | custom-call | tf_op jit(solution)/shard_map/pallas_call | solution.py:507
  (40 shorter events, 0.1 us)
Async XLA Ops:
  1.6 22.4 %collective-permute-start.2 = (f32[32,1024]{1,0:T(8,128)S(1)}, f32[32,1024]{1,0:T(8,128)S(1)}, u32[]{:S(2)}, u32[]{:S(2)}) collective-permute-start(f32[32,1024]{1,0:T(8,128)S(1)} %shard_map.176.after_ref.own_ref), channel_id=1, source_target_pairs={{0,1},{1,2},{2,3},{3,4},{4,5},{5,6},{6,7},{7,8},{8,9},{9,10},{10,1... | collective-permute-start | bytes 393224 | tf_op jit(solution)/shard_map/ppermute | solution.py:414
  3.7 20.3 %collective-permute-start.3 = (f32[32,1024]{1,0:T(8,128)S(1)}, f32[32,1024]{1,0:T(8,128)S(1)}, u32[]{:S(2)}, u32[]{:S(2)}) collective-permute-start(f32[32,1024]{1,0:T(8,128)S(1)} %shard_map.176.after_ref.own_ref), channel_id=1, source_target_pairs={{0,15},{1,0},{2,1},{3,2},{4,3},{5,4},{6,5},{7,6},{8,7},{9,8},{10,9... | collective-permute-start | bytes 393224 | tf_op jit(solution)/shard_map/ppermute | solution.py:414
  8.4 15.7 %copy-start.4 = (f32[5,2,4,512]{3,2,1,0:T(4,128)S(1)}, f32[5,2,4,512]{3,2,1,0:T(4,128)}, u32[]{:S(2)}) copy-start(f32[5,2,4,512]{3,2,1,0:T(4,128)} %primal_ref.3) | copy-start | bytes 245764
  8.4 28.4 %copy-start.7 = (f32[32,7,3,3,3]{0,1,4,3,2:T(8,128)S(1)}, f32[32,7,3,3,3]{0,1,4,3,2:T(8,128)}, u32[]{:S(2)}) copy-start(f32[32,7,3,3,3]{0,1,4,3,2:T(8,128)} %param.24) | copy-start | bytes 72580
  8.4 28.4 %copy-start.14 = (f32[32]{0:T(128)S(1)}, f32[32]{0:T(128)}, u32[]{:S(2)}) copy-start(f32[32]{0:T(128)} %bias_ref.2) | copy-start | bytes 388
  8.4 29.9 %copy-start.9 = (f32[5,32]{1,0:T(8,128)S(1)}, f32[5,32]{1,0:T(8,128)}, u32[]{:S(2)}) copy-start(f32[5,32]{1,0:T(8,128)} %mix_ref.2) | copy-start | bytes 1924
  8.4 29.9 %copy-start.12 = (f32[32]{0:T(128)S(1)}, f32[32]{0:T(128)}, u32[]{:S(2)}) copy-start(f32[32]{0:T(128)} %slope_ref.2) | copy-start | bytes 388
  8.4 29.9 %copy-start.13 = (f32[5]{0:T(128)S(1)}, f32[5]{0:T(128)}, u32[]{:S(2)}) copy-start(f32[5]{0:T(128)} %shift_ref.2) | copy-start | bytes 64
  8.4 44.3 %copy-start.5 = (s32[16,16,12]{1,0,2:T(8,128)S(1)}, s32[16,16,12]{1,0,2:T(8,128)}, u32[]{:S(2)}) copy-start(s32[16,16,12]{1,0,2:T(8,128)} %param.22) | copy-start | bytes 36868
  8.4 44.3 %copy-start.8 = (s32[1,16,12]{1,0,2:T(1,128)S(1)}, s32[1,16,12]{1,0,2:T(1,128)}, u32[]{:S(2)}) copy-start(s32[1,16,12]{1,0,2:T(1,128)} %param.21) | copy-start | bytes 2308
  8.4 44.3 %copy-start.11 = (s32[1,16]{1,0:T(1,128)S(1)}, s32[1,16]{1,0:T(1,128)}, u32[]{:S(2)}) copy-start(s32[1,16]{1,0:T(1,128)} %cnt_ref.1) | copy-start | bytes 196
  20.5 13.3 %all-to-all-start = ((f32[16,3,16,128]{3,2,1,0:T(8,128)}), f32[16,3,16,128]{3,2,1,0:T(8,128)S(1)}, u32[]{:S(2)}, u32[]{:S(2)}) async-start(f32[16,3,16,128]{3,2,1,0:T(8,128)} %get-tuple-element.16), calls=%async_computation | async-start | bytes 786432 | tf_op jit(solution)/shard_map/all_to_all | solution.py:465
  24.1 12.7 %collective-permute-start.4 = (f32[64,1024]{1,0:T(8,128)S(1)}, f32[64,1024]{1,0:T(8,128)S(1)}, u32[]{:S(2)}, u32[]{:S(2)}) collective-permute-start(f32[64,1024]{1,0:T(8,128)S(1)} %get-tuple-element.17.own_ref.sp_ref), channel_id=1, source_target_pairs={{0,16},{16,32},{32,48},{48,64},{64,80},{80,96},{96,112},{112,0},{1... | collective-permute-start | bytes 786440 | tf_op jit(solution)/shard_map/ppermute | solution.py:414
  24.1 12.6 %collective-permute-start.5 = (f32[64,1024]{1,0:T(8,128)S(1)}, f32[64,1024]{1,0:T(8,128)S(1)}, u32[]{:S(2)}, u32[]{:S(2)}) collective-permute-start(f32[64,1024]{1,0:T(8,128)S(1)} %get-tuple-element.18.sm_ref), channel_id=1, source_target_pairs={{0,112},{16,0},{32,16},{48,32},{64,48},{80,64},{96,80},{112,96},{1... | collective-permute-start | bytes 786440 | tf_op jit(solution)/shard_map/ppermute | solution.py:414
  33.8 4.5 %collective-permute-start = (f32[48,128]{1,0:T(8,128)S(1)}, f32[48,128]{1,0:T(8,128)S(1)}, u32[]{:S(2)}, u32[]{:S(2)}) collective-permute-start(f32[48,128]{1,0:T(8,128)S(1)} %shard_map.177.total_ref), channel_id=1, source_target_pairs={{0,16},{16,32},{32,48},{48,64},{64,80},{80,96},{96,112},{112,0},{1... | collective-permute-start | bytes 73736 | tf_op jit(solution)/shard_map/ppermute | solution.py:414
  33.8 4.5 %collective-permute-start.1 = (f32[48,128]{1,0:T(8,128)S(1)}, f32[48,128]{1,0:T(8,128)S(1)}, u32[]{:S(2)}, u32[]{:S(2)}) collective-permute-start(f32[48,128]{1,0:T(8,128)S(1)} %shard_map.177.total_ref), channel_id=1, source_target_pairs={{0,112},{16,0},{32,16},{48,32},{64,48},{80,64},{96,80},{112,96},{1... | collective-permute-start | bytes 73736 | tf_op jit(solution)/shard_map/ppermute | solution.py:414
  52.7 2.8 %copy-start.1 = (bf16[16,1536,128]{2,1,0:T(8,128)(2,1)S(1)}, bf16[16,1536,128]{2,1,0:T(8,128)(2,1)}, u32[]{:S(2)}) copy-start(bf16[16,1536,128]{2,1,0:T(8,128)(2,1)} %copy-done) | copy-start | bytes 18874372
  58.3 11.6 %copy-start.6 = (f32[32,6,3,3,3]{0,4,3,2,1:T(4,128)S(1)}, f32[32,6,3,3,3]{0,4,3,2,1:T(4,128)}, u32[]{:S(2)}) copy-start(f32[32,6,3,3,3]{0,4,3,2,1:T(4,128)} %param.29) | copy-start | bytes 62212
  58.3 11.6 %copy-start.15 = (f32[32]{0:T(128)S(1)}, f32[32]{0:T(128)}, u32[]{:S(2)}) copy-start(f32[32]{0:T(128)} %bias_ref.3) | copy-start | bytes 388
  58.3 13.4 %copy-start.10 = (f32[5,32]{1,0:T(8,128)S(1)}, f32[5,32]{1,0:T(8,128)}, u32[]{:S(2)}) copy-start(f32[5,32]{1,0:T(8,128)} %mix_ref.3) | copy-start | bytes 1924
  58.3 13.4 %copy-start.16 = (f32[32]{0:T(128)S(1)}, f32[32]{0:T(128)}, u32[]{:S(2)}) copy-start(f32[32]{0:T(128)} %slope_ref.3) | copy-start | bytes 388
  58.3 13.4 %copy-start.17 = (f32[5]{0:T(128)S(1)}, f32[5]{0:T(128)}, u32[]{:S(2)}) copy-start(f32[5]{0:T(128)} %shift_ref.3) | copy-start | bytes 64
  64.4 7.2 %collective-permute-start.6 = (f32[16,128]{1,0:T(8,128)S(1)}, f32[16,128]{1,0:T(8,128)S(1)}, u32[]{:S(2)}, u32[]{:S(2)}) collective-permute-start(f32[16,128]{1,0:T(8,128)S(1)} %get-tuple-element.25), channel_id=1, source_target_pairs={{0,1},{1,2},{2,3},{3,4},{4,5},{5,6},{6,7},{7,8},{8,9},{9,10},{10,1... | collective-permute-start | bytes 24584 | tf_op jit(solution)/shard_map/ppermute | solution.py:414
  64.9 6.7 %collective-permute-start.7 = (f32[16,128]{1,0:T(8,128)S(1)}, f32[16,128]{1,0:T(8,128)S(1)}, u32[]{:S(2)}, u32[]{:S(2)}) collective-permute-start(f32[16,128]{1,0:T(8,128)S(1)} %get-tuple-element.26), channel_id=1, source_target_pairs={{0,15},{1,0},{2,1},{3,2},{4,3},{5,4},{6,5},{7,6},{8,7},{9,8},{10,9... | collective-permute-start | bytes 24584 | tf_op jit(solution)/shard_map/ppermute | solution.py:414
  (3 other events, 8.0 us)

commit v5 on v4

--- a/solution.py
+++ b/solution.py
@@ -16,6 +16,10 @@
 def split(x):
     hi = x.astype(BF16)
     return hi, (x - hi.astype(F32)).astype(BF16)
+
+
+def is_even(axis):
+    return (lax.axis_index(axis) & 1) == 0
 
 
 def joined(a):
@@ -145,30 +149,45 @@
     final_ref[...] = out_ref[1:17]
 
 
-def rims_kernel(own_ref, left_ref, right_ref, primal_ref, sp_ref, sm_ref):
+def rims_kernel(own_ref, first_ref, second_ref, primal_ref, sp_ref, sm_ref, a_ref, b_ref):
     t = lax.axis_index("tile")
-    ok = (t > 0, None, t < 15)
-    for k, src in enumerate((left_ref, own_ref, right_ref)):
-        for z in range(2):
+    even, even_plane = is_even("tile"), is_even("plane")
+
+    def left(rows, lanes):
+        return jnp.where(even, second_ref[rows, lanes], first_ref[rows, lanes])
+
+    def right(rows, lanes):
+        return jnp.where(even, first_ref[rows, lanes], second_ref[rows, lanes])
+
+    every = slice(None)
+    for z in range(2):
+        rows = slice(z * 8, z * 8 + 8)
+        blocks = (
+            jnp.where(t > 0, left(rows, every), 0.0),
+            own_ref[rows, :],
+            jnp.where(t < 15, right(rows, every), 0.0),
+        )
+        for k, block in enumerate(blocks):
             base = z * 24 + k * 8
-            block = src[z * 8 : z * 8 + 8, :]
-            if ok[k] is not None:
-                block = jnp.where(ok[k], block, 0.0)
-            for out in (sp_ref, sm_ref):
+            for out in (sp_ref, sm_ref, a_ref, b_ref):
                 out[base : base + 8, :] = block
     for z, out in ((0, sm_ref), (1, sp_ref)):
+        half = slice(z * 512, (z + 1) * 512)
         for row in range(6):
             for c in range(5):
                 if row == 0:
-                    v = jnp.where(ok[0], left_ref[21 + c : 22 + c, z * 512 : (z + 1) * 512], 0.0)
+                    v = jnp.where(t > 0, left(slice(21 + c, 22 + c), half), 0.0)
                 elif row == 5:
-                    v = jnp.where(ok[2], right_ref[16 + c : 17 + c, z * 512 : (z + 1) * 512], 0.0)
+                    v = jnp.where(t < 15, right(slice(16 + c, 17 + c), half), 0.0)
                 else:
                     v = primal_ref[c, z, row - 1 : row, :]
                 i = row * 5 + c
                 lane = (i // 16) * 512
                 out[48 + i % 16 : 49 + i % 16, lane : lane + 512] = v
         out[62:64, 512:1024] = jnp.zeros((2, 512), F32)
+    up, down = sp_ref[48:64, :], sm_ref[48:64, :]
+    a_ref[48:64, :] = jnp.where(even_plane, up, down)
+    b_ref[48:64, :] = jnp.where(even_plane, down, up)
 
 
 def total_kernel(got_ref, out_ref):
@@ -182,13 +201,21 @@
         out_ref[k * 16 : k * 16 + 16, :] = total
 
 
-def dual_inputs(own_ref, prev_ref, next_ref):
+def plane_sides(first_ref, second_ref, rows):
     p = lax.axis_index("plane")
+    even = is_even("plane")
+    first, second = first_ref[rows, :], second_ref[rows, :]
+    before = jnp.where(p > 0, jnp.where(even, second, first), 0.0)
+    return before, jnp.where(p < 7, jnp.where(even, first, second), 0.0)
+
+
+def dual_inputs(own_ref, first_ref, second_ref):
+    before, after = plane_sides(first_ref, second_ref, slice(0, 48))
     return jnp.concatenate(
         [
-            jnp.where(p > 0, prev_ref[0:48, :], 0.0),
+            before,
             own_ref[0:48, :],
-            jnp.where(p < 7, next_ref[0:48, :], 0.0),
+            after,
             jnp.zeros((8, 1024), F32),
         ],
         0,
@@ -196,7 +223,7 @@
 
 
 def dual_known_kernel(
-    own_ref, prev_ref, next_ref, kern_ref, bias_ref, known_ref, last_ref, tt_ref, lt_ref
+    own_ref, first_ref, second_ref, kern_ref, bias_ref, known_ref, last_ref, tt_ref, lt_ref
 ):
     tt_ref[...] = jnp.zeros((80, 96), F32)
     lt_ref[...] = jnp.zeros((80, 128), F32)
@@ -211,7 +238,7 @@
                     i = db * 24 + (z + dz) * 3 + da
                     lt_ref[i : i + 1, z * 32 : (z + 1) * 32] = four[:, z * 32 : (z + 1) * 32]
     last_ref[...] = joined(lt_ref[...].T)
-    x = dual_inputs(own_ref, prev_ref, next_ref)
+    x = dual_inputs(own_ref, first_ref, second_ref)
     tt = joined(tt_ref[...].T)
     bias = column(bias_ref, 32)
     for z in range(4):
@@ -228,18 +255,15 @@
 
 
 def dual_kernel_body(
-    total_ref, tprev_ref, tnext_ref, own_ref, prev_ref, next_ref, known_ref, last_ref,
+    total_ref, ta_ref, tb_ref, own_ref, first_ref, second_ref, known_ref, last_ref,
     mix_ref, slope_ref, shift_ref, new_ref, send_ref, y_ref,
 ):
-    p = lax.axis_index("plane")
     y_ref[...] = jnp.zeros((80, 1024), F32)
-    for first, src, keep in ((0, tprev_ref, p > 0), (2, total_ref, None), (4, tnext_ref, p < 7)):
-        v = src[...]
-        if keep is not None:
-            v = jnp.where(keep, v, 0.0)
+    before, after = plane_sides(ta_ref, tb_ref, slice(0, 48))
+    for start, v in ((0, before), (2, total_ref[...]), (4, after)):
         for k in range(3):
             for z in range(2):
-                row = 24 + (first + z) * 3 + k
+                row = 24 + (start + z) * 3 + k
                 for b in range(8):
                     i = k * 16 + z * 8 + b
                     y_ref[row : row + 1, b * 128 : (b + 1) * 128] = v[i : i + 1]
@@ -248,8 +272,10 @@
     mix = joined(jnp.concatenate([mix_ref[...], jnp.zeros((3, 32), F32)], 0))
     h = dot3(last_ref[...], y_ref[...]) + known_ref[...]
     dual_rows = (
-        jnp.where(p > 0, prev_ref[32:40, :], 0.0), own_ref[8:16, :], own_ref[32:40, :],
-        jnp.where(p < 7, next_ref[8:16, :], 0.0),
+        plane_sides(first_ref, second_ref, slice(32, 40))[0],
+        own_ref[8:16, :],
+        own_ref[32:40, :],
+        plane_sides(first_ref, second_ref, slice(8, 16))[1],
     )
     for z in range(4):
         g = h[z * 32 : (z + 1) * 32]
@@ -264,10 +290,13 @@
 
 
 def back_kernel(
-    pix_ref, bin_ref, cnt_ref, nd_ref, wh_ref, wl_ref,
-    out_ref, up_ref, down_ref, tab_ref, acc_ref,
+    pix_ref, bin_ref, cnt_ref, nd_ref, wh_ref, wl_ref, new_ref,
+    out_ref, first_ref, second_ref, new_hbm, tab_ref, acc_ref, sem,
 ):
     t = lax.axis_index("tile")
+    even = is_even("tile")
+    copy = pltpu.make_async_copy(new_ref, new_hbm, sem)
+    copy.start()
     for a in range(16):
         for b in range(8):
             v = nd_ref[a, b]
@@ -310,24 +339,21 @@
     for q in range(16):
         v = acc_ref[q, 0:4] + acc_ref[q, 4:8]
         out_ref[q * 4 : q * 4 + 4, :] = v
-        if q < 4:
-            up_ref[q * 4 : q * 4 + 4, :] = v
-        if q >= 12:
-            down_ref[q * 4 - 48 : q * 4 - 44, :] = v
+    up, down = out_ref[0:16, :], out_ref[48:64, :]
+    first_ref[...] = jnp.where(even, down, up)
+    second_ref[...] = jnp.where(even, up, down)
+    copy.wait()
 
 
 def primal_known_kernel(
-    sp_ref, sm_ref, prev_ref, next_ref, kern_ref, bias_ref, known_ref, last_ref,
+    sp_ref, sm_ref, first_ref, second_ref, kern_ref, bias_ref, known_ref, last_ref,
     tt_ref, lt_ref, x_ref,
 ):
-    p = lax.axis_index("plane")
-    keeps = (p > 0, None, None, p < 7)
-    for plane, src in enumerate((prev_ref, sm_ref, sp_ref, next_ref)):
+    before, after = plane_sides(first_ref, second_ref, slice(48, 64))
+    for plane, v in enumerate((before, sm_ref[48:64, :], sp_ref[48:64, :], after)):
         for half in range(2):
-            v = src[48:64, half * 512 : (half + 1) * 512]
-            if keeps[plane] is not None:
-                v = jnp.where(keeps[plane], v, 0.0)
-            x_ref[plane * 32 + half * 16 : plane * 32 + half * 16 + 16, :] = v
+            i = plane * 32 + half * 16
+            x_ref[i : i + 16, :] = v[:, half * 512 : (half + 1) * 512]
     tt_ref[...] = jnp.zeros((96, 384), F32)
     lt_ref[...] = jnp.zeros((80, 256), F32)
     for dz in range(3):
@@ -361,22 +387,26 @@
 
 
 def primal_kernel_body(
-    back_ref, above_ref, below_ref, known_ref, last_ref, primal_ref,
+    back_ref, first_ref, second_ref, known_ref, last_ref, primal_ref,
     mix_ref, slope_ref, shift_ref, new_ref, y_ref,
 ):
     p = lax.axis_index("plane")
     t = lax.axis_index("tile")
     keeps = (p > 0, None, None, p < 7)
+    even = is_even("tile")
+    first, second = first_ref[...], second_ref[...]
+    above = jnp.where(t > 0, jnp.where(even, second, first), 0.0)
+    below = jnp.where(t < 15, jnp.where(even, first, second), 0.0)
     y_ref[...] = jnp.zeros((80, 512), F32)
     for plane in range(4):
         for row in range(6):
             for col in range(4):
                 if row == 0:
                     i = col * 4 + plane
-                    v = jnp.where(t > 0, above_ref[i : i + 1, :], 0.0)
+                    v = above[i : i + 1]
                 elif row == 5:
                     i = col * 4 + plane
-                    v = jnp.where(t < 15, below_ref[i : i + 1, :], 0.0)
+                    v = below[i : i + 1]
                 else:
                     i = (row * 4 - 4 + col) * 4 + plane
                     v = back_ref[i : i + 1, :]
@@ -409,9 +439,12 @@
     )
 
 
-def ring(array, axis, step):
+def swaps(first, second, axis):
     count = lax.axis_size(axis)
-    return lax.ppermute(array, axis, [(i, (i + step) % count) for i in range(count)])
+    a = lax.ppermute(first, axis, [(i, i ^ 1) for i in range(count)])
+    pairs = [(i, (i - 1 if i % 2 == 0 else i + 1) % count) for i in range(count)]
+    b = lax.ppermute(second, axis, pairs)
+    return a, b
 
 
 def per_device(
@@ -432,8 +465,7 @@
             pltpu.SemaphoreType.DMA((3,)),
         ],
     )(hbm(dual), hbm(measured), hbm(primal))[0]
-    left = ring(own, "tile", 1)
-    right = ring(own, "tile", -1)
+    near = swaps(own, own, "tile")
 
     terms, w_hi, w_lo = pl.pallas_call(
         project_kernel,
@@ -459,56 +491,61 @@
         compiler_params=pltpu.CompilerParams(vmem_limit_bytes=18 << 20),
         cost_estimate=pl.CostEstimate(flops=1 << 31, bytes_accessed=25 << 20, transcendentals=0),
     )(hbm(pix), hbm(bins), hbm(slot_count), hbm(primal), hbm(footprint_weights), own)
-    sp, sm = call(rims_kernel, [((64, 1024), F32)] * 2, [VMEM] * 4)(own, left, right, primal)
-    prev = ring(sp, "plane", 1)
-    after = ring(sm, "plane", -1)
+    terms, near = lax.optimization_barrier((terms, near))
+    sp, sm, side_a, side_b = call(
+        rims_kernel, [((64, 1024), F32)] * 4, [VMEM] * 4
+    )(own, *near, primal)
+    sides = swaps(side_a, side_b, "plane")
     got = lax.all_to_all(terms, "tile", 0, 0, tiled=True)
     total = call(total_kernel, [((48, 128), F32)], [VMEM])(got)[0]
-    tprev = ring(total, "plane", 1)
-    tnext = ring(total, "plane", -1)
+    rows = swaps(total, total, "plane")
 
     known, last = call(
         dual_known_kernel, [((128, 1024), F32), ((128, 240), BF16)],
         [VMEM] * 4 + [SMEM],
         [pltpu.VMEM((80, 96), F32), pltpu.VMEM((80, 128), F32)],
-    )(sp, prev, after, jnp.transpose(dual_kernel, (2, 3, 4, 1, 0)), dual_bias)
-
-    new_dual, send = call(
+    )(sp, *sides, jnp.transpose(dual_kernel, (2, 3, 4, 1, 0)), dual_bias)
+
+    new_rows, send = call(
         dual_kernel_body, [((5, 2, 1, 1024), F32), ((16, 8, 4, 128), F32)],
         [VMEM] * 9 + [SMEM] * 2, [pltpu.VMEM((80, 1024), F32)],
     )(
-        total, tprev, tnext, sp, prev, after, known, last, dual_mixing,
+        total, *rows, sp, *sides, known, last, dual_mixing,
         dual_slope, dual_shift,
     )
     leading = lax.all_to_all(send, "tile", 0, 0, tiled=True)
 
-    back, up, down = pl.pallas_call(
+    back, edge_a, edge_b, new_dual = pl.pallas_call(
         back_kernel,
         name="back",
         out_shape=(
             jax.ShapeDtypeStruct((64, 128), F32),
             jax.ShapeDtypeStruct((16, 128), F32),
             jax.ShapeDtypeStruct((16, 128), F32),
+            jax.ShapeDtypeStruct((5, 2, 1, 1024), F32),
         ),
-        in_specs=[SMEM, SMEM, SMEM, VMEM, VMEM, VMEM],
-        out_specs=(VMEM, VMEM, VMEM),
-        scratch_shapes=[pltpu.VMEM((16, 8, 8, 128), F32), pltpu.VMEM((17, 8, 128), F32)],
+        in_specs=[SMEM, SMEM, SMEM, VMEM, VMEM, VMEM, VMEM],
+        out_specs=(VMEM, VMEM, VMEM, HBM),
+        scratch_shapes=[
+            pltpu.VMEM((16, 8, 8, 128), F32),
+            pltpu.VMEM((17, 8, 128), F32),
+            pltpu.SemaphoreType.DMA,
+        ],
         compiler_params=pltpu.CompilerParams(vmem_limit_bytes=4 << 20),
-    )(pix, bins, slot_count, leading, w_hi, w_lo)
-    above = ring(down, "tile", 1)
-    below = ring(up, "tile", -1)
+    )(pix, bins, slot_count, leading, w_hi, w_lo, new_rows)
+    edges = swaps(edge_a, edge_b, "tile")
 
     known, last = call(
         primal_known_kernel, [((256, 512), F32), ((256, 240), BF16)],
         [VMEM] * 5 + [SMEM],
         [pltpu.VMEM((96, 384), F32), pltpu.VMEM((80, 256), F32), pltpu.VMEM((128, 512), F32)],
-    )(sp, sm, prev, after, jnp.transpose(primal_kernel, (1, 2, 3, 4, 0)), primal_bias)
+    )(sp, sm, *sides, jnp.transpose(primal_kernel, (1, 2, 3, 4, 0)), primal_bias)
 
     new_primal = call(
         primal_kernel_body, [((5, 2, 4, 512), F32)], [VMEM] * 7 + [SMEM] * 2,
         [pltpu.VMEM((80, 512), F32)],
     )(
-        back, above, below, known, last, primal, primal_mixing, primal_slope, primal_shift,
+        back, *edges, known, last, primal, primal_mixing, primal_slope, primal_shift,
     )[0]
     return new_primal, new_dual
 

time: 73.8 us -> 73.1 us (level)
  waiting for transfers between devices: 6.83 us -> 9.82 us
  starting transfers between devices: 21.6 us -> 19.1 us
    ppermute x8, waiting for transfers between devices: 0.13 us -> 3.39 us  [the longest x4 3.38 us: swaps(): b = lax.ppermute(second, axis, pairs)]
    ppermute x8, starting transfers between devices: 18.1 us -> 15.5 us  [the longest x4 12.8 us: swaps(): b = lax.ppermute(second, axis, pairs)]
  transfers between devices with their start and end apart: 9 -> 9, of which waited for: 2 -> 3; matrix products, arithmetic and copies ran while one was open for 0% -> 0% of each run, Pallas kernels for 14% -> 14%
where the time goes in v5:
time: 73.1 us; the launch traced here: 72.8 us
  Pallas kernels  20.1 us (27%)
  starting transfers between devices  19.1 us (26%)
  blocking collectives  12.1 us (17%)
  local copies, waits for them, and re-layouts  10.9 us (15%)
  waiting for transfers between devices  9.82 us (13%)
  between operations  0.84 us (1%)
    ppermute x4, starting transfers between devices, swaps(): b = lax.ppermute(second, axis, pairs)  12.8 us
    all_to_all x1, blocking collectives, per_device(): leading = lax.all_to_all(send, 'tile', 0, 0, tiled=True)  12.1 us
    unnamed x36, local copies, waits for them, and re-layouts  10.9 us
    pallas_call x1, Pallas kernels, per_device(): pl.pallas_call(project_kernel, name='project', out_shape=(jax.ShapeDtypeS...  6.76 us
    all_to_all x1, waiting for transfers between devices, per_device(): got = lax.all_to_all(terms, 'tile', 0, 0, tiled=True)  6.43 us
    pallas_call x1, Pallas kernels, per_device(): pl.pallas_call(back_kernel, name='back', out_shape=(jax.ShapeDtypeStruct(...  6.18 us
    all_to_all x1, starting transfers between devices, per_device(): got = lax.all_to_all(terms, 'tile', 0, 0, tiled=True)  3.55 us
    ppermute x4, waiting for transfers between devices, swaps(): b = lax.ppermute(second, axis, pairs)  3.38 us
  transfers between devices with their start and end apart: 9, of which 3 were waited for; matrix products, arithmetic and copies ran while one was open for 0% of the time, Pallas kernels for 14%

profile of v5, /device:TPU:0, one launch (start us, length us, event | category | flops | bytes accessed | tf_op | source)
XLA Modules:
  0.0 72.8 jit_solution(10684350165814314492)
XLA Ops:
  0.6 1.0 %shard_map.176.after_ref.own_ref = f32[32,1024]{1,0:T(8,128)S(1)} custom-call(f32[5,2,1,1024]{3,2,1,0:T(1,128)} %dual_hbm.1, f32[2,1,1024]{2,1,0:T(1,128)} %measured_hbm.1, f32[5,2,4,512]{3,2,1,0:T(4,128)} %primal_ref.3), custom_call_target="tpu_custom_call" | custom-call | tf_op jit(solution)/shard_map/pallas_call | solution.py:459
  1.6 2.1 %collective-permute-start = (f32[32,1024]{1,0:T(8,128)S(1)}, f32[32,1024]{1,0:T(8,128)S(1)}, u32[]{:S(2)}, u32[]{:S(2)}) collective-permute-start(f32[32,1024]{1,0:T(8,128)S(1)} %shard_map.176.after_ref.own_ref), channel_id=1, source_target_pairs={{0,1},{1,0},{2,3},{3,2},{4,5},{5,4},{6,7},{7,6},{8,9},{9,8},{10,11... | collective-permute-start | bytes 393224 | tf_op jit(solution)/shard_map/ppermute | solution.py:444
  3.7 5.0 %collective-permute-start.1 = (f32[32,1024]{1,0:T(8,128)S(1)}, f32[32,1024]{1,0:T(8,128)S(1)}, u32[]{:S(2)}, u32[]{:S(2)}) collective-permute-start(f32[32,1024]{1,0:T(8,128)S(1)} %shard_map.176.after_ref.own_ref), channel_id=1, source_target_pairs={{0,15},{1,2},{2,1},{3,4},{4,3},{5,6},{6,5},{7,8},{8,7},{9,10},{10,... | collective-permute-start | bytes 393224 | tf_op jit(solution)/shard_map/ppermute | solution.py:446
  8.8 6.8 %project.1 = (f32[16,3,16,128]{3,2,1,0:T(8,128)}, bf16[16,1536,128]{2,1,0:T(8,128)(2,1)S(1)}, bf16[16,1536,128]{2,1,0:T(8,128)(2,1)S(1)}) custom-call(s32[12,1,16]{2,1,0:T(1,128)} %bitcast.8, s32[12,16,16]{2,1,0:T(8,128)} %bitcast.4, s32[1,16]{1,0:T(1,128)} %cnt_ref.1, f32[5,2,4,512]{3,2,1,0:T(4,128)} %primal_ref.3, f32[1,16,12,128,128]{4,3,2,1,0:T(8,128)} %w_hbm.1, ...), custom_call_target="tpu_custom_call" | custom-call | flops 2147483648 | bytes 26214400 | tf_op jit(solution)/shard_map/project/pallas_call | solution.py:470
  15.5 2.6 %copy-done = bf16[16,1536,128]{2,1,0:T(8,128)(2,1)} copy-done((bf16[16,1536,128]{2,1,0:T(8,128)(2,1)}, bf16[16,1536,128]{2,1,0:T(8,128)(2,1)S(1)}, u32[]{:S(2)}) %copy-start) | copy-done | bytes 6291480
  18.2 2.6 %copy-done.2 = bf16[16,1536,128]{2,1,0:T(8,128)(2,1)} copy-done((bf16[16,1536,128]{2,1,0:T(8,128)(2,1)}, bf16[16,1536,128]{2,1,0:T(8,128)(2,1)S(1)}, u32[]{:S(2)}) %copy-start.2) | copy-done | bytes 6291480
  20.8 3.6 %all-to-all-start = ((f32[16,3,16,128]{3,2,1,0:T(8,128)}), f32[16,3,16,128]{3,2,1,0:T(8,128)S(1)}, u32[]{:S(2)}, u32[]{:S(2)}) async-start(f32[16,3,16,128]{3,2,1,0:T(8,128)} %get-tuple-element.23), calls=%async_computation | async-start | bytes 786432 | tf_op jit(solution)/shard_map/all_to_all | solution.py:499
  24.4 0.1 shard_map.178
  24.5 0.1 collective-permute-start.4
  24.6 2.9 %collective-permute-start.5 = (f32[64,1024]{1,0:T(8,128)S(1)}, f32[64,1024]{1,0:T(8,128)S(1)}, u32[]{:S(2)}, u32[]{:S(2)}) collective-permute-start(f32[64,1024]{1,0:T(8,128)S(1)} %get-tuple-element.28), channel_id=1, source_target_pairs={{0,112},{16,32},{32,16},{48,64},{64,48},{80,96},{96,80},{112,0},{1... | collective-permute-start | bytes 786440 | tf_op jit(solution)/shard_map/ppermute | solution.py:446
  27.4 6.4 %all-to-all-done.got_ref = f32[16,3,16,128]{3,2,1,0:T(8,128)S(1)} async-done(((f32[16,3,16,128]{3,2,1,0:T(8,128)}), f32[16,3,16,128]{3,2,1,0:T(8,128)S(1)}, u32[]{:S(2)}, u32[]{:S(2)}) %all-to-all-start) | async-done | bytes 393248 | tf_op jit(solution)/shard_map/all_to_all | solution.py:499
  34.0 2.9 %collective-permute-start.3 = (f32[48,128]{1,0:T(8,128)S(1)}, f32[48,128]{1,0:T(8,128)S(1)}, u32[]{:S(2)}, u32[]{:S(2)}) collective-permute-start(f32[48,128]{1,0:T(8,128)S(1)} %shard_map.177.total_ref), channel_id=1, source_target_pairs={{0,112},{16,32},{32,16},{48,64},{64,48},{80,96},{96,80},{112,0},{1... | collective-permute-start | bytes 73736 | tf_op jit(solution)/shard_map/ppermute | solution.py:446
  36.9 1.4 %shard_map.179 = (f32[128,1024]{1,0:T(8,128)S(1)}, bf16[128,240]{1,0:T(8,128)(2,1)S(1)}) custom-call(f32[64,1024]{1,0:T(8,128)S(1)} %get-tuple-element.26.own_ref.sp_ref, f32[64,1024]{1,0:T(8,128)S(1)} %collective-permute-done.4.first_ref, f32[64,1024]{1,0:T(8,128)S(1)} %collective-permute-done.5.second_ref, f32[3,3,3,7,32]{4,3,2,1,0:T(8,128)S(1)} %bitcast.7, ...), custom_call_target="tpu_custom_call" | custom-call | tf_op jit(solution)/shard_map/pallas_call | solution.py:503
  38.2 0.3 collective-permute-done.3.tb_ref
  38.5 1.2 %shard_map.180 = (f32[5,2,1,1024]{3,2,1,0:T(1,128)S(1)}, f32[16,8,4,128]{3,2,1,0:T(4,128)S(1)}) custom-call(f32[48,128]{1,0:T(8,128)S(1)} %shard_map.177.total_ref, f32[48,128]{1,0:T(8,128)S(1)} %collective-permute-done.2.ta_ref, f32[48,128]{1,0:T(8,128)S(1)} %collective-permute-done.3.tb_ref, f32[64,1024]{1,0:T(8,128)S(1)} %get-tuple-element.26.own_ref.sp_ref, ...), custom_call_target="tpu_custom_call" | custom-call | tf_op jit(solution)/shard_map/pallas_call | solution.py:509
  39.7 12.1 %all_to_all.10.nd_ref = f32[16,8,4,128]{3,2,1,0:T(4,128)S(1)} all-to-all(f32[16,8,4,128]{3,2,1,0:T(4,128)S(1)} %get-tuple-element.31), channel_id=1, replica_groups=mesh['plane'=8,'tile'=16] {'tile'}, dimensions={0} | all-to-all | bytes 524288 | tf_op jit(solution)/shard_map/all_to_all | solution.py:516
  51.8 2.8 %copy-done.1 = bf16[16,1536,128]{2,1,0:T(8,128)(2,1)S(1)} copy-done((bf16[16,1536,128]{2,1,0:T(8,128)(2,1)S(1)}, bf16[16,1536,128]{2,1,0:T(8,128)(2,1)}, u32[]{:S(2)}) %copy-start.1) | copy-done | bytes 6291480
  54.6 2.8 %copy-done.3 = bf16[16,1536,128]{2,1,0:T(8,128)(2,1)S(1)} copy-done((bf16[16,1536,128]{2,1,0:T(8,128)(2,1)S(1)}, bf16[16,1536,128]{2,1,0:T(8,128)(2,1)}, u32[]{:S(2)}) %copy-start.3) | copy-done | bytes 6291480
  57.4 6.2 %back.1 = (f32[64,128]{1,0:T(8,128)S(1)}, f32[16,128]{1,0:T(8,128)S(1)}, f32[16,128]{1,0:T(8,128)S(1)}, f32[5,2,1,1024]{3,2,1,0:T(1,128)}) custom-call(s32[12,1,16]{2,1,0:T(1,128)S(1)} %bitcast.9, s32[12,16,16]{2,1,0:T(8,128)S(1)} %bitcast.5, s32[1,16]{1,0:T(1,128)S(1)} %copy-done.11, f32[16,8,4,128]{3,2,1,0:T(4,128)S(1)} %all_to_all.10.nd_ref, ...), custom_call_target="tpu_custom_call" | custom-call | tf_op jit(solution)/shard_map/back/pallas_call | solution.py:518
  63.6 0.5 collective-permute-start.6
  64.1 2.1 %collective-permute-start.7 = (f32[16,128]{1,0:T(8,128)S(1)}, f32[16,128]{1,0:T(8,128)S(1)}, u32[]{:S(2)}, u32[]{:S(2)}) collective-permute-start(f32[16,128]{1,0:T(8,128)S(1)} %get-tuple-element.37), channel_id=1, source_target_pairs={{0,15},{1,2},{2,1},{3,4},{4,3},{5,6},{6,5},{7,8},{8,7},{9,10},{10,... | collective-permute-start | bytes 24584 | tf_op jit(solution)/shard_map/ppermute | solution.py:446
  66.1 1.8 %shard_map.181 = (f32[256,512]{1,0:T(8,128)S(1)}, bf16[256,240]{1,0:T(8,128)(2,1)S(1)}) custom-call(f32[64,1024]{1,0:T(8,128)S(1)} %get-tuple-element.26.own_ref.sp_ref, f32[64,1024]{1,0:T(8,128)S(1)} %get-tuple-element.38.sm_ref, f32[64,1024]{1,0:T(8,128)S(1)} %collective-permute-done.4.first_ref, f32[64,1024]{1,0:T(8,128)S(1)} %collective-permute-done.5.second_ref, ...), custom_call_target="tpu_custom_call" | custom-call | tf_op jit(solution)/shard_map/pallas_call | solution.py:538
  67.9 3.1 %collective-permute-done.7.second_ref = f32[16,128]{1,0:T(8,128)S(1)} collective-permute-done((f32[16,128]{1,0:T(8,128)S(1)}, f32[16,128]{1,0:T(8,128)S(1)}, u32[]{:S(2)}, u32[]{:S(2)}) %collective-permute-start.7) | collective-permute-done | bytes 8224 | tf_op jit(solution)/shard_map/ppermute | solution.py:446
  71.0 1.7 %shard_map.182 = f32[5,2,4,512]{3,2,1,0:T(4,128)} custom-call(f32[64,128]{1,0:T(8,128)S(1)} %get-tuple-element.35.back_ref, f32[16,128]{1,0:T(8,128)S(1)} %collective-permute-done.6.first_ref, f32[16,128]{1,0:T(8,128)S(1)} %collective-permute-done.7.second_ref, f32[256,512]{1,0:T(8,128)S(1)} %get-tuple-element.39.known_ref, ...), custom_call_target="tpu_custom_call" | custom-call | tf_op jit(solution)/shard_map/pallas_call | solution.py:544
  (40 shorter events, 0.2 us)
Async XLA Ops:
  1.6 19.2 %collective-permute-start = (f32[32,1024]{1,0:T(8,128)S(1)}, f32[32,1024]{1,0:T(8,128)S(1)}, u32[]{:S(2)}, u32[]{:S(2)}) collective-permute-start(f32[32,1024]{1,0:T(8,128)S(1)} %shard_map.176.after_ref.own_ref), channel_id=1, source_target_pairs={{0,1},{1,0},{2,3},{3,2},{4,5},{5,4},{6,7},{7,6},{8,9},{9,8},{10,11... | collective-permute-start | bytes 393224 | tf_op jit(solution)/shard_map/ppermute | solution.py:444
  3.7 17.1 %collective-permute-start.1 = (f32[32,1024]{1,0:T(8,128)S(1)}, f32[32,1024]{1,0:T(8,128)S(1)}, u32[]{:S(2)}, u32[]{:S(2)}) collective-permute-start(f32[32,1024]{1,0:T(8,128)S(1)} %shard_map.176.after_ref.own_ref), channel_id=1, source_target_pairs={{0,15},{1,2},{2,1},{3,4},{4,3},{5,6},{6,5},{7,8},{8,7},{9,10},{10,... | collective-permute-start | bytes 393224 | tf_op jit(solution)/shard_map/ppermute | solution.py:446
  8.7 15.7 %copy-start.4 = (f32[5,2,4,512]{3,2,1,0:T(4,128)S(1)}, f32[5,2,4,512]{3,2,1,0:T(4,128)}, u32[]{:S(2)}) copy-start(f32[5,2,4,512]{3,2,1,0:T(4,128)} %primal_ref.3) | copy-start | bytes 245764
  8.7 28.1 %copy-start.7 = (f32[32,7,3,3,3]{0,1,4,3,2:T(8,128)S(1)}, f32[32,7,3,3,3]{0,1,4,3,2:T(8,128)}, u32[]{:S(2)}) copy-start(f32[32,7,3,3,3]{0,1,4,3,2:T(8,128)} %param.24) | copy-start | bytes 72580
  8.7 28.1 %copy-start.14 = (f32[32]{0:T(128)S(1)}, f32[32]{0:T(128)}, u32[]{:S(2)}) copy-start(f32[32]{0:T(128)} %bias_ref.2) | copy-start | bytes 388
  8.7 29.8 %copy-start.9 = (f32[5,32]{1,0:T(8,128)S(1)}, f32[5,32]{1,0:T(8,128)}, u32[]{:S(2)}) copy-start(f32[5,32]{1,0:T(8,128)} %mix_ref.2) | copy-start | bytes 1924
  8.7 29.8 %copy-start.12 = (f32[32]{0:T(128)S(1)}, f32[32]{0:T(128)}, u32[]{:S(2)}) copy-start(f32[32]{0:T(128)} %slope_ref.2) | copy-start | bytes 388
  8.7 29.8 %copy-start.13 = (f32[5]{0:T(128)S(1)}, f32[5]{0:T(128)}, u32[]{:S(2)}) copy-start(f32[5]{0:T(128)} %shift_ref.2) | copy-start | bytes 64
  8.7 43.0 %copy-start.5 = (s32[16,16,12]{1,0,2:T(8,128)S(1)}, s32[16,16,12]{1,0,2:T(8,128)}, u32[]{:S(2)}) copy-start(s32[16,16,12]{1,0,2:T(8,128)} %param.22) | copy-start | bytes 36868
  8.7 43.0 %copy-start.8 = (s32[1,16,12]{1,0,2:T(1,128)S(1)}, s32[1,16,12]{1,0,2:T(1,128)}, u32[]{:S(2)}) copy-start(s32[1,16,12]{1,0,2:T(1,128)} %param.21) | copy-start | bytes 2308
  8.8 43.0 %copy-start.11 = (s32[1,16]{1,0:T(1,128)S(1)}, s32[1,16]{1,0:T(1,128)}, u32[]{:S(2)}) copy-start(s32[1,16]{1,0:T(1,128)} %cnt_ref.1) | copy-start | bytes 196
  20.8 13.0 %all-to-all-start = ((f32[16,3,16,128]{3,2,1,0:T(8,128)}), f32[16,3,16,128]{3,2,1,0:T(8,128)S(1)}, u32[]{:S(2)}, u32[]{:S(2)}) async-start(f32[16,3,16,128]{3,2,1,0:T(8,128)} %get-tuple-element.23), calls=%async_computation | async-start | bytes 786432 | tf_op jit(solution)/shard_map/all_to_all | solution.py:499
  24.5 12.4 %collective-permute-start.4 = (f32[64,1024]{1,0:T(8,128)S(1)}, f32[64,1024]{1,0:T(8,128)S(1)}, u32[]{:S(2)}, u32[]{:S(2)}) collective-permute-start(f32[64,1024]{1,0:T(8,128)S(1)} %get-tuple-element.27), channel_id=1, source_target_pairs={{0,16},{16,0},{32,48},{48,32},{64,80},{80,64},{96,112},{112,96},{1... | collective-permute-start | bytes 786440 | tf_op jit(solution)/shard_map/ppermute | solution.py:444
  24.6 12.3 %collective-permute-start.5 = (f32[64,1024]{1,0:T(8,128)S(1)}, f32[64,1024]{1,0:T(8,128)S(1)}, u32[]{:S(2)}, u32[]{:S(2)}) collective-permute-start(f32[64,1024]{1,0:T(8,128)S(1)} %get-tuple-element.28), channel_id=1, source_target_pairs={{0,112},{16,32},{32,16},{48,64},{64,48},{80,96},{96,80},{112,0},{1... | collective-permute-start | bytes 786440 | tf_op jit(solution)/shard_map/ppermute | solution.py:446
  33.9 4.4 %collective-permute-start.2 = (f32[48,128]{1,0:T(8,128)S(1)}, f32[48,128]{1,0:T(8,128)S(1)}, u32[]{:S(2)}, u32[]{:S(2)}) collective-permute-start(f32[48,128]{1,0:T(8,128)S(1)} %shard_map.177.total_ref), channel_id=1, source_target_pairs={{0,16},{16,0},{32,48},{48,32},{64,80},{80,64},{96,112},{112,96},{1... | collective-permute-start | bytes 73736 | tf_op jit(solution)/shard_map/ppermute | solution.py:444
  34.0 4.5 %collective-permute-start.3 = (f32[48,128]{1,0:T(8,128)S(1)}, f32[48,128]{1,0:T(8,128)S(1)}, u32[]{:S(2)}, u32[]{:S(2)}) collective-permute-start(f32[48,128]{1,0:T(8,128)S(1)} %shard_map.177.total_ref), channel_id=1, source_target_pairs={{0,112},{16,32},{32,16},{48,64},{64,48},{80,96},{96,80},{112,0},{1... | collective-permute-start | bytes 73736 | tf_op jit(solution)/shard_map/ppermute | solution.py:446
  51.8 2.8 %copy-start.1 = (bf16[16,1536,128]{2,1,0:T(8,128)(2,1)S(1)}, bf16[16,1536,128]{2,1,0:T(8,128)(2,1)}, u32[]{:S(2)}) copy-start(bf16[16,1536,128]{2,1,0:T(8,128)(2,1)} %copy-done) | copy-start | bytes 18874372
  57.4 8.8 %copy-start.6 = (f32[32,6,3,3,3]{0,4,3,2,1:T(4,128)S(1)}, f32[32,6,3,3,3]{0,4,3,2,1:T(4,128)}, u32[]{:S(2)}) copy-start(f32[32,6,3,3,3]{0,4,3,2,1:T(4,128)} %param.29) | copy-start | bytes 62212
  57.4 8.8 %copy-start.15 = (f32[32]{0:T(128)S(1)}, f32[32]{0:T(128)}, u32[]{:S(2)}) copy-start(f32[32]{0:T(128)} %bias_ref.3) | copy-start | bytes 388
  57.4 13.7 %copy-start.10 = (f32[5,32]{1,0:T(8,128)S(1)}, f32[5,32]{1,0:T(8,128)}, u32[]{:S(2)}) copy-start(f32[5,32]{1,0:T(8,128)} %mix_ref.3) | copy-start | bytes 1924
  57.4 13.7 %copy-start.16 = (f32[32]{0:T(128)S(1)}, f32[32]{0:T(128)}, u32[]{:S(2)}) copy-start(f32[32]{0:T(128)} %slope_ref.3) | copy-start | bytes 388
  57.4 13.7 %copy-start.17 = (f32[5]{0:T(128)S(1)}, f32[5]{0:T(128)}, u32[]{:S(2)}) copy-start(f32[5]{0:T(128)} %shift_ref.3) | copy-start | bytes 64
  63.6 4.4 %collective-permute-start.6 = (f32[16,128]{1,0:T(8,128)S(1)}, f32[16,128]{1,0:T(8,128)S(1)}, u32[]{:S(2)}, u32[]{:S(2)}) collective-permute-start(f32[16,128]{1,0:T(8,128)S(1)} %get-tuple-element.36), channel_id=1, source_target_pairs={{0,1},{1,0},{2,3},{3,2},{4,5},{5,4},{6,7},{7,6},{8,9},{9,8},{10,11... | collective-permute-start | bytes 24584 | tf_op jit(solution)/shard_map/ppermute | solution.py:444
  64.1 7.0 %collective-permute-start.7 = (f32[16,128]{1,0:T(8,128)S(1)}, f32[16,128]{1,0:T(8,128)S(1)}, u32[]{:S(2)}, u32[]{:S(2)}) collective-permute-start(f32[16,128]{1,0:T(8,128)S(1)} %get-tuple-element.37), channel_id=1, source_target_pairs={{0,15},{1,2},{2,1},{3,4},{4,3},{5,6},{6,5},{7,8},{8,7},{9,10},{10,... | collective-permute-start | bytes 24584 | tf_op jit(solution)/shard_map/ppermute | solution.py:446
  (3 other events, 8.0 us)

commit v6 on v5

--- a/solution.py
+++ b/solution.py
@@ -50,7 +50,14 @@
     return left + mid + right
 
 
-def pack_kernel(dual_hbm, measured_hbm, primal_hbm, out_ref, dual_ref, measured_ref, primal_ref, sem):
+HEAD = 4
+
+
+def pack_kernel(
+    dual_hbm, measured_hbm, primal_hbm, w_hbm,
+    out_ref, head_ref, dual_ref, measured_ref, primal_ref, sem,
+):
+    head = pltpu.make_async_copy(w_hbm.at[0, pl.ds(0, HEAD)], head_ref, sem.at[3])
     copies = [
         pltpu.make_async_copy(src, dst, sem.at[i])
         for i, (src, dst) in enumerate(
@@ -59,6 +66,7 @@
     ]
     for copy in copies:
         copy.start()
+    head.start()
     for copy in copies:
         copy.wait()
     zero = jnp.zeros((1, 1024), F32)
@@ -74,34 +82,35 @@
                 i = 16 + k * 5 + c
                 out_ref[i : i + 1, z * 512 : (z + 1) * 512] = primal_ref[c, z, row : row + 1, :]
     out_ref[26:32, :] = jnp.zeros((6, 1024), F32)
+    head.wait()
+
+
+def index_copies(pix_hbm, bin_hbm, cnt_hbm, pix_ref, bin_ref, cnt_ref, sem):
+    t = lax.axis_index("tile")
+    return [
+        pltpu.make_async_copy(pix_hbm, pix_ref, sem.at[0]),
+        pltpu.make_async_copy(bin_hbm.at[:, pl.ds(t, 1), :], bin_ref, sem.at[1]),
+        pltpu.make_async_copy(cnt_hbm, cnt_ref, sem.at[2]),
+    ]
 
 
 def project_kernel(
-    pix_hbm, bin_hbm, cnt_hbm, primal_hbm, w_hbm, after_ref,
+    pix_hbm, bin_hbm, cnt_hbm, primal_hbm, w_hbm, head_ref,
     final_ref, wh_ref, wl_ref,
     out_ref, hi_ref, lo_ref, hot_ref, pix_ref, bin_ref, cnt_ref, primal_ref, w_ref, sem, w_sem,
 ):
-    del after_ref
-    t = lax.axis_index("tile")
-    copies = [
-        pltpu.make_async_copy(src, dst, sem.at[i])
-        for i, (src, dst) in enumerate(
-            (
-                (primal_hbm.at[1], primal_ref),
-                (pix_hbm, pix_ref),
-                (bin_hbm.at[:, pl.ds(t, 1), :], bin_ref),
-                (cnt_hbm, cnt_ref),
-            )
-        )
-    ]
+    copies = index_copies(pix_hbm, bin_hbm, cnt_hbm, pix_ref, bin_ref, cnt_ref, sem)
+    copies.append(pltpu.make_async_copy(primal_hbm.at[1], primal_ref, sem.at[3]))
     for copy in copies:
         copy.start()
 
     def fetch(i):
-        part = pl.ds(i * 2, 2)
-        return pltpu.make_async_copy(w_hbm.at[0, part], w_ref.at[part], w_sem.at[i])
-
-    for i in range(8):
+        return pltpu.make_async_copy(
+            w_hbm.at[0, pl.ds(HEAD + i * 2, 2)], w_ref.at[pl.ds(i * 2, 2)], w_sem.at[i]
+        )
+
+    rest = (16 - HEAD) // 2
+    for i in range(rest):
         fetch(i).start()
     row = lax.broadcasted_iota(jnp.int32, (16, 128), 0)
     for b in range(9):
@@ -121,7 +130,7 @@
         )
         hi_ref[q], lo_ref[q] = split(v)
 
-    def angle(a):
+    def angle(a, source, at):
         count = cnt_ref[0, a]
         parts = []
         for s in range(12):
@@ -130,7 +139,7 @@
             hot = hot_ref[b]
             parts.append(jnp.concatenate([hi_ref[q] * hot, lo_ref[q] * hot], 0))
         left = jnp.concatenate(parts, 1)
-        w_hi, w_lo = split(w_ref[a].reshape(12 * 128, 128))
+        w_hi, w_lo = split(source[at].reshape(12 * 128, 128))
         wh_ref[a], wl_ref[a] = w_hi, w_lo
         right = jnp.concatenate([w_hi, w_lo], 1)
         d = jnp.dot(left, right, preferred_element_type=F32)
@@ -139,13 +148,19 @@
         out_ref[a, 2] = res
         out_ref[a + 2, 0] = res
 
+    def first(i, carry):
+        for k in (i * 2, i * 2 + 1):
+            angle(k, head_ref, k)
+        return carry
+
     def chunk(i, carry):
         fetch(i).wait()
-        angle(i * 2)
-        angle(i * 2 + 1)
+        for k in (i * 2, i * 2 + 1):
+            angle(HEAD + k, w_ref, k)
         return carry
 
-    lax.fori_loop(0, 8, chunk, 0)
+    lax.fori_loop(0, HEAD // 2, first, 0)
+    lax.fori_loop(0, rest, chunk, 0)
     final_ref[...] = out_ref[1:17]
 
 
@@ -290,13 +305,15 @@
 
 
 def back_kernel(
-    pix_ref, bin_ref, cnt_ref, nd_ref, wh_ref, wl_ref, new_ref,
-    out_ref, first_ref, second_ref, new_hbm, tab_ref, acc_ref, sem,
-):
-    t = lax.axis_index("tile")
+    pix_hbm, bin_hbm, cnt_hbm, nd_ref, wh_ref, wl_ref, new_ref,
+    out_ref, first_ref, second_ref, new_hbm, tab_ref, acc_ref, pix_ref, bin_ref, cnt_ref, sem,
+):
     even = is_even("tile")
-    copy = pltpu.make_async_copy(new_ref, new_hbm, sem)
-    copy.start()
+    copies = index_copies(pix_hbm, bin_hbm, cnt_hbm, pix_ref, bin_ref, cnt_ref, sem)
+    for copy in copies:
+        copy.start()
+    out_copy = pltpu.make_async_copy(new_ref, new_hbm, sem.at[3])
+    out_copy.start()
     for a in range(16):
         for b in range(8):
             v = nd_ref[a, b]
@@ -305,11 +322,13 @@
             tab_ref[a, b, 4:8] = v - hi
     acc_ref[...] = jnp.zeros_like(acc_ref)
     zero = jnp.zeros((8, 128), F32)
+    for copy in copies:
+        copy.wait()
 
     def angle(a):
         count = cnt_ref[0, a]
         for s in range(0, 12, 2):
-            one, two = (tab_ref[a, bin_ref[s + i, t, a]] for i in range(2))
+            one, two = (tab_ref[a, bin_ref[s + i, 0, a]] for i in range(2))
             left = jnp.concatenate(
                 [jnp.concatenate([one, zero], 1), jnp.concatenate([zero, two], 1)], 0
             ).astype(BF16)
@@ -342,7 +361,7 @@
     up, down = out_ref[0:16, :], out_ref[48:64, :]
     first_ref[...] = jnp.where(even, down, up)
     second_ref[...] = jnp.where(even, up, down)
-    copy.wait()
+    out_copy.wait()
 
 
 def primal_known_kernel(
@@ -456,15 +475,16 @@
     bins = jnp.transpose(bin_index, (2, 0, 1))
     hbm = lambda x: pltpu.with_memory_space_constraint(x, pltpu.HBM)
 
-    own = call(
-        pack_kernel, [((32, 1024), F32)], [HBM] * 3,
+    own, head = call(
+        pack_kernel, [((32, 1024), F32), ((HEAD, 12, 128, 128), F32)], [HBM] * 4,
         [
             pltpu.VMEM((5, 2, 1, 1024), F32),
             pltpu.VMEM((2, 1, 1024), F32),
             pltpu.VMEM((5, 2, 4, 512), F32),
-            pltpu.SemaphoreType.DMA((3,)),
+            pltpu.SemaphoreType.DMA((4,)),
         ],
-    )(hbm(dual), hbm(measured), hbm(primal))[0]
+        4 << 20,
+    )(hbm(dual), hbm(measured), hbm(primal), hbm(footprint_weights))
     near = swaps(own, own, "tile")
 
     terms, w_hi, w_lo = pl.pallas_call(
@@ -484,13 +504,13 @@
             pltpu.SMEM((12, 1, 16), jnp.int32),
             pltpu.SMEM((1, 16), jnp.int32),
             pltpu.VMEM((2, 4, 512), F32),
-            pltpu.VMEM((16, 12, 128, 128), F32),
+            pltpu.VMEM((16 - HEAD, 12, 128, 128), F32),
             pltpu.SemaphoreType.DMA((4,)),
             pltpu.SemaphoreType.DMA((8,)),
         ],
         compiler_params=pltpu.CompilerParams(vmem_limit_bytes=18 << 20),
         cost_estimate=pl.CostEstimate(flops=1 << 31, bytes_accessed=25 << 20, transcendentals=0),
-    )(hbm(pix), hbm(bins), hbm(slot_count), hbm(primal), hbm(footprint_weights), own)
+    )(hbm(pix), hbm(bins), hbm(slot_count), hbm(primal), hbm(footprint_weights), head)
     terms, near = lax.optimization_barrier((terms, near))
     sp, sm, side_a, side_b = call(
         rims_kernel, [((64, 1024), F32)] * 4, [VMEM] * 4
@@ -524,15 +544,20 @@
             jax.ShapeDtypeStruct((16, 128), F32),
             jax.ShapeDtypeStruct((5, 2, 1, 1024), F32),
         ),
-        in_specs=[SMEM, SMEM, SMEM, VMEM, VMEM, VMEM, VMEM],
+        in_specs=[HBM, HBM, HBM, VMEM, VMEM, VMEM, VMEM],
         out_specs=(VMEM, VMEM, VMEM, HBM),
         scratch_shapes=[
             pltpu.VMEM((16, 8, 8, 128), F32),
             pltpu.VMEM((17, 8, 128), F32),
-            pltpu.SemaphoreType.DMA,
+            pltpu.SMEM((12, 1, 16), jnp.int32),
+            pltpu.SMEM((12, 1, 16), jnp.int32),
+            pltpu.SMEM((1, 16), jnp.int32),
+            pltpu.SemaphoreType.DMA((4,)),
         ],
         compiler_params=pltpu.CompilerParams(vmem_limit_bytes=4 << 20),
-    )(pix, bins, slot_count, leading, w_hi, w_lo, new_rows)
+    )(
+        hbm(pix), hbm(bins), hbm(slot_count), leading, w_hi, w_lo, new_rows,
+    )
     edges = swaps(edge_a, edge_b, "tile")
 
     known, last = call(

time: 73.1 us -> 73.2 us (level)
    pallas_call x1, Pallas kernels: 6.18 us -> 4.88 us  [per_device(): pl.pallas_call(back_kernel, name='back', out_shape=(jax.ShapeDtypeStruct(...]
    pallas_call x1, Pallas kernels: 0.98 us -> 2.02 us  [per_device(): call(pack_kernel, [((32, 1024), F32), ((HEAD, 12, 128, 128), F32)], [HBM]...]
    unnamed x36 -> x30, local copies, waits for them, and re-layouts: 10.9 us -> 10.9 us
where the time goes in v6:
time: 73.2 us; the launch traced here: 72.8 us
  Pallas kernels  20.2 us (28%)
  starting transfers between devices  19.1 us (26%)
  blocking collectives  12.1 us (17%)
  local copies, waits for them, and re-layouts  10.9 us (15%)
  waiting for transfers between devices  9.83 us (13%)
  between operations  0.8 us (1%)
    ppermute x4, starting transfers between devices, swaps(): b = lax.ppermute(second, axis, pairs)  12.8 us
    all_to_all x1, blocking collectives, per_device(): leading = lax.all_to_all(send, 'tile', 0, 0, tiled=True)  12.1 us
    unnamed x30, local copies, waits for them, and re-layouts  10.9 us
    pallas_call x1, Pallas kernels, per_device(): pl.pallas_call(project_kernel, name='project', out_shape=(jax.ShapeDtypeS...  7.13 us
    all_to_all x1, waiting for transfers between devices, per_device(): got = lax.all_to_all(terms, 'tile', 0, 0, tiled=True)  6.43 us
    pallas_call x1, Pallas kernels, per_device(): pl.pallas_call(back_kernel, name='back', out_shape=(jax.ShapeDtypeStruct(...  4.88 us
    all_to_all x1, starting transfers between devices, per_device(): got = lax.all_to_all(terms, 'tile', 0, 0, tiled=True)  3.55 us
    ppermute x4, waiting for transfers between devices, swaps(): b = lax.ppermute(second, axis, pairs)  3.39 us
  transfers between devices with their start and end apart: 9, of which 3 were waited for; matrix products, arithmetic and copies ran while one was open for 0% of the time, Pallas kernels for 14%

profile of v6, /device:TPU:0, one launch (start us, length us, event | category | flops | bytes accessed | tf_op | source)
XLA Modules:
  0.0 72.8 jit_solution(13580376703165685809)
XLA Ops:
  0.6 2.0 %shard_map.176 = (f32[32,1024]{1,0:T(8,128)S(1)}, f32[4,12,128,128]{3,2,1,0:T(8,128)S(1)}) custom-call(f32[5,2,1,1024]{3,2,1,0:T(1,128)} %dual_hbm.1, f32[2,1,1024]{2,1,0:T(1,128)} %measured_hbm.1, f32[5,2,4,512]{3,2,1,0:T(4,128)} %primal_ref.3, f32[1,16,12,128,128]{4,3,2,1,0:T(8,128)} %w_hbm.3), custom_call_target="tpu_custom_call" | custom-call | tf_op jit(solution)/shard_map/pallas_call | solution.py:478
  2.7 2.1 %collective-permute-start = (f32[32,1024]{1,0:T(8,128)S(1)}, f32[32,1024]{1,0:T(8,128)S(1)}, u32[]{:S(2)}, u32[]{:S(2)}) collective-permute-start(f32[32,1024]{1,0:T(8,128)S(1)} %get-tuple-element.26.own_ref), channel_id=1, source_target_pairs={{0,1},{1,0},{2,3},{3,2},{4,5},{5,4},{6,7},{7,6},{8,9},{9,8},{10,11... | collective-permute-start | bytes 393224 | tf_op jit(solution)/shard_map/ppermute | solution.py:463
  4.8 5.0 %collective-permute-start.1 = (f32[32,1024]{1,0:T(8,128)S(1)}, f32[32,1024]{1,0:T(8,128)S(1)}, u32[]{:S(2)}, u32[]{:S(2)}) collective-permute-start(f32[32,1024]{1,0:T(8,128)S(1)} %get-tuple-element.26.own_ref), channel_id=1, source_target_pairs={{0,15},{1,2},{2,1},{3,4},{4,3},{5,6},{6,5},{7,8},{8,7},{9,10},{10,... | collective-permute-start | bytes 393224 | tf_op jit(solution)/shard_map/ppermute | solution.py:465
  9.8 7.1 %project.1 = (f32[16,3,16,128]{3,2,1,0:T(8,128)}, bf16[16,1536,128]{2,1,0:T(8,128)(2,1)S(1)}, bf16[16,1536,128]{2,1,0:T(8,128)(2,1)S(1)}) custom-call(s32[12,1,16]{2,1,0:T(1,128)} %bitcast.8, s32[12,16,16]{2,1,0:T(8,128)} %bitcast.6, s32[1,16]{1,0:T(1,128)} %cnt_hbm.3, f32[5,2,4,512]{3,2,1,0:T(4,128)} %primal_ref.3, f32[1,16,12,128,128]{4,3,2,1,0:T(8,128)} %w_hbm.3, ...), custom_call_target="tpu_custom_call" | custom-call | flops 2147483648 | bytes 26214400 | tf_op jit(solution)/shard_map/project/pallas_call | solution.py:490
  16.9 2.6 %copy-done = bf16[16,1536,128]{2,1,0:T(8,128)(2,1)} copy-done((bf16[16,1536,128]{2,1,0:T(8,128)(2,1)}, bf16[16,1536,128]{2,1,0:T(8,128)(2,1)S(1)}, u32[]{:S(2)}) %copy-start) | copy-done | bytes 6291480
  19.5 2.6 %copy-done.2 = bf16[16,1536,128]{2,1,0:T(8,128)(2,1)} copy-done((bf16[16,1536,128]{2,1,0:T(8,128)(2,1)}, bf16[16,1536,128]{2,1,0:T(8,128)(2,1)S(1)}, u32[]{:S(2)}) %copy-start.2) | copy-done | bytes 6291480
  22.2 3.6 %all-to-all-start = ((f32[16,3,16,128]{3,2,1,0:T(8,128)}), f32[16,3,16,128]{3,2,1,0:T(8,128)S(1)}, u32[]{:S(2)}, u32[]{:S(2)}) async-start(f32[16,3,16,128]{3,2,1,0:T(8,128)} %get-tuple-element.27), calls=%async_computation | async-start | bytes 786432 | tf_op jit(solution)/shard_map/all_to_all | solution.py:519
  25.7 0.1 shard_map.178
  25.8 0.1 collective-permute-start.4
  25.9 2.9 %collective-permute-start.5 = (f32[64,1024]{1,0:T(8,128)S(1)}, f32[64,1024]{1,0:T(8,128)S(1)}, u32[]{:S(2)}, u32[]{:S(2)}) collective-permute-start(f32[64,1024]{1,0:T(8,128)S(1)} %get-tuple-element.32), channel_id=1, source_target_pairs={{0,112},{16,32},{32,16},{48,64},{64,48},{80,96},{96,80},{112,0},{1... | collective-permute-start | bytes 786440 | tf_op jit(solution)/shard_map/ppermute | solution.py:465
  28.8 6.4 %all-to-all-done.got_ref = f32[16,3,16,128]{3,2,1,0:T(8,128)S(1)} async-done(((f32[16,3,16,128]{3,2,1,0:T(8,128)}), f32[16,3,16,128]{3,2,1,0:T(8,128)S(1)}, u32[]{:S(2)}, u32[]{:S(2)}) %all-to-all-start) | async-done | bytes 393248 | tf_op jit(solution)/shard_map/all_to_all | solution.py:519
  35.3 2.9 %collective-permute-start.3 = (f32[48,128]{1,0:T(8,128)S(1)}, f32[48,128]{1,0:T(8,128)S(1)}, u32[]{:S(2)}, u32[]{:S(2)}) collective-permute-start(f32[48,128]{1,0:T(8,128)S(1)} %shard_map.177.total_ref), channel_id=1, source_target_pairs={{0,112},{16,32},{32,16},{48,64},{64,48},{80,96},{96,80},{112,0},{1... | collective-permute-start | bytes 73736 | tf_op jit(solution)/shard_map/ppermute | solution.py:465
  38.2 1.4 %shard_map.179 = (f32[128,1024]{1,0:T(8,128)S(1)}, bf16[128,240]{1,0:T(8,128)(2,1)S(1)}) custom-call(f32[64,1024]{1,0:T(8,128)S(1)} %get-tuple-element.30.own_ref.sp_ref, f32[64,1024]{1,0:T(8,128)S(1)} %collective-permute-done.4.first_ref, f32[64,1024]{1,0:T(8,128)S(1)} %collective-permute-done.5.second_ref, f32[3,3,3,7,32]{4,3,2,1,0:T(8,128)S(1)} %bitcast.5, ...), custom_call_target="tpu_custom_call" | custom-call | tf_op jit(solution)/shard_map/pallas_call | solution.py:523
  39.6 0.3 collective-permute-done.3.tb_ref
  39.9 1.2 %shard_map.180 = (f32[5,2,1,1024]{3,2,1,0:T(1,128)S(1)}, f32[16,8,4,128]{3,2,1,0:T(4,128)S(1)}) custom-call(f32[48,128]{1,0:T(8,128)S(1)} %shard_map.177.total_ref, f32[48,128]{1,0:T(8,128)S(1)} %collective-permute-done.2.ta_ref, f32[48,128]{1,0:T(8,128)S(1)} %collective-permute-done.3.tb_ref, f32[64,1024]{1,0:T(8,128)S(1)} %get-tuple-element.30.own_ref.sp_ref, ...), custom_call_target="tpu_custom_call" | custom-call | tf_op jit(solution)/shard_map/pallas_call | solution.py:529
  41.1 12.1 %all_to_all.10.nd_ref = f32[16,8,4,128]{3,2,1,0:T(4,128)S(1)} all-to-all(f32[16,8,4,128]{3,2,1,0:T(4,128)S(1)} %get-tuple-element.35), channel_id=1, replica_groups=mesh['plane'=8,'tile'=16] {'tile'}, dimensions={0} | all-to-all | bytes 524288 | tf_op jit(solution)/shard_map/all_to_all | solution.py:536
  53.1 2.8 %copy-done.1 = bf16[16,1536,128]{2,1,0:T(8,128)(2,1)S(1)} copy-done((bf16[16,1536,128]{2,1,0:T(8,128)(2,1)S(1)}, bf16[16,1536,128]{2,1,0:T(8,128)(2,1)}, u32[]{:S(2)}) %copy-start.1) | copy-done | bytes 6291480
  55.9 2.8 %copy-done.3 = bf16[16,1536,128]{2,1,0:T(8,128)(2,1)S(1)} copy-done((bf16[16,1536,128]{2,1,0:T(8,128)(2,1)S(1)}, bf16[16,1536,128]{2,1,0:T(8,128)(2,1)}, u32[]{:S(2)}) %copy-start.3) | copy-done | bytes 6291480
  58.7 4.9 %back.1 = (f32[64,128]{1,0:T(8,128)S(1)}, f32[16,128]{1,0:T(8,128)S(1)}, f32[16,128]{1,0:T(8,128)S(1)}, f32[5,2,1,1024]{3,2,1,0:T(1,128)}) custom-call(s32[12,1,16]{2,1,0:T(1,128)} %bitcast.9, s32[12,16,16]{2,1,0:T(8,128)} %bitcast.7, s32[1,16]{1,0:T(1,128)} %cnt_hbm.3, f32[16,8,4,128]{3,2,1,0:T(4,128)S(1)} %all_to_all.10.nd_ref, ...), custom_call_target="tpu_custom_call" | custom-call | tf_op jit(solution)/shard_map/back/pallas_call | solution.py:538
  63.6 0.5 collective-permute-start.6
  64.1 2.1 %collective-permute-start.7 = (f32[16,128]{1,0:T(8,128)S(1)}, f32[16,128]{1,0:T(8,128)S(1)}, u32[]{:S(2)}, u32[]{:S(2)}) collective-permute-start(f32[16,128]{1,0:T(8,128)S(1)} %get-tuple-element.41), channel_id=1, source_target_pairs={{0,15},{1,2},{2,1},{3,4},{4,3},{5,6},{6,5},{7,8},{8,7},{9,10},{10,... | collective-permute-start | bytes 24584 | tf_op jit(solution)/shard_map/ppermute | solution.py:465
  66.2 1.8 %shard_map.181 = (f32[256,512]{1,0:T(8,128)S(1)}, bf16[256,240]{1,0:T(8,128)(2,1)S(1)}) custom-call(f32[64,1024]{1,0:T(8,128)S(1)} %get-tuple-element.30.own_ref.sp_ref, f32[64,1024]{1,0:T(8,128)S(1)} %get-tuple-element.42.sm_ref, f32[64,1024]{1,0:T(8,128)S(1)} %collective-permute-done.4.first_ref, f32[64,1024]{1,0:T(8,128)S(1)} %collective-permute-done.5.second_ref, ...), custom_call_target="tpu_custom_call" | custom-call | tf_op jit(solution)/shard_map/pallas_call | solution.py:563
  68.0 3.1 %collective-permute-done.7.second_ref = f32[16,128]{1,0:T(8,128)S(1)} collective-permute-done((f32[16,128]{1,0:T(8,128)S(1)}, f32[16,128]{1,0:T(8,128)S(1)}, u32[]{:S(2)}, u32[]{:S(2)}) %collective-permute-start.7) | collective-permute-done | bytes 8224 | tf_op jit(solution)/shard_map/ppermute | solution.py:465
  71.1 1.7 %shard_map.182 = f32[5,2,4,512]{3,2,1,0:T(4,128)} custom-call(f32[64,128]{1,0:T(8,128)S(1)} %get-tuple-element.39.back_ref, f32[16,128]{1,0:T(8,128)S(1)} %collective-permute-done.6.first_ref, f32[16,128]{1,0:T(8,128)S(1)} %collective-permute-done.7.second_ref, f32[256,512]{1,0:T(8,128)S(1)} %get-tuple-element.43.known_ref, ...), custom_call_target="tpu_custom_call" | custom-call | tf_op jit(solution)/shard_map/pallas_call | solution.py:569
  (34 shorter events, 0.2 us)
Async XLA Ops:
  2.7 19.5 %collective-permute-start = (f32[32,1024]{1,0:T(8,128)S(1)}, f32[32,1024]{1,0:T(8,128)S(1)}, u32[]{:S(2)}, u32[]{:S(2)}) collective-permute-start(f32[32,1024]{1,0:T(8,128)S(1)} %get-tuple-element.26.own_ref), channel_id=1, source_target_pairs={{0,1},{1,0},{2,3},{3,2},{4,5},{5,4},{6,7},{7,6},{8,9},{9,8},{10,11... | collective-permute-start | bytes 393224 | tf_op jit(solution)/shard_map/ppermute | solution.py:463
  4.8 17.4 %collective-permute-start.1 = (f32[32,1024]{1,0:T(8,128)S(1)}, f32[32,1024]{1,0:T(8,128)S(1)}, u32[]{:S(2)}, u32[]{:S(2)}) collective-permute-start(f32[32,1024]{1,0:T(8,128)S(1)} %get-tuple-element.26.own_ref), channel_id=1, source_target_pairs={{0,15},{1,2},{2,1},{3,4},{4,3},{5,6},{6,5},{7,8},{8,7},{9,10},{10,... | collective-permute-start | bytes 393224 | tf_op jit(solution)/shard_map/ppermute | solution.py:465
  9.7 16.0 %copy-start.4 = (f32[5,2,4,512]{3,2,1,0:T(4,128)S(1)}, f32[5,2,4,512]{3,2,1,0:T(4,128)}, u32[]{:S(2)}) copy-start(f32[5,2,4,512]{3,2,1,0:T(4,128)} %primal_ref.3) | copy-start | bytes 245764
  9.7 28.5 %copy-start.6 = (f32[32,7,3,3,3]{0,1,4,3,2:T(8,128)S(1)}, f32[32,7,3,3,3]{0,1,4,3,2:T(8,128)}, u32[]{:S(2)}) copy-start(f32[32,7,3,3,3]{0,1,4,3,2:T(8,128)} %param.24) | copy-start | bytes 72580
  9.7 28.5 %copy-start.11 = (f32[32]{0:T(128)S(1)}, f32[32]{0:T(128)}, u32[]{:S(2)}) copy-start(f32[32]{0:T(128)} %bias_ref.2) | copy-start | bytes 388
  9.7 30.1 %copy-start.7 = (f32[5,32]{1,0:T(8,128)S(1)}, f32[5,32]{1,0:T(8,128)}, u32[]{:S(2)}) copy-start(f32[5,32]{1,0:T(8,128)} %mix_ref.2) | copy-start | bytes 1924
  9.7 30.1 %copy-start.9 = (f32[32]{0:T(128)S(1)}, f32[32]{0:T(128)}, u32[]{:S(2)}) copy-start(f32[32]{0:T(128)} %slope_ref.2) | copy-start | bytes 388
  9.8 30.1 %copy-start.10 = (f32[5]{0:T(128)S(1)}, f32[5]{0:T(128)}, u32[]{:S(2)}) copy-start(f32[5]{0:T(128)} %shift_ref.2) | copy-start | bytes 64
  16.9 2.6 %copy-start = (bf16[16,1536,128]{2,1,0:T(8,128)(2,1)}, bf16[16,1536,128]{2,1,0:T(8,128)(2,1)S(1)}, u32[]{:S(2)}) copy-start(bf16[16,1536,128]{2,1,0:T(8,128)(2,1)S(1)} %get-tuple-element.36.wh_ref) | copy-start | bytes 18874372
  19.5 2.6 %copy-start.2 = (bf16[16,1536,128]{2,1,0:T(8,128)(2,1)}, bf16[16,1536,128]{2,1,0:T(8,128)(2,1)S(1)}, u32[]{:S(2)}) copy-start(bf16[16,1536,128]{2,1,0:T(8,128)(2,1)S(1)} %get-tuple-element.37.wl_ref) | copy-start | bytes 18874372
  22.2 13.0 %all-to-all-start = ((f32[16,3,16,128]{3,2,1,0:T(8,128)}), f32[16,3,16,128]{3,2,1,0:T(8,128)S(1)}, u32[]{:S(2)}, u32[]{:S(2)}) async-start(f32[16,3,16,128]{3,2,1,0:T(8,128)} %get-tuple-element.27), calls=%async_computation | async-start | bytes 786432 | tf_op jit(solution)/shard_map/all_to_all | solution.py:519
  25.8 12.4 %collective-permute-start.4 = (f32[64,1024]{1,0:T(8,128)S(1)}, f32[64,1024]{1,0:T(8,128)S(1)}, u32[]{:S(2)}, u32[]{:S(2)}) collective-permute-start(f32[64,1024]{1,0:T(8,128)S(1)} %get-tuple-element.31), channel_id=1, source_target_pairs={{0,16},{16,0},{32,48},{48,32},{64,80},{80,64},{96,112},{112,96},{1... | collective-permute-start | bytes 786440 | tf_op jit(solution)/shard_map/ppermute | solution.py:463
  25.9 12.3 %collective-permute-start.5 = (f32[64,1024]{1,0:T(8,128)S(1)}, f32[64,1024]{1,0:T(8,128)S(1)}, u32[]{:S(2)}, u32[]{:S(2)}) collective-permute-start(f32[64,1024]{1,0:T(8,128)S(1)} %get-tuple-element.32), channel_id=1, source_target_pairs={{0,112},{16,32},{32,16},{48,64},{64,48},{80,96},{96,80},{112,0},{1... | collective-permute-start | bytes 786440 | tf_op jit(solution)/shard_map/ppermute | solution.py:465
  35.2 4.4 %collective-permute-start.2 = (f32[48,128]{1,0:T(8,128)S(1)}, f32[48,128]{1,0:T(8,128)S(1)}, u32[]{:S(2)}, u32[]{:S(2)}) collective-permute-start(f32[48,128]{1,0:T(8,128)S(1)} %shard_map.177.total_ref), channel_id=1, source_target_pairs={{0,16},{16,0},{32,48},{48,32},{64,80},{80,64},{96,112},{112,96},{1... | collective-permute-start | bytes 73736 | tf_op jit(solution)/shard_map/ppermute | solution.py:463
  35.3 4.5 %collective-permute-start.3 = (f32[48,128]{1,0:T(8,128)S(1)}, f32[48,128]{1,0:T(8,128)S(1)}, u32[]{:S(2)}, u32[]{:S(2)}) collective-permute-start(f32[48,128]{1,0:T(8,128)S(1)} %shard_map.177.total_ref), channel_id=1, source_target_pairs={{0,112},{16,32},{32,16},{48,64},{64,48},{80,96},{96,80},{112,0},{1... | collective-permute-start | bytes 73736 | tf_op jit(solution)/shard_map/ppermute | solution.py:465
  53.1 2.8 %copy-start.1 = (bf16[16,1536,128]{2,1,0:T(8,128)(2,1)S(1)}, bf16[16,1536,128]{2,1,0:T(8,128)(2,1)}, u32[]{:S(2)}) copy-start(bf16[16,1536,128]{2,1,0:T(8,128)(2,1)} %copy-done) | copy-start | bytes 18874372
  55.9 2.8 %copy-start.3 = (bf16[16,1536,128]{2,1,0:T(8,128)(2,1)S(1)}, bf16[16,1536,128]{2,1,0:T(8,128)(2,1)}, u32[]{:S(2)}) copy-start(bf16[16,1536,128]{2,1,0:T(8,128)(2,1)} %copy-done.2) | copy-start | bytes 18874372
  58.7 7.5 %copy-start.5 = (f32[32,6,3,3,3]{0,4,3,2,1:T(4,128)S(1)}, f32[32,6,3,3,3]{0,4,3,2,1:T(4,128)}, u32[]{:S(2)}) copy-start(f32[32,6,3,3,3]{0,4,3,2,1:T(4,128)} %param.29) | copy-start | bytes 62212
  58.7 7.5 %copy-start.12 = (f32[32]{0:T(128)S(1)}, f32[32]{0:T(128)}, u32[]{:S(2)}) copy-start(f32[32]{0:T(128)} %bias_ref.3) | copy-start | bytes 388
  58.7 12.4 %copy-start.8 = (f32[5,32]{1,0:T(8,128)S(1)}, f32[5,32]{1,0:T(8,128)}, u32[]{:S(2)}) copy-start(f32[5,32]{1,0:T(8,128)} %mix_ref.3) | copy-start | bytes 1924
  58.7 12.4 %copy-start.13 = (f32[32]{0:T(128)S(1)}, f32[32]{0:T(128)}, u32[]{:S(2)}) copy-start(f32[32]{0:T(128)} %slope_ref.3) | copy-start | bytes 388
  58.7 12.4 %copy-start.14 = (f32[5]{0:T(128)S(1)}, f32[5]{0:T(128)}, u32[]{:S(2)}) copy-start(f32[5]{0:T(128)} %shift_ref.3) | copy-start | bytes 64
  63.6 4.3 %collective-permute-start.6 = (f32[16,128]{1,0:T(8,128)S(1)}, f32[16,128]{1,0:T(8,128)S(1)}, u32[]{:S(2)}, u32[]{:S(2)}) collective-permute-start(f32[16,128]{1,0:T(8,128)S(1)} %get-tuple-element.40), channel_id=1, source_target_pairs={{0,1},{1,0},{2,3},{3,2},{4,5},{5,4},{6,7},{7,6},{8,9},{9,8},{10,11... | collective-permute-start | bytes 24584 | tf_op jit(solution)/shard_map/ppermute | solution.py:463
  64.1 7.0 %collective-permute-start.7 = (f32[16,128]{1,0:T(8,128)S(1)}, f32[16,128]{1,0:T(8,128)S(1)}, u32[]{:S(2)}, u32[]{:S(2)}) collective-permute-start(f32[16,128]{1,0:T(8,128)S(1)} %get-tuple-element.41), channel_id=1, source_target_pairs={{0,15},{1,2},{2,1},{3,4},{4,3},{5,6},{6,5},{7,8},{8,7},{9,10},{10,... | collective-permute-start | bytes 24584 | tf_op jit(solution)/shard_map/ppermute | solution.py:465

commit v7 on v6

--- a/solution.py
+++ b/solution.py
@@ -50,14 +50,12 @@
     return left + mid + right
 
 
-HEAD = 4
-
-
-def pack_kernel(
-    dual_hbm, measured_hbm, primal_hbm, w_hbm,
-    out_ref, head_ref, dual_ref, measured_ref, primal_ref, sem,
-):
-    head = pltpu.make_async_copy(w_hbm.at[0, pl.ds(0, HEAD)], head_ref, sem.at[3])
+CHUNK = 8
+ROOM = 96 + CHUNK
+SURE = 48
+
+
+def pack_kernel(dual_hbm, measured_hbm, primal_hbm, out_ref, dual_ref, measured_ref, primal_ref, sem):
     copies = [
         pltpu.make_async_copy(src, dst, sem.at[i])
         for i, (src, dst) in enumerate(
@@ -66,7 +64,6 @@
     ]
     for copy in copies:
         copy.start()
-    head.start()
     for copy in copies:
         copy.wait()
     zero = jnp.zeros((1, 1024), F32)
@@ -82,7 +79,6 @@
                 i = 16 + k * 5 + c
                 out_ref[i : i + 1, z * 512 : (z + 1) * 512] = primal_ref[c, z, row : row + 1, :]
     out_ref[26:32, :] = jnp.zeros((6, 1024), F32)
-    head.wait()
 
 
 def index_copies(pix_hbm, bin_hbm, cnt_hbm, pix_ref, bin_ref, cnt_ref, sem):
@@ -94,31 +90,59 @@
     ]
 
 
+def list_pairs(cnt_ref, list_ref):
+    base = 0
+    for a in range(16):
+        for k in range(3):
+            list_ref[base + k] = a * 8 + 3 + k
+        base = base + ((cnt_ref[0, a] - 5) >> 1)
+    for k in range(CHUNK):
+        list_ref[base + k] = 128 + 3
+    return (base + CHUNK - 1) // CHUNK
+
+
+def pair_at(list_ref, cnt_ref, i):
+    code = list_ref[i]
+    a, k = (code >> 3) & 15, code & 7
+    return a, k, jnp.where(code < 128, cnt_ref[0, a], 0)
+
+
 def project_kernel(
-    pix_hbm, bin_hbm, cnt_hbm, primal_hbm, w_hbm, head_ref,
-    final_ref, wh_ref, wl_ref,
-    out_ref, hi_ref, lo_ref, hot_ref, pix_ref, bin_ref, cnt_ref, primal_ref, w_ref, sem, w_sem,
+    pix_hbm, bin_hbm, cnt_hbm, primal_hbm, w_hbm, after_ref,
+    out_ref, wh_ref, wl_ref,
+    acc_ref, hi_ref, lo_ref, hot_ref, pix_ref, bin_ref, cnt_ref, list_ref, primal_ref, w_ref,
+    sem, sure_sem, w_sem,
 ):
+    del after_ref
     copies = index_copies(pix_hbm, bin_hbm, cnt_hbm, pix_ref, bin_ref, cnt_ref, sem)
     copies.append(pltpu.make_async_copy(primal_hbm.at[1], primal_ref, sem.at[3]))
-    for copy in copies:
+    for copy in copies[::-1]:
         copy.start()
 
+    def fetch_sure(a):
+        return pltpu.make_async_copy(
+            w_hbm.at[a, pl.ds(0, 3)], w_ref.at[pl.ds(a * 3, 3)], sure_sem.at[a]
+        )
+
     def fetch(i):
-        return pltpu.make_async_copy(
-            w_hbm.at[0, pl.ds(HEAD + i * 2, 2)], w_ref.at[pl.ds(i * 2, 2)], w_sem.at[i]
-        )
-
-    rest = (16 - HEAD) // 2
-    for i in range(rest):
-        fetch(i).start()
+        a, k, _ = pair_at(list_ref, cnt_ref, i)
+        return pltpu.make_async_copy(w_hbm.at[a, k], w_ref.at[SURE + i], w_sem.at[i])
+
+    for a in range(16):
+        fetch_sure(a).start()
+    copies[2].wait()
+    steps = list_pairs(cnt_ref, list_ref)
+    for c in range(6):
+
+        @pl.when(c < steps)
+        def _():
+            for j in range(CHUNK):
+                fetch(c * CHUNK + j).start()
+
     row = lax.broadcasted_iota(jnp.int32, (16, 128), 0)
     for b in range(9):
         hot_ref[b] = jnp.where((row & 7) == b, 1.0, 0.0).astype(BF16)
-    out_ref[1, 0] = jnp.zeros((16, 128), F32)
-    out_ref[16, 2] = jnp.zeros((16, 128), F32)
-    for copy in copies:
-        copy.wait()
+    copies[3].wait()
     for q in range(16):
         r, col = q // 4, (q % 4) * 128
         v = jnp.concatenate(
@@ -129,39 +153,47 @@
             0,
         )
         hi_ref[q], lo_ref[q] = split(v)
-
-    def angle(a, source, at):
-        count = cnt_ref[0, a]
+    copies[0].wait()
+    copies[1].wait()
+
+    def operands(i, a, k, count):
         parts = []
-        for s in range(12):
-            q = pix_ref[s, 0, a]
-            b = jnp.where(s < count, bin_ref[s, 0, a], 8)
-            hot = hot_ref[b]
+        for s in (k * 2, k * 2 + 1):
+            q, b = pix_ref[s, 0, a], bin_ref[s, 0, a]
+            hot = hot_ref[b if count is None else jnp.where(s < count, b, 8)]
             parts.append(jnp.concatenate([hi_ref[q] * hot, lo_ref[q] * hot], 0))
-        left = jnp.concatenate(parts, 1)
-        w_hi, w_lo = split(source[at].reshape(12 * 128, 128))
-        wh_ref[a], wl_ref[a] = w_hi, w_lo
-        right = jnp.concatenate([w_hi, w_lo], 1)
+        w_hi, w_lo = split(w_ref[i])
+        wh_ref[i], wl_ref[i] = w_hi, w_lo
+        return jnp.concatenate(parts, 1), jnp.concatenate([w_hi, w_lo], 1)
+
+    def product(left, right):
         d = jnp.dot(left, right, preferred_element_type=F32)
-        res = d[0:16, 0:128] + (d[0:16, 128:256] + d[16:32, 0:128])
-        out_ref[a + 1, 1] = res
-        out_ref[a, 2] = res
-        out_ref[a + 2, 0] = res
-
-    def first(i, carry):
-        for k in (i * 2, i * 2 + 1):
-            angle(k, head_ref, k)
+        return d[0:16, 0:128] + (d[0:16, 128:256] + d[16:32, 0:128])
+
+    def sure_step(c, carry):
+        for j in range(4):
+            fetch_sure(c * 4 + j).wait()
+        for j in range(4):
+            a = c * 4 + j
+            lefts, rights = zip(*(operands(a * 3 + k, a, k, None) for k in range(3)))
+            acc_ref[a] = product(jnp.concatenate(lefts, 1), jnp.concatenate(rights, 0))
         return carry
 
-    def chunk(i, carry):
-        fetch(i).wait()
-        for k in (i * 2, i * 2 + 1):
-            angle(HEAD + k, w_ref, k)
+    def step(c, carry):
+        for j in range(CHUNK):
+            fetch(c * CHUNK + j).wait()
+        for j in range(CHUNK):
+            i = c * CHUNK + j
+            a, k, count = pair_at(list_ref, cnt_ref, i)
+            acc_ref[a] += product(*operands(SURE + i, a, k, count))
         return carry
 
-    lax.fori_loop(0, HEAD // 2, first, 0)
-    lax.fori_loop(0, rest, chunk, 0)
-    final_ref[...] = out_ref[1:17]
+    lax.fori_loop(0, 4, sure_step, 0)
+    lax.fori_loop(0, steps, step, 0)
+    zero = jnp.zeros((16, 128), F32)
+    for a in range(16):
+        for k in range(3):
+            out_ref[a, k] = acc_ref[a + k - 1] if 0 <= a + k - 1 < 16 else zero
 
 
 def rims_kernel(own_ref, first_ref, second_ref, primal_ref, sp_ref, sm_ref, a_ref, b_ref):
@@ -306,7 +338,8 @@
 
 def back_kernel(
     pix_hbm, bin_hbm, cnt_hbm, nd_ref, wh_ref, wl_ref, new_ref,
-    out_ref, first_ref, second_ref, new_hbm, tab_ref, acc_ref, pix_ref, bin_ref, cnt_ref, sem,
+    out_ref, first_ref, second_ref, new_hbm, tab_ref, acc_ref, pix_ref, bin_ref, cnt_ref, list_ref,
+    sem,
 ):
     even = is_even("tile")
     copies = index_copies(pix_hbm, bin_hbm, cnt_hbm, pix_ref, bin_ref, cnt_ref, sem)
@@ -325,36 +358,38 @@
     for copy in copies:
         copy.wait()
 
-    def angle(a):
-        count = cnt_ref[0, a]
-        for s in range(0, 12, 2):
-            one, two = (tab_ref[a, bin_ref[s + i, 0, a]] for i in range(2))
-            left = jnp.concatenate(
-                [jnp.concatenate([one, zero], 1), jnp.concatenate([zero, two], 1)], 0
-            ).astype(BF16)
-            right = jnp.concatenate(
-                [
-                    jnp.concatenate(
-                        [w[a, (s + i) * 128 : (s + i + 1) * 128, :] for i in range(2)], 1
-                    )
-                    for w in (wh_ref, wl_ref)
-                ],
-                0,
-            )
-            d = lax.dot_general(
-                left, right, (((1,), (1,)), ((), ())), preferred_element_type=F32
-            )
-            d = d[:, 0:128] + d[:, 128:256]
-            for i in range(2):
-                q = jnp.where(s + i < count, pix_ref[s + i, 0, a], 16)
-                acc_ref[q] += d[i * 8 : i * 8 + 8]
-
-    def chunk(i, carry):
-        for k in range(4):
-            angle(i * 4 + k)
+    steps = list_pairs(cnt_ref, list_ref)
+
+    def pair(i, a, k, count):
+        slots = (k * 2, k * 2 + 1)
+        one, two = (tab_ref[a, bin_ref[s, 0, a]] for s in slots)
+        left = jnp.concatenate(
+            [jnp.concatenate([one, zero], 1), jnp.concatenate([zero, two], 1)], 0
+        ).astype(BF16)
+        right = jnp.concatenate(
+            [jnp.concatenate([w[i, 0:128, :], w[i, 128:256, :]], 1) for w in (wh_ref, wl_ref)], 0
+        )
+        d = lax.dot_general(left, right, (((1,), (1,)), ((), ())), preferred_element_type=F32)
+        d = d[:, 0:128] + d[:, 128:256]
+        for n, s in enumerate(slots):
+            q = pix_ref[s, 0, a]
+            acc_ref[q if count is None else jnp.where(s < count, q, 16)] += d[n * 8 : n * 8 + 8]
+
+    def sure_step(c, carry):
+        for j in range(4):
+            for k in range(3):
+                a = c * 4 + j
+                pair(a * 3 + k, a, k, None)
         return carry
 
-    lax.fori_loop(0, 4, chunk, 0)
+    def step(c, carry):
+        for j in range(CHUNK):
+            i = c * CHUNK + j
+            pair(SURE + i, *pair_at(list_ref, cnt_ref, i))
+        return carry
+
+    lax.fori_loop(0, 4, sure_step, 0)
+    lax.fori_loop(0, steps, step, 0)
     for q in range(16):
         v = acc_ref[q, 0:4] + acc_ref[q, 4:8]
         out_ref[q * 4 : q * 4 + 4, :] = v
@@ -475,16 +510,17 @@
     bins = jnp.transpose(bin_index, (2, 0, 1))
     hbm = lambda x: pltpu.with_memory_space_constraint(x, pltpu.HBM)
 
-    own, head = call(
-        pack_kernel, [((32, 1024), F32), ((HEAD, 12, 128, 128), F32)], [HBM] * 4,
+    own = call(
+        pack_kernel, [((32, 1024), F32)], [HBM] * 3,
         [
             pltpu.VMEM((5, 2, 1, 1024), F32),
             pltpu.VMEM((2, 1, 1024), F32),
             pltpu.VMEM((5, 2, 4, 512), F32),
-            pltpu.SemaphoreType.DMA((4,)),
+            pltpu.SemaphoreType.DMA((3,)),
         ],
-        4 << 20,
-    )(hbm(dual), hbm(measured), hbm(primal), hbm(footprint_weights))
+    )(hbm(dual), hbm(measured), hbm(primal))[0]
+    pairs = footprint_weights.reshape(16, 6, 256, 128)
+
     near = swaps(own, own, "tile")
 
     terms, w_hi, w_lo = pl.pallas_call(
@@ -492,25 +528,27 @@
         name="project",
         out_shape=(
             jax.ShapeDtypeStruct((16, 3, 16, 128), F32),
-            jax.ShapeDtypeStruct((16, 1536, 128), BF16),
-            jax.ShapeDtypeStruct((16, 1536, 128), BF16),
+            jax.ShapeDtypeStruct((ROOM, 256, 128), BF16),
+            jax.ShapeDtypeStruct((ROOM, 256, 128), BF16),
         ),
         in_specs=[HBM] * 5 + [VMEM],
         out_specs=(VMEM, VMEM, VMEM),
-        scratch_shapes=[pltpu.VMEM((18, 3, 16, 128), F32)]
+        scratch_shapes=[pltpu.VMEM((16, 16, 128), F32)]
         + [pltpu.VMEM((16, 16, 128), BF16)] * 3
         + [
             pltpu.SMEM((12, 1, 16), jnp.int32),
             pltpu.SMEM((12, 1, 16), jnp.int32),
             pltpu.SMEM((1, 16), jnp.int32),
+            pltpu.SMEM((128,), jnp.int32),
             pltpu.VMEM((2, 4, 512), F32),
-            pltpu.VMEM((16 - HEAD, 12, 128, 128), F32),
+            pltpu.VMEM((ROOM, 256, 128), F32),
             pltpu.SemaphoreType.DMA((4,)),
-            pltpu.SemaphoreType.DMA((8,)),
+            pltpu.SemaphoreType.DMA((16,)),
+            pltpu.SemaphoreType.DMA((ROOM - SURE,)),
         ],
         compiler_params=pltpu.CompilerParams(vmem_limit_bytes=18 << 20),
         cost_estimate=pl.CostEstimate(flops=1 << 31, bytes_accessed=25 << 20, transcendentals=0),
-    )(hbm(pix), hbm(bins), hbm(slot_count), hbm(primal), hbm(footprint_weights), head)
+    )(hbm(pix), hbm(bins), hbm(slot_count), hbm(primal), hbm(pairs), own)
     terms, near = lax.optimization_barrier((terms, near))
     sp, sm, side_a, side_b = call(
         rims_kernel, [((64, 1024), F32)] * 4, [VMEM] * 4
@@ -552,6 +590,7 @@
             pltpu.SMEM((12, 1, 16), jnp.int32),
             pltpu.SMEM((12, 1, 16), jnp.int32),
             pltpu.SMEM((1, 16), jnp.int32),
+            pltpu.SMEM((128,), jnp.int32),
             pltpu.SemaphoreType.DMA((4,)),
         ],
         compiler_params=pltpu.CompilerParams(vmem_limit_bytes=4 << 20),

time: 73.2 us -> 72.7 us (level)
  Pallas kernels: 20.2 us -> 19.3 us
    pallas_call x1, Pallas kernels: 2.02 us -> 0.98 us  [per_device(): call(pack_kernel, [((32, 1024), F32)], [HBM] * 3, [pltpu.VMEM((5, 2, 1, 1...]
    unnamed x30, local copies, waits for them, and re-layouts: 10.9 us -> 11.6 us
where the time goes in v7:
time: 72.7 us; the launch traced here: 72.3 us
  Pallas kernels  19.3 us (27%)
  starting transfers between devices  18.6 us (26%)
  blocking collectives  12.1 us (17%)
  local copies, waits for them, and re-layouts  11.6 us (16%)
  waiting for transfers between devices  9.92 us (14%)
  between operations  0.81 us (1%)
    ppermute x4, starting transfers between devices, swaps(): b = lax.ppermute(second, axis, pairs)  12.7 us
    all_to_all x1, blocking collectives, per_device(): leading = lax.all_to_all(send, 'tile', 0, 0, tiled=True)  12.1 us
    unnamed x30, local copies, waits for them, and re-layouts  11.6 us
    pallas_call x1, Pallas kernels, per_device(): pl.pallas_call(project_kernel, name='project', out_shape=(jax.ShapeDtypeS...  6.87 us
    all_to_all x1, waiting for transfers between devices, per_device(): got = lax.all_to_all(terms, 'tile', 0, 0, tiled=True)  6.42 us
    pallas_call x1, Pallas kernels, per_device(): pl.pallas_call(back_kernel, name='back', out_shape=(jax.ShapeDtypeStruct(...  5.27 us
    all_to_all x1, starting transfers between devices, per_device(): got = lax.all_to_all(terms, 'tile', 0, 0, tiled=True)  3.55 us
    ppermute x4, waiting for transfers between devices, swaps(): b = lax.ppermute(second, axis, pairs)  3.49 us
  transfers between devices with their start and end apart: 9, of which 3 were waited for; matrix products, arithmetic and copies ran while one was open for 0% of the time, Pallas kernels for 14%

profile of v7, /device:TPU:0, one launch (start us, length us, event | category | flops | bytes accessed | tf_op | source)
XLA Modules:
  0.0 72.3 jit_solution(5286558245624699559)
XLA Ops:
  0.6 1.0 %shard_map.176.after_ref.own_ref = f32[32,1024]{1,0:T(8,128)S(1)} custom-call(f32[5,2,1,1024]{3,2,1,0:T(1,128)} %dual_hbm.1, f32[2,1,1024]{2,1,0:T(1,128)} %measured_hbm.1, f32[5,2,4,512]{3,2,1,0:T(4,128)} %primal_ref.3), custom_call_target="tpu_custom_call" | custom-call | tf_op jit(solution)/shard_map/pallas_call | solution.py:513
  1.6 2.1 %collective-permute-start = (f32[32,1024]{1,0:T(8,128)S(1)}, f32[32,1024]{1,0:T(8,128)S(1)}, u32[]{:S(2)}, u32[]{:S(2)}) collective-permute-start(f32[32,1024]{1,0:T(8,128)S(1)} %shard_map.176.after_ref.own_ref), channel_id=1, source_target_pairs={{0,1},{1,0},{2,3},{3,2},{4,5},{5,4},{6,7},{7,6},{8,9},{9,8},{10,11... | collective-permute-start | bytes 393224 | tf_op jit(solution)/shard_map/ppermute | solution.py:498
  3.7 5.0 %collective-permute-start.1 = (f32[32,1024]{1,0:T(8,128)S(1)}, f32[32,1024]{1,0:T(8,128)S(1)}, u32[]{:S(2)}, u32[]{:S(2)}) collective-permute-start(f32[32,1024]{1,0:T(8,128)S(1)} %shard_map.176.after_ref.own_ref), channel_id=1, source_target_pairs={{0,15},{1,2},{2,1},{3,4},{4,3},{5,6},{6,5},{7,8},{8,7},{9,10},{10,... | collective-permute-start | bytes 393224 | tf_op jit(solution)/shard_map/ppermute | solution.py:500
  8.7 6.9 %project.1 = (f32[16,3,16,128]{3,2,1,0:T(8,128)}, bf16[104,256,128]{2,1,0:T(8,128)(2,1)S(1)}, bf16[104,256,128]{2,1,0:T(8,128)(2,1)S(1)}) custom-call(s32[12,1,16]{2,1,0:T(1,128)} %bitcast.10, s32[12,16,16]{2,1,0:T(8,128)} %bitcast.8, s32[1,16]{1,0:T(1,128)} %cnt_hbm.3, f32[5,2,4,512]{3,2,1,0:T(4,128)} %primal_ref.3, f32[16,6,256,128]{3,2,1,0:T(8,128)} %bitcast.7, ...), custom_call_target="tpu_custom_call" | custom-call | flops 2147483648 | bytes 26214400 | tf_op jit(solution)/shard_map/project/pallas_call | solution.py:526
  15.6 2.8 %copy-done = bf16[104,256,128]{2,1,0:T(8,128)(2,1)} copy-done((bf16[104,256,128]{2,1,0:T(8,128)(2,1)}, bf16[104,256,128]{2,1,0:T(8,128)(2,1)S(1)}, u32[]{:S(2)}) %copy-start) | copy-done | bytes 6815768
  18.4 2.9 %copy-done.2 = bf16[104,256,128]{2,1,0:T(8,128)(2,1)} copy-done((bf16[104,256,128]{2,1,0:T(8,128)(2,1)}, bf16[104,256,128]{2,1,0:T(8,128)(2,1)S(1)}, u32[]{:S(2)}) %copy-start.2) | copy-done | bytes 6815768
  21.3 3.6 %all-to-all-start = ((f32[16,3,16,128]{3,2,1,0:T(8,128)}), f32[16,3,16,128]{3,2,1,0:T(8,128)S(1)}, u32[]{:S(2)}, u32[]{:S(2)}) async-start(f32[16,3,16,128]{3,2,1,0:T(8,128)} %get-tuple-element.23), calls=%async_computation | async-start | bytes 786432 | tf_op jit(solution)/shard_map/all_to_all | solution.py:557
  24.9 0.1 shard_map.178
  25.0 0.1 collective-permute-start.4
  25.1 2.9 %collective-permute-start.5 = (f32[64,1024]{1,0:T(8,128)S(1)}, f32[64,1024]{1,0:T(8,128)S(1)}, u32[]{:S(2)}, u32[]{:S(2)}) collective-permute-start(f32[64,1024]{1,0:T(8,128)S(1)} %get-tuple-element.28), channel_id=1, source_target_pairs={{0,112},{16,32},{32,16},{48,64},{64,48},{80,96},{96,80},{112,0},{1... | collective-permute-start | bytes 786440 | tf_op jit(solution)/shard_map/ppermute | solution.py:500
  27.9 6.4 %all-to-all-done.got_ref = f32[16,3,16,128]{3,2,1,0:T(8,128)S(1)} async-done(((f32[16,3,16,128]{3,2,1,0:T(8,128)}), f32[16,3,16,128]{3,2,1,0:T(8,128)S(1)}, u32[]{:S(2)}, u32[]{:S(2)}) %all-to-all-start) | async-done | bytes 393248 | tf_op jit(solution)/shard_map/all_to_all | solution.py:557
  34.5 2.9 %collective-permute-start.3 = (f32[48,128]{1,0:T(8,128)S(1)}, f32[48,128]{1,0:T(8,128)S(1)}, u32[]{:S(2)}, u32[]{:S(2)}) collective-permute-start(f32[48,128]{1,0:T(8,128)S(1)} %shard_map.177.total_ref), channel_id=1, source_target_pairs={{0,112},{16,32},{32,16},{48,64},{64,48},{80,96},{96,80},{112,0},{1... | collective-permute-start | bytes 73736 | tf_op jit(solution)/shard_map/ppermute | solution.py:500
  37.3 1.4 %shard_map.179 = (f32[128,1024]{1,0:T(8,128)S(1)}, bf16[128,240]{1,0:T(8,128)(2,1)S(1)}) custom-call(f32[64,1024]{1,0:T(8,128)S(1)} %get-tuple-element.26.own_ref.sp_ref, f32[64,1024]{1,0:T(8,128)S(1)} %collective-permute-done.4.first_ref, f32[64,1024]{1,0:T(8,128)S(1)} %collective-permute-done.5.second_ref, f32[3,3,3,7,32]{4,3,2,1,0:T(8,128)S(1)} %bitcast.6, ...), custom_call_target="tpu_custom_call" | custom-call | tf_op jit(solution)/shard_map/pallas_call | solution.py:561
  38.7 0.3 collective-permute-done.3.tb_ref
  39.0 1.2 %shard_map.180 = (f32[5,2,1,1024]{3,2,1,0:T(1,128)S(1)}, f32[16,8,4,128]{3,2,1,0:T(4,128)S(1)}) custom-call(f32[48,128]{1,0:T(8,128)S(1)} %shard_map.177.total_ref, f32[48,128]{1,0:T(8,128)S(1)} %collective-permute-done.2.ta_ref, f32[48,128]{1,0:T(8,128)S(1)} %collective-permute-done.3.tb_ref, f32[64,1024]{1,0:T(8,128)S(1)} %get-tuple-element.26.own_ref.sp_ref, ...), custom_call_target="tpu_custom_call" | custom-call | tf_op jit(solution)/shard_map/pallas_call | solution.py:567
  40.2 12.1 %all_to_all.10.nd_ref = f32[16,8,4,128]{3,2,1,0:T(4,128)S(1)} all-to-all(f32[16,8,4,128]{3,2,1,0:T(4,128)S(1)} %get-tuple-element.31), channel_id=1, replica_groups=mesh['plane'=8,'tile'=16] {'tile'}, dimensions={0} | all-to-all | bytes 524288 | tf_op jit(solution)/shard_map/all_to_all | solution.py:574
  52.3 2.9 %copy-done.1 = bf16[104,256,128]{2,1,0:T(8,128)(2,1)S(1)} copy-done((bf16[104,256,128]{2,1,0:T(8,128)(2,1)S(1)}, bf16[104,256,128]{2,1,0:T(8,128)(2,1)}, u32[]{:S(2)}) %copy-start.1) | copy-done | bytes 6815768
  55.2 2.9 %copy-done.3 = bf16[104,256,128]{2,1,0:T(8,128)(2,1)S(1)} copy-done((bf16[104,256,128]{2,1,0:T(8,128)(2,1)S(1)}, bf16[104,256,128]{2,1,0:T(8,128)(2,1)}, u32[]{:S(2)}) %copy-start.3) | copy-done | bytes 6815768
  58.2 5.3 %back.1 = (f32[64,128]{1,0:T(8,128)S(1)}, f32[16,128]{1,0:T(8,128)S(1)}, f32[16,128]{1,0:T(8,128)S(1)}, f32[5,2,1,1024]{3,2,1,0:T(1,128)}) custom-call(s32[12,1,16]{2,1,0:T(1,128)} %bitcast.11, s32[12,16,16]{2,1,0:T(8,128)} %bitcast.9, s32[1,16]{1,0:T(1,128)} %cnt_hbm.3, f32[16,8,4,128]{3,2,1,0:T(4,128)S(1)} %all_to_all.10.nd_ref, ...), custom_call_target="tpu_custom_call" | custom-call | tf_op jit(solution)/shard_map/back/pallas_call | solution.py:576
  63.4 0.1 collective-permute-start.6
  63.5 2.0 %collective-permute-start.7 = (f32[16,128]{1,0:T(8,128)S(1)}, f32[16,128]{1,0:T(8,128)S(1)}, u32[]{:S(2)}, u32[]{:S(2)}) collective-permute-start(f32[16,128]{1,0:T(8,128)S(1)} %get-tuple-element.37), channel_id=1, source_target_pairs={{0,15},{1,2},{2,1},{3,4},{4,3},{5,6},{6,5},{7,8},{8,7},{9,10},{10,... | collective-permute-start | bytes 24584 | tf_op jit(solution)/shard_map/ppermute | solution.py:500
  65.6 1.8 %shard_map.181 = (f32[256,512]{1,0:T(8,128)S(1)}, bf16[256,240]{1,0:T(8,128)(2,1)S(1)}) custom-call(f32[64,1024]{1,0:T(8,128)S(1)} %get-tuple-element.26.own_ref.sp_ref, f32[64,1024]{1,0:T(8,128)S(1)} %get-tuple-element.38.sm_ref, f32[64,1024]{1,0:T(8,128)S(1)} %collective-permute-done.4.first_ref, f32[64,1024]{1,0:T(8,128)S(1)} %collective-permute-done.5.second_ref, ...), custom_call_target="tpu_custom_call" | custom-call | tf_op jit(solution)/shard_map/pallas_call | solution.py:602
  67.4 3.2 %collective-permute-done.7.second_ref = f32[16,128]{1,0:T(8,128)S(1)} collective-permute-done((f32[16,128]{1,0:T(8,128)S(1)}, f32[16,128]{1,0:T(8,128)S(1)}, u32[]{:S(2)}, u32[]{:S(2)}) %collective-permute-start.7) | collective-permute-done | bytes 8224 | tf_op jit(solution)/shard_map/ppermute | solution.py:500
  70.6 1.7 %shard_map.182 = f32[5,2,4,512]{3,2,1,0:T(4,128)} custom-call(f32[64,128]{1,0:T(8,128)S(1)} %get-tuple-element.35.back_ref, f32[16,128]{1,0:T(8,128)S(1)} %collective-permute-done.6.first_ref, f32[16,128]{1,0:T(8,128)S(1)} %collective-permute-done.7.second_ref, f32[256,512]{1,0:T(8,128)S(1)} %get-tuple-element.39.known_ref, ...), custom_call_target="tpu_custom_call" | custom-call | tf_op jit(solution)/shard_map/pallas_call | solution.py:608
  (34 shorter events, 0.2 us)
Async XLA Ops:
  1.6 19.7 %collective-permute-start = (f32[32,1024]{1,0:T(8,128)S(1)}, f32[32,1024]{1,0:T(8,128)S(1)}, u32[]{:S(2)}, u32[]{:S(2)}) collective-permute-start(f32[32,1024]{1,0:T(8,128)S(1)} %shard_map.176.after_ref.own_ref), channel_id=1, source_target_pairs={{0,1},{1,0},{2,3},{3,2},{4,5},{5,4},{6,7},{7,6},{8,9},{9,8},{10,11... | collective-permute-start | bytes 393224 | tf_op jit(solution)/shard_map/ppermute | solution.py:498
  3.7 17.6 %collective-permute-start.1 = (f32[32,1024]{1,0:T(8,128)S(1)}, f32[32,1024]{1,0:T(8,128)S(1)}, u32[]{:S(2)}, u32[]{:S(2)}) collective-permute-start(f32[32,1024]{1,0:T(8,128)S(1)} %shard_map.176.after_ref.own_ref), channel_id=1, source_target_pairs={{0,15},{1,2},{2,1},{3,4},{4,3},{5,6},{6,5},{7,8},{8,7},{9,10},{10,... | collective-permute-start | bytes 393224 | tf_op jit(solution)/shard_map/ppermute | solution.py:500
  8.7 16.2 %copy-start.4 = (f32[5,2,4,512]{3,2,1,0:T(4,128)S(1)}, f32[5,2,4,512]{3,2,1,0:T(4,128)}, u32[]{:S(2)}) copy-start(f32[5,2,4,512]{3,2,1,0:T(4,128)} %primal_ref.3) | copy-start | bytes 245764
  8.7 28.6 %copy-start.6 = (f32[32,7,3,3,3]{0,1,4,3,2:T(8,128)S(1)}, f32[32,7,3,3,3]{0,1,4,3,2:T(8,128)}, u32[]{:S(2)}) copy-start(f32[32,7,3,3,3]{0,1,4,3,2:T(8,128)} %param.24) | copy-start | bytes 72580
  8.7 28.6 %copy-start.11 = (f32[32]{0:T(128)S(1)}, f32[32]{0:T(128)}, u32[]{:S(2)}) copy-start(f32[32]{0:T(128)} %bias_ref.2) | copy-start | bytes 388
  8.7 30.3 %copy-start.7 = (f32[5,32]{1,0:T(8,128)S(1)}, f32[5,32]{1,0:T(8,128)}, u32[]{:S(2)}) copy-start(f32[5,32]{1,0:T(8,128)} %mix_ref.2) | copy-start | bytes 1924
  8.7 30.3 %copy-start.9 = (f32[32]{0:T(128)S(1)}, f32[32]{0:T(128)}, u32[]{:S(2)}) copy-start(f32[32]{0:T(128)} %slope_ref.2) | copy-start | bytes 388
  8.7 30.3 %copy-start.10 = (f32[5]{0:T(128)S(1)}, f32[5]{0:T(128)}, u32[]{:S(2)}) copy-start(f32[5]{0:T(128)} %shift_ref.2) | copy-start | bytes 64
  15.6 2.8 %copy-start = (bf16[104,256,128]{2,1,0:T(8,128)(2,1)}, bf16[104,256,128]{2,1,0:T(8,128)(2,1)S(1)}, u32[]{:S(2)}) copy-start(bf16[104,256,128]{2,1,0:T(8,128)(2,1)S(1)} %get-tuple-element.32.wh_ref) | copy-start | bytes 20447236
  18.4 2.9 %copy-start.2 = (bf16[104,256,128]{2,1,0:T(8,128)(2,1)}, bf16[104,256,128]{2,1,0:T(8,128)(2,1)S(1)}, u32[]{:S(2)}) copy-start(bf16[104,256,128]{2,1,0:T(8,128)(2,1)S(1)} %get-tuple-element.33.wl_ref) | copy-start | bytes 20447236
  21.3 13.0 %all-to-all-start = ((f32[16,3,16,128]{3,2,1,0:T(8,128)}), f32[16,3,16,128]{3,2,1,0:T(8,128)S(1)}, u32[]{:S(2)}, u32[]{:S(2)}) async-start(f32[16,3,16,128]{3,2,1,0:T(8,128)} %get-tuple-element.23), calls=%async_computation | async-start | bytes 786432 | tf_op jit(solution)/shard_map/all_to_all | solution.py:557
  25.0 12.4 %collective-permute-start.4 = (f32[64,1024]{1,0:T(8,128)S(1)}, f32[64,1024]{1,0:T(8,128)S(1)}, u32[]{:S(2)}, u32[]{:S(2)}) collective-permute-start(f32[64,1024]{1,0:T(8,128)S(1)} %get-tuple-element.27), channel_id=1, source_target_pairs={{0,16},{16,0},{32,48},{48,32},{64,80},{80,64},{96,112},{112,96},{1... | collective-permute-start | bytes 786440 | tf_op jit(solution)/shard_map/ppermute | solution.py:498
  25.1 12.3 %collective-permute-start.5 = (f32[64,1024]{1,0:T(8,128)S(1)}, f32[64,1024]{1,0:T(8,128)S(1)}, u32[]{:S(2)}, u32[]{:S(2)}) collective-permute-start(f32[64,1024]{1,0:T(8,128)S(1)} %get-tuple-element.28), channel_id=1, source_target_pairs={{0,112},{16,32},{32,16},{48,64},{64,48},{80,96},{96,80},{112,0},{1... | collective-permute-start | bytes 786440 | tf_op jit(solution)/shard_map/ppermute | solution.py:500
  34.4 4.4 %collective-permute-start.2 = (f32[48,128]{1,0:T(8,128)S(1)}, f32[48,128]{1,0:T(8,128)S(1)}, u32[]{:S(2)}, u32[]{:S(2)}) collective-permute-start(f32[48,128]{1,0:T(8,128)S(1)} %shard_map.177.total_ref), channel_id=1, source_target_pairs={{0,16},{16,0},{32,48},{48,32},{64,80},{80,64},{96,112},{112,96},{1... | collective-permute-start | bytes 73736 | tf_op jit(solution)/shard_map/ppermute | solution.py:498
  34.5 4.5 %collective-permute-start.3 = (f32[48,128]{1,0:T(8,128)S(1)}, f32[48,128]{1,0:T(8,128)S(1)}, u32[]{:S(2)}, u32[]{:S(2)}) collective-permute-start(f32[48,128]{1,0:T(8,128)S(1)} %shard_map.177.total_ref), channel_id=1, source_target_pairs={{0,112},{16,32},{32,16},{48,64},{64,48},{80,96},{96,80},{112,0},{1... | collective-permute-start | bytes 73736 | tf_op jit(solution)/shard_map/ppermute | solution.py:500
  52.3 2.9 %copy-start.1 = (bf16[104,256,128]{2,1,0:T(8,128)(2,1)S(1)}, bf16[104,256,128]{2,1,0:T(8,128)(2,1)}, u32[]{:S(2)}) copy-start(bf16[104,256,128]{2,1,0:T(8,128)(2,1)} %copy-done) | copy-start | bytes 20447236
  55.2 2.9 %copy-start.3 = (bf16[104,256,128]{2,1,0:T(8,128)(2,1)S(1)}, bf16[104,256,128]{2,1,0:T(8,128)(2,1)}, u32[]{:S(2)}) copy-start(bf16[104,256,128]{2,1,0:T(8,128)(2,1)} %copy-done.2) | copy-start | bytes 20447236
  58.1 7.4 %copy-start.5 = (f32[32,6,3,3,3]{0,4,3,2,1:T(4,128)S(1)}, f32[32,6,3,3,3]{0,4,3,2,1:T(4,128)}, u32[]{:S(2)}) copy-start(f32[32,6,3,3,3]{0,4,3,2,1:T(4,128)} %param.29) | copy-start | bytes 62212
  58.1 7.4 %copy-start.12 = (f32[32]{0:T(128)S(1)}, f32[32]{0:T(128)}, u32[]{:S(2)}) copy-start(f32[32]{0:T(128)} %bias_ref.3) | copy-start | bytes 388
  58.1 12.4 %copy-start.8 = (f32[5,32]{1,0:T(8,128)S(1)}, f32[5,32]{1,0:T(8,128)}, u32[]{:S(2)}) copy-start(f32[5,32]{1,0:T(8,128)} %mix_ref.3) | copy-start | bytes 1924
  58.1 12.4 %copy-start.13 = (f32[32]{0:T(128)S(1)}, f32[32]{0:T(128)}, u32[]{:S(2)}) copy-start(f32[32]{0:T(128)} %slope_ref.3) | copy-start | bytes 388
  58.2 12.4 %copy-start.14 = (f32[5]{0:T(128)S(1)}, f32[5]{0:T(128)}, u32[]{:S(2)}) copy-start(f32[5]{0:T(128)} %shift_ref.3) | copy-start | bytes 64
  63.4 3.9 %collective-permute-start.6 = (f32[16,128]{1,0:T(8,128)S(1)}, f32[16,128]{1,0:T(8,128)S(1)}, u32[]{:S(2)}, u32[]{:S(2)}) collective-permute-start(f32[16,128]{1,0:T(8,128)S(1)} %get-tuple-element.36), channel_id=1, source_target_pairs={{0,1},{1,0},{2,3},{3,2},{4,5},{5,4},{6,7},{7,6},{8,9},{9,8},{10,11... | collective-permute-start | bytes 24584 | tf_op jit(solution)/shard_map/ppermute | solution.py:498
  63.5 7.1 %collective-permute-start.7 = (f32[16,128]{1,0:T(8,128)S(1)}, f32[16,128]{1,0:T(8,128)S(1)}, u32[]{:S(2)}, u32[]{:S(2)}) collective-permute-start(f32[16,128]{1,0:T(8,128)S(1)} %get-tuple-element.37), channel_id=1, source_target_pairs={{0,15},{1,2},{2,1},{3,4},{4,3},{5,6},{6,5},{7,8},{8,7},{9,10},{10,... | collective-permute-start | bytes 24584 | tf_op jit(solution)/shard_map/ppermute | solution.py:500

commit v8 on v7

--- a/solution.py
+++ b/solution.py
@@ -399,17 +399,37 @@
     out_copy.wait()
 
 
-def primal_known_kernel(
-    sp_ref, sm_ref, first_ref, second_ref, kern_ref, bias_ref, known_ref, last_ref,
-    tt_ref, lt_ref, x_ref,
+def finish(g, mix, slope, shift):
+    g = jnp.where(g > 0, g, slope * g)
+    return dot3(mix, g) + shift
+
+
+def primal_inner_kernel(
+    sp_ref, sm_ref, first_ref, second_ref, back_ref, primal_ref, kern_ref, mix_ref,
+    bias_ref, slope_ref, shift_ref, part_ref, rim_ref, out_hbm,
+    tt_ref, lt_ref, lr_ref, x_ref, y_ref, out_ref, sem,
 ):
+    p = lax.axis_index("plane")
+    keeps = (p > 0, None, None, p < 7)
     before, after = plane_sides(first_ref, second_ref, slice(48, 64))
     for plane, v in enumerate((before, sm_ref[48:64, :], sp_ref[48:64, :], after)):
         for half in range(2):
             i = plane * 32 + half * 16
             x_ref[i : i + 16, :] = v[:, half * 512 : (half + 1) * 512]
+    y_ref[...] = jnp.zeros((80, 512), F32)
+    for plane in range(4):
+        for row in range(1, 5):
+            for col in range(4):
+                i = (row * 4 - 4 + col) * 4 + plane
+                v = back_ref[i : i + 1, :]
+                if keeps[plane] is not None:
+                    v = jnp.where(keeps[plane], v, 0.0)
+                i = 24 + plane * 6 + row
+                y_ref[i : i + 1, col * 128 : (col + 1) * 128] = v
+    spread_columns(y_ref, 512)
     tt_ref[...] = jnp.zeros((96, 384), F32)
     lt_ref[...] = jnp.zeros((80, 256), F32)
+    lr_ref[...] = jnp.zeros((32, 128), F32)
     for dz in range(3):
         for dr in range(3):
             block = jnp.concatenate(
@@ -429,21 +449,38 @@
                         i = db * 24 + (z + dz) * 6 + r + dr
                         lane = z * 128 + r * 32
                         lt_ref[i : i + 1, lane : lane + 32] = four[:, r * 32 : (r + 1) * 32]
-    last_ref[...] = joined(lt_ref[...].T)
+                    if dr != 1:
+                        i = db * 8 + (z + dz) * 2 + dr // 2
+                        k = z * 2 + dr // 2
+                        lr_ref[i : i + 1, k * 32 : (k + 1) * 32] = four[:, k * 32 : (k + 1) * 32]
+    rim_ref[...] = joined(lr_ref[...].T)
     tt = joined(tt_ref[...].T)
-    bias = column(bias_ref, 32)
+    bias, slope, shift = column(bias_ref, 32), column(slope_ref, 32), column(shift_ref, 5)
+    mix = joined(jnp.concatenate([mix_ref[...], jnp.zeros((3, 32), F32)], 0))
+    own = dot3(joined(lt_ref[...].T), y_ref[...])
     for z in range(2):
         h = dot3(tt, x_ref[z * 32 : z * 32 + 96])
         for r in range(4):
             g = shifted_sum([h[r * 96 + i * 32 : r * 96 + (i + 1) * 32] for i in range(3)]) + bias
             i = (z * 4 + r) * 32
-            known_ref[i : i + 32, :] = g
-
-
-def primal_kernel_body(
-    back_ref, first_ref, second_ref, known_ref, last_ref, primal_ref,
-    mix_ref, slope_ref, shift_ref, new_ref, y_ref,
+            g = g + own[i : i + 32]
+            if r in (0, 3):
+                i = (z * 2 + r // 3) * 32
+                part_ref[i : i + 32, :] = g
+            else:
+                out = finish(g, mix, slope, shift)
+                for c in range(5):
+                    out_ref[c, z, r - 1 : r, :] = out[c : c + 1] + primal_ref[c, z, r : r + 1, :]
+    copy = pltpu.make_async_copy(out_ref, out_hbm.at[:, :, 1:3, :], sem)
+    copy.start()
+    copy.wait()
+
+
+def primal_outer_kernel(
+    first_ref, second_ref, part_ref, rim_ref, primal_ref, mix_ref, slope_ref, shift_ref,
+    inner_hbm, out_hbm, y_ref, out_ref, sem,
 ):
+    del inner_hbm
     p = lax.axis_index("plane")
     t = lax.axis_index("tile")
     keeps = (p > 0, None, None, p < 7)
@@ -451,35 +488,38 @@
     first, second = first_ref[...], second_ref[...]
     above = jnp.where(t > 0, jnp.where(even, second, first), 0.0)
     below = jnp.where(t < 15, jnp.where(even, first, second), 0.0)
-    y_ref[...] = jnp.zeros((80, 512), F32)
     for plane in range(4):
-        for row in range(6):
+        for rim, src in enumerate((above, below)):
             for col in range(4):
-                if row == 0:
-                    i = col * 4 + plane
-                    v = above[i : i + 1]
-                elif row == 5:
-                    i = col * 4 + plane
-                    v = below[i : i + 1]
-                else:
-                    i = (row * 4 - 4 + col) * 4 + plane
-                    v = back_ref[i : i + 1, :]
+                i = col * 4 + plane
+                v = src[i : i + 1]
                 if keeps[plane] is not None:
                     v = jnp.where(keeps[plane], v, 0.0)
-                i = 24 + plane * 6 + row
+                i = 8 + plane * 2 + rim
                 y_ref[i : i + 1, col * 128 : (col + 1) * 128] = v
-    spread_columns(y_ref, 512)
+    mid = y_ref[8:16, :]
+    lane = lax.broadcasted_iota(jnp.int32, mid.shape, 1)
+    y_ref[0:8, :] = jnp.where(lane == 0, 0.0, pltpu.roll(mid, 1, 1))
+    y_ref[16:24, :] = jnp.where(lane == 511, 0.0, pltpu.roll(mid, 511, 1))
+    y_ref[24:32, :] = jnp.zeros((8, 512), F32)
     slope, shift = column(slope_ref, 32), column(shift_ref, 5)
     mix = joined(jnp.concatenate([mix_ref[...], jnp.zeros((3, 32), F32)], 0))
-    h = dot3(last_ref[...], y_ref[...]) + known_ref[...]
-    for z in range(2):
-        for r in range(4):
-            i = (z * 4 + r) * 32
-            g = h[i : i + 32]
-            g = jnp.where(g > 0, g, slope * g)
-            out = dot3(mix, g) + shift
+    h = dot3(rim_ref[...], y_ref[...]) + part_ref[...]
+    copies = []
+    for rim, row in enumerate((0, 3)):
+        for z in range(2):
+            i = (z * 2 + rim) * 32
+            out = finish(h[i : i + 32], mix, slope, shift)
             for c in range(5):
-                new_ref[c, z, r : r + 1, :] = out[c : c + 1, :] + primal_ref[c, z, r : r + 1, :]
+                out_ref[rim, c, z] = out[c : c + 1] + primal_ref[c, z, row : row + 1, :]
+        copies.append(
+            pltpu.make_async_copy(
+                out_ref.at[rim], out_hbm.at[:, :, row : row + 1, :], sem.at[rim]
+            )
+        )
+        copies[-1].start()
+    for copy in copies:
+        copy.wait()
 
 
 def call(body, outs, in_specs, scratch=(), limit=8 << 20):
@@ -599,18 +639,47 @@
     )
     edges = swaps(edge_a, edge_b, "tile")
 
-    known, last = call(
-        primal_known_kernel, [((256, 512), F32), ((256, 240), BF16)],
-        [VMEM] * 5 + [SMEM],
-        [pltpu.VMEM((96, 384), F32), pltpu.VMEM((80, 256), F32), pltpu.VMEM((128, 512), F32)],
-    )(sp, sm, *sides, jnp.transpose(primal_kernel, (1, 2, 3, 4, 0)), primal_bias)
-
-    new_primal = call(
-        primal_kernel_body, [((5, 2, 4, 512), F32)], [VMEM] * 7 + [SMEM] * 2,
-        [pltpu.VMEM((80, 512), F32)],
+    part, rim, inner = pl.pallas_call(
+        primal_inner_kernel,
+        name="primal_inner",
+        out_shape=(
+            jax.ShapeDtypeStruct((128, 512), F32),
+            jax.ShapeDtypeStruct((128, 96), BF16),
+            jax.ShapeDtypeStruct((5, 2, 4, 512), F32),
+        ),
+        in_specs=[VMEM] * 8 + [SMEM] * 3,
+        out_specs=(VMEM, VMEM, HBM),
+        scratch_shapes=[
+            pltpu.VMEM((96, 384), F32),
+            pltpu.VMEM((80, 256), F32),
+            pltpu.VMEM((32, 128), F32),
+            pltpu.VMEM((128, 512), F32),
+            pltpu.VMEM((80, 512), F32),
+            pltpu.VMEM((5, 2, 2, 512), F32),
+            pltpu.SemaphoreType.DMA,
+        ],
+        compiler_params=pltpu.CompilerParams(vmem_limit_bytes=8 << 20),
     )(
-        back, *edges, known, last, primal, primal_mixing, primal_slope, primal_shift,
-    )[0]
+        sp, sm, *sides, back, primal, jnp.transpose(primal_kernel, (1, 2, 3, 4, 0)),
+        primal_mixing, primal_bias, primal_slope, primal_shift,
+    )
+
+    new_primal = pl.pallas_call(
+        primal_outer_kernel,
+        name="primal_outer",
+        out_shape=jax.ShapeDtypeStruct((5, 2, 4, 512), F32),
+        in_specs=[VMEM] * 6 + [SMEM] * 2 + [HBM],
+        out_specs=HBM,
+        scratch_shapes=[
+            pltpu.VMEM((32, 512), F32),
+            pltpu.VMEM((2, 5, 2, 1, 512), F32),
+            pltpu.SemaphoreType.DMA((2,)),
+        ],
+        input_output_aliases={8: 0},
+        compiler_params=pltpu.CompilerParams(vmem_limit_bytes=8 << 20),
+    )(
+        *edges, part, rim, primal, primal_mixing, primal_slope, primal_shift, hbm(inner),
+    )
     return new_primal, new_dual
 
 

time: 72.7 us -> 72.3 us (level)
  starting transfers between devices: 18.6 us -> 17 us
  Pallas kernels: 19.3 us -> 20.4 us
    pallas_call x2, Pallas kernels: 3.49 us -> 4.6 us  [the longest x1 3 us: per_device(): pl.pallas_call(primal_inner_kernel, name='primal_inner', out_shape=(jax.S...]
    ppermute x4, starting transfers between devices: 2.36 us -> 1.48 us  [swaps(): a = lax.ppermute(first, axis, [(i, i ^ 1) for i in range(count)])]
    ppermute x4, starting transfers between devices: 12.7 us -> 12 us  [swaps(): b = lax.ppermute(second, axis, pairs)]
  transfers between devices with their start and end apart: 9 -> 9, of which waited for: 3 -> 3; matrix products, arithmetic and copies ran while one was open for 0% -> 0% of each run, Pallas kernels for 14% -> 16%
where the time goes in v8:
time: 72.3 us; the launch traced here: 71.9 us
  Pallas kernels  20.4 us (28%)
  starting transfers between devices  17 us (24%)
  blocking collectives  12 us (17%)
  local copies, waits for them, and re-layouts  11.6 us (16%)
  waiting for transfers between devices  10.1 us (14%)
  between operations  0.81 us (1%)
    all_to_all x1, blocking collectives, per_device(): leading = lax.all_to_all(send, 'tile', 0, 0, tiled=True)  12 us
    ppermute x4, starting transfers between devices, swaps(): b = lax.ppermute(second, axis, pairs)  12 us
    unnamed x30, local copies, waits for them, and re-layouts  11.6 us
    pallas_call x1, Pallas kernels, per_device(): pl.pallas_call(project_kernel, name='project', out_shape=(jax.ShapeDtypeS...  6.85 us
    all_to_all x1, waiting for transfers between devices, per_device(): got = lax.all_to_all(terms, 'tile', 0, 0, tiled=True)  6.71 us
    pallas_call x1, Pallas kernels, per_device(): pl.pallas_call(back_kernel, name='back', out_shape=(jax.ShapeDtypeStruct(...  5.27 us
    all_to_all x1, starting transfers between devices, per_device(): got = lax.all_to_all(terms, 'tile', 0, 0, tiled=True)  3.55 us
    ppermute x4, waiting for transfers between devices, swaps(): b = lax.ppermute(second, axis, pairs)  3.39 us
  transfers between devices with their start and end apart: 9, of which 3 were waited for; matrix products, arithmetic and copies ran while one was open for 0% of the time, Pallas kernels for 16%

profile of v8, /device:TPU:0, one launch (start us, length us, event | category | flops | bytes accessed | tf_op | source)
XLA Modules:
  0.0 71.9 jit_solution(3109411064859875803)
XLA Ops:
  0.6 1.0 %shard_map.176.after_ref.own_ref = f32[32,1024]{1,0:T(8,128)S(1)} custom-call(f32[5,2,1,1024]{3,2,1,0:T(1,128)} %dual_hbm.1, f32[2,1,1024]{2,1,0:T(1,128)} %measured_hbm.1, f32[5,2,4,512]{3,2,1,0:T(4,128)} %primal_ref.5), custom_call_target="tpu_custom_call" | custom-call | tf_op jit(solution)/shard_map/pallas_call | solution.py:553
  1.6 6.7 %collective-permute-start.1 = (f32[32,1024]{1,0:T(8,128)S(1)}, f32[32,1024]{1,0:T(8,128)S(1)}, u32[]{:S(2)}, u32[]{:S(2)}) collective-permute-start(f32[32,1024]{1,0:T(8,128)S(1)} %shard_map.176.after_ref.own_ref), channel_id=1, source_target_pairs={{0,15},{1,2},{2,1},{3,4},{4,3},{5,6},{6,5},{7,8},{8,7},{9,10},{10,... | collective-permute-start | bytes 393224 | tf_op jit(solution)/shard_map/ppermute | solution.py:540
  8.3 6.9 %project.1 = (f32[16,3,16,128]{3,2,1,0:T(8,128)}, bf16[104,256,128]{2,1,0:T(8,128)(2,1)S(1)}, bf16[104,256,128]{2,1,0:T(8,128)(2,1)S(1)}) custom-call(s32[12,1,16]{2,1,0:T(1,128)} %bitcast.10, s32[12,16,16]{2,1,0:T(8,128)} %bitcast.8, s32[1,16]{1,0:T(1,128)} %cnt_hbm.3, f32[5,2,4,512]{3,2,1,0:T(4,128)} %primal_ref.5, f32[16,6,256,128]{3,2,1,0:T(8,128)} %bitcast.7, ...), custom_call_target="tpu_custom_call" | custom-call | flops 2147483648 | bytes 26214400 | tf_op jit(solution)/shard_map/project/pallas_call | solution.py:566
  15.2 2.8 %copy-done = bf16[104,256,128]{2,1,0:T(8,128)(2,1)} copy-done((bf16[104,256,128]{2,1,0:T(8,128)(2,1)}, bf16[104,256,128]{2,1,0:T(8,128)(2,1)S(1)}, u32[]{:S(2)}) %copy-start) | copy-done | bytes 6815768
  18.0 2.9 %copy-done.2 = bf16[104,256,128]{2,1,0:T(8,128)(2,1)} copy-done((bf16[104,256,128]{2,1,0:T(8,128)(2,1)}, bf16[104,256,128]{2,1,0:T(8,128)(2,1)S(1)}, u32[]{:S(2)}) %copy-start.2) | copy-done | bytes 6815768
  20.9 3.6 %all-to-all-start = ((f32[16,3,16,128]{3,2,1,0:T(8,128)}), f32[16,3,16,128]{3,2,1,0:T(8,128)S(1)}, u32[]{:S(2)}, u32[]{:S(2)}) async-start(f32[16,3,16,128]{3,2,1,0:T(8,128)} %get-tuple-element.24), calls=%async_computation | async-start | bytes 786432 | tf_op jit(solution)/shard_map/all_to_all | solution.py:597
  24.5 0.1 shard_map.178
  24.6 0.1 collective-permute-start.4
  24.7 2.9 %collective-permute-start.5 = (f32[64,1024]{1,0:T(8,128)S(1)}, f32[64,1024]{1,0:T(8,128)S(1)}, u32[]{:S(2)}, u32[]{:S(2)}) collective-permute-start(f32[64,1024]{1,0:T(8,128)S(1)} %get-tuple-element.29), channel_id=1, source_target_pairs={{0,112},{16,32},{32,16},{48,64},{64,48},{80,96},{96,80},{112,0},{1... | collective-permute-start | bytes 786440 | tf_op jit(solution)/shard_map/ppermute | solution.py:540
  27.5 6.7 %all-to-all-done.got_ref = f32[16,3,16,128]{3,2,1,0:T(8,128)S(1)} async-done(((f32[16,3,16,128]{3,2,1,0:T(8,128)}), f32[16,3,16,128]{3,2,1,0:T(8,128)S(1)}, u32[]{:S(2)}, u32[]{:S(2)}) %all-to-all-start) | async-done | bytes 393248 | tf_op jit(solution)/shard_map/all_to_all | solution.py:597
  34.3 0.4 collective-permute-start.3
  34.7 1.3 %collective-permute-start.2 = (f32[48,128]{1,0:T(8,128)S(1)}, f32[48,128]{1,0:T(8,128)S(1)}, u32[]{:S(2)}, u32[]{:S(2)}) collective-permute-start(f32[48,128]{1,0:T(8,128)S(1)} %shard_map.177.total_ref), channel_id=1, source_target_pairs={{0,16},{16,0},{32,48},{48,32},{64,80},{80,64},{96,112},{112,96},{1... | collective-permute-start | bytes 73736 | tf_op jit(solution)/shard_map/ppermute | solution.py:538
  36.0 1.4 %shard_map.179 = (f32[128,1024]{1,0:T(8,128)S(1)}, bf16[128,240]{1,0:T(8,128)(2,1)S(1)}) custom-call(f32[64,1024]{1,0:T(8,128)S(1)} %get-tuple-element.27.own_ref.sp_ref, f32[64,1024]{1,0:T(8,128)S(1)} %collective-permute-done.4.first_ref, f32[64,1024]{1,0:T(8,128)S(1)} %collective-permute-done.5.second_ref, f32[3,3,3,7,32]{4,3,2,1,0:T(8,128)S(1)} %bitcast.5, ...), custom_call_target="tpu_custom_call" | custom-call | tf_op jit(solution)/shard_map/pallas_call | solution.py:601
  37.3 1.5 %collective-permute-done.3.tb_ref = f32[48,128]{1,0:T(8,128)S(1)} collective-permute-done((f32[48,128]{1,0:T(8,128)S(1)}, f32[48,128]{1,0:T(8,128)S(1)}, u32[]{:S(2)}, u32[]{:S(2)}) %collective-permute-start.3) | collective-permute-done | bytes 24608 | tf_op jit(solution)/shard_map/ppermute | solution.py:540
  38.8 1.2 %shard_map.180 = (f32[5,2,1,1024]{3,2,1,0:T(1,128)S(1)}, f32[16,8,4,128]{3,2,1,0:T(4,128)S(1)}) custom-call(f32[48,128]{1,0:T(8,128)S(1)} %shard_map.177.total_ref, f32[48,128]{1,0:T(8,128)S(1)} %collective-permute-done.2.ta_ref, f32[48,128]{1,0:T(8,128)S(1)} %collective-permute-done.3.tb_ref, f32[64,1024]{1,0:T(8,128)S(1)} %get-tuple-element.27.own_ref.sp_ref, ...), custom_call_target="tpu_custom_call" | custom-call | tf_op jit(solution)/shard_map/pallas_call | solution.py:607
  40.0 12.0 %all_to_all.10.nd_ref = f32[16,8,4,128]{3,2,1,0:T(4,128)S(1)} all-to-all(f32[16,8,4,128]{3,2,1,0:T(4,128)S(1)} %get-tuple-element.32), channel_id=1, replica_groups=mesh['plane'=8,'tile'=16] {'tile'}, dimensions={0} | all-to-all | bytes 524288 | tf_op jit(solution)/shard_map/all_to_all | solution.py:614
  52.0 2.9 %copy-done.1 = bf16[104,256,128]{2,1,0:T(8,128)(2,1)S(1)} copy-done((bf16[104,256,128]{2,1,0:T(8,128)(2,1)S(1)}, bf16[104,256,128]{2,1,0:T(8,128)(2,1)}, u32[]{:S(2)}) %copy-start.1) | copy-done | bytes 6815768
  55.0 2.9 %copy-done.3 = bf16[104,256,128]{2,1,0:T(8,128)(2,1)S(1)} copy-done((bf16[104,256,128]{2,1,0:T(8,128)(2,1)S(1)}, bf16[104,256,128]{2,1,0:T(8,128)(2,1)}, u32[]{:S(2)}) %copy-start.3) | copy-done | bytes 6815768
  57.9 5.3 %back.1 = (f32[64,128]{1,0:T(8,128)S(1)}, f32[16,128]{1,0:T(8,128)S(1)}, f32[16,128]{1,0:T(8,128)S(1)}, f32[5,2,1,1024]{3,2,1,0:T(1,128)}) custom-call(s32[12,1,16]{2,1,0:T(1,128)} %bitcast.11, s32[12,16,16]{2,1,0:T(8,128)} %bitcast.9, s32[1,16]{1,0:T(1,128)} %cnt_hbm.3, f32[16,8,4,128]{3,2,1,0:T(4,128)S(1)} %all_to_all.10.nd_ref, ...), custom_call_target="tpu_custom_call" | custom-call | tf_op jit(solution)/shard_map/back/pallas_call | solution.py:616
  63.2 0.1 collective-permute-start.6
  63.3 2.1 %collective-permute-start.7 = (f32[16,128]{1,0:T(8,128)S(1)}, f32[16,128]{1,0:T(8,128)S(1)}, u32[]{:S(2)}, u32[]{:S(2)}) collective-permute-start(f32[16,128]{1,0:T(8,128)S(1)} %get-tuple-element.37), channel_id=1, source_target_pairs={{0,15},{1,2},{2,1},{3,4},{4,3},{5,6},{6,5},{7,8},{8,7},{9,10},{10,... | collective-permute-start | bytes 24584 | tf_op jit(solution)/shard_map/ppermute | solution.py:540
  65.4 3.0 %primal_inner.1 = (f32[128,512]{1,0:T(8,128)S(1)}, bf16[128,96]{1,0:T(8,128)(2,1)S(1)}, f32[5,2,4,512]{3,2,1,0:T(4,128)}) custom-call(f32[64,1024]{1,0:T(8,128)S(1)} %get-tuple-element.27.own_ref.sp_ref, f32[64,1024]{1,0:T(8,128)S(1)} %get-tuple-element.38.sm_ref, f32[64,1024]{1,0:T(8,128)S(1)} %collective-permute-done.4.first_ref, ...), custom_call_target="tpu_custom_call" | custom-call | tf_op jit(solution)/shard_map/primal_inner/pallas_call | solution.py:642
  68.4 1.9 %collective-permute-done.7.second_ref = f32[16,128]{1,0:T(8,128)S(1)} collective-permute-done((f32[16,128]{1,0:T(8,128)S(1)}, f32[16,128]{1,0:T(8,128)S(1)}, u32[]{:S(2)}, u32[]{:S(2)}) %collective-permute-start.7) | collective-permute-done | bytes 8224 | tf_op jit(solution)/shard_map/ppermute | solution.py:540
  70.3 1.6 %primal_outer.1 = f32[5,2,4,512]{3,2,1,0:T(4,128)} custom-call(f32[16,128]{1,0:T(8,128)S(1)} %collective-permute-done.6.first_ref, f32[16,128]{1,0:T(8,128)S(1)} %collective-permute-done.7.second_ref, f32[128,512]{1,0:T(8,128)S(1)} %get-tuple-element.40.part_ref, bf16[128,96]{1,0:T(8,128)(2,1)S(1)} %get-tuple-element.41.rim_ref, ...), custom_call_target="tpu_custom_call", output_to_operand_aliasing={{}: (8, {})} | custom-call | tf_op jit(solution)/shard_map/primal_outer/pallas_call | solution.py:667
  (34 shorter events, 0.1 us)
Async XLA Ops:
  1.6 19.3 %collective-permute-start.1 = (f32[32,1024]{1,0:T(8,128)S(1)}, f32[32,1024]{1,0:T(8,128)S(1)}, u32[]{:S(2)}, u32[]{:S(2)}) collective-permute-start(f32[32,1024]{1,0:T(8,128)S(1)} %shard_map.176.after_ref.own_ref), channel_id=1, source_target_pairs={{0,15},{1,2},{2,1},{3,4},{4,3},{5,6},{6,5},{7,8},{8,7},{9,10},{10,... | collective-permute-start | bytes 393224 | tf_op jit(solution)/shard_map/ppermute | solution.py:540
  8.3 12.6 %collective-permute-start = (f32[32,1024]{1,0:T(8,128)S(1)}, f32[32,1024]{1,0:T(8,128)S(1)}, u32[]{:S(2)}, u32[]{:S(2)}) collective-permute-start(f32[32,1024]{1,0:T(8,128)S(1)} %shard_map.176.after_ref.own_ref), channel_id=1, source_target_pairs={{0,1},{1,0},{2,3},{3,2},{4,5},{5,4},{6,7},{7,6},{8,9},{9,8},{10,11... | collective-permute-start | bytes 393224 | tf_op jit(solution)/shard_map/ppermute | solution.py:538
  8.3 16.2 %copy-start.4 = (f32[5,2,4,512]{3,2,1,0:T(4,128)S(1)}, f32[5,2,4,512]{3,2,1,0:T(4,128)}, u32[]{:S(2)}) copy-start(f32[5,2,4,512]{3,2,1,0:T(4,128)} %primal_ref.5) | copy-start | bytes 245764
  8.3 27.6 %copy-start.5 = (f32[32,7,3,3,3]{0,1,4,3,2:T(8,128)S(1)}, f32[32,7,3,3,3]{0,1,4,3,2:T(8,128)}, u32[]{:S(2)}) copy-start(f32[32,7,3,3,3]{0,1,4,3,2:T(8,128)} %param.24) | copy-start | bytes 72580
  8.3 27.7 %copy-start.13 = (f32[32]{0:T(128)S(1)}, f32[32]{0:T(128)}, u32[]{:S(2)}) copy-start(f32[32]{0:T(128)} %bias_ref.2) | copy-start | bytes 388
  8.3 30.5 %copy-start.8 = (f32[5,32]{1,0:T(8,128)S(1)}, f32[5,32]{1,0:T(8,128)}, u32[]{:S(2)}) copy-start(f32[5,32]{1,0:T(8,128)} %mix_ref.3) | copy-start | bytes 1924
  8.3 30.5 %copy-start.11 = (f32[32]{0:T(128)S(1)}, f32[32]{0:T(128)}, u32[]{:S(2)}) copy-start(f32[32]{0:T(128)} %slope_ref.3) | copy-start | bytes 388
  8.3 30.5 %copy-start.12 = (f32[5]{0:T(128)S(1)}, f32[5]{0:T(128)}, u32[]{:S(2)}) copy-start(f32[5]{0:T(128)} %shift_ref.3) | copy-start | bytes 64
  15.2 2.8 %copy-start = (bf16[104,256,128]{2,1,0:T(8,128)(2,1)}, bf16[104,256,128]{2,1,0:T(8,128)(2,1)S(1)}, u32[]{:S(2)}) copy-start(bf16[104,256,128]{2,1,0:T(8,128)(2,1)S(1)} %get-tuple-element.33.wh_ref) | copy-start | bytes 20447236
  18.0 2.9 %copy-start.2 = (bf16[104,256,128]{2,1,0:T(8,128)(2,1)}, bf16[104,256,128]{2,1,0:T(8,128)(2,1)S(1)}, u32[]{:S(2)}) copy-start(bf16[104,256,128]{2,1,0:T(8,128)(2,1)S(1)} %get-tuple-element.34.wl_ref) | copy-start | bytes 20447236
  20.9 13.3 %all-to-all-start = ((f32[16,3,16,128]{3,2,1,0:T(8,128)}), f32[16,3,16,128]{3,2,1,0:T(8,128)S(1)}, u32[]{:S(2)}, u32[]{:S(2)}) async-start(f32[16,3,16,128]{3,2,1,0:T(8,128)} %get-tuple-element.24), calls=%async_computation | async-start | bytes 786432 | tf_op jit(solution)/shard_map/all_to_all | solution.py:597
  24.6 11.4 %collective-permute-start.4 = (f32[64,1024]{1,0:T(8,128)S(1)}, f32[64,1024]{1,0:T(8,128)S(1)}, u32[]{:S(2)}, u32[]{:S(2)}) collective-permute-start(f32[64,1024]{1,0:T(8,128)S(1)} %get-tuple-element.28), channel_id=1, source_target_pairs={{0,16},{16,0},{32,48},{48,32},{64,80},{80,64},{96,112},{112,96},{1... | collective-permute-start | bytes 786440 | tf_op jit(solution)/shard_map/ppermute | solution.py:538
  24.7 11.3 %collective-permute-start.5 = (f32[64,1024]{1,0:T(8,128)S(1)}, f32[64,1024]{1,0:T(8,128)S(1)}, u32[]{:S(2)}, u32[]{:S(2)}) collective-permute-start(f32[64,1024]{1,0:T(8,128)S(1)} %get-tuple-element.29), channel_id=1, source_target_pairs={{0,112},{16,32},{32,16},{48,64},{64,48},{80,96},{96,80},{112,0},{1... | collective-permute-start | bytes 786440 | tf_op jit(solution)/shard_map/ppermute | solution.py:540
  34.3 4.5 %collective-permute-start.3 = (f32[48,128]{1,0:T(8,128)S(1)}, f32[48,128]{1,0:T(8,128)S(1)}, u32[]{:S(2)}, u32[]{:S(2)}) collective-permute-start(f32[48,128]{1,0:T(8,128)S(1)} %shard_map.177.total_ref), channel_id=1, source_target_pairs={{0,112},{16,32},{32,16},{48,64},{64,48},{80,96},{96,80},{112,0},{1... | collective-permute-start | bytes 73736 | tf_op jit(solution)/shard_map/ppermute | solution.py:540
  34.7 4.1 %collective-permute-start.2 = (f32[48,128]{1,0:T(8,128)S(1)}, f32[48,128]{1,0:T(8,128)S(1)}, u32[]{:S(2)}, u32[]{:S(2)}) collective-permute-start(f32[48,128]{1,0:T(8,128)S(1)} %shard_map.177.total_ref), channel_id=1, source_target_pairs={{0,16},{16,0},{32,48},{48,32},{64,80},{80,64},{96,112},{112,96},{1... | collective-permute-start | bytes 73736 | tf_op jit(solution)/shard_map/ppermute | solution.py:538
  52.0 2.9 %copy-start.1 = (bf16[104,256,128]{2,1,0:T(8,128)(2,1)S(1)}, bf16[104,256,128]{2,1,0:T(8,128)(2,1)}, u32[]{:S(2)}) copy-start(bf16[104,256,128]{2,1,0:T(8,128)(2,1)} %copy-done) | copy-start | bytes 20447236
  55.0 2.9 %copy-start.3 = (bf16[104,256,128]{2,1,0:T(8,128)(2,1)S(1)}, bf16[104,256,128]{2,1,0:T(8,128)(2,1)}, u32[]{:S(2)}) copy-start(bf16[104,256,128]{2,1,0:T(8,128)(2,1)} %copy-done.2) | copy-start | bytes 20447236
  57.9 7.5 %copy-start.6 = (f32[32,6,3,3,3]{0,4,3,2,1:T(4,128)S(1)}, f32[32,6,3,3,3]{0,4,3,2,1:T(4,128)}, u32[]{:S(2)}) copy-start(f32[32,6,3,3,3]{0,4,3,2,1:T(4,128)} %param.29) | copy-start | bytes 62212
  57.9 7.5 %copy-start.7 = (f32[5,32]{1,0:T(8,128)S(1)}, f32[5,32]{1,0:T(8,128)}, u32[]{:S(2)}) copy-start(f32[5,32]{1,0:T(8,128)} %mix_ref.5) | copy-start | bytes 1924
  57.9 7.5 %copy-start.9 = (f32[32]{0:T(128)S(1)}, f32[32]{0:T(128)}, u32[]{:S(2)}) copy-start(f32[32]{0:T(128)} %slope_ref.5) | copy-start | bytes 388
  57.9 7.5 %copy-start.10 = (f32[5]{0:T(128)S(1)}, f32[5]{0:T(128)}, u32[]{:S(2)}) copy-start(f32[5]{0:T(128)} %shift_ref.5) | copy-start | bytes 64
  57.9 7.5 %copy-start.14 = (f32[32]{0:T(128)S(1)}, f32[32]{0:T(128)}, u32[]{:S(2)}) copy-start(f32[32]{0:T(128)} %bias_ref.3) | copy-start | bytes 388
  63.2 5.2 %collective-permute-start.6 = (f32[16,128]{1,0:T(8,128)S(1)}, f32[16,128]{1,0:T(8,128)S(1)}, u32[]{:S(2)}, u32[]{:S(2)}) collective-permute-start(f32[16,128]{1,0:T(8,128)S(1)} %get-tuple-element.36), channel_id=1, source_target_pairs={{0,1},{1,0},{2,3},{3,2},{4,5},{5,4},{6,7},{7,6},{8,9},{9,8},{10,11... | collective-permute-start | bytes 24584 | tf_op jit(solution)/shard_map/ppermute | solution.py:538
  63.3 7.0 %collective-permute-start.7 = (f32[16,128]{1,0:T(8,128)S(1)}, f32[16,128]{1,0:T(8,128)S(1)}, u32[]{:S(2)}, u32[]{:S(2)}) collective-permute-start(f32[16,128]{1,0:T(8,128)S(1)} %get-tuple-element.37), channel_id=1, source_target_pairs={{0,15},{1,2},{2,1},{3,4},{4,3},{5,6},{6,5},{7,8},{8,7},{9,10},{10,... | collective-permute-start | bytes 24584 | tf_op jit(solution)/shard_map/ppermute | solution.py:540

commit v9 on v8

--- a/solution.py
+++ b/solution.py
@@ -38,7 +38,13 @@
     out = jnp.zeros((rows, 128), F32)
     for i in range(count):
         out = jnp.where(index == i, ref[i], out)
-    return out[:, 0:1]
+    return out
+
+
+def tail_weights(mix_ref, slope_ref, shift_ref, cols_ref, mix_out_ref):
+    cols_ref[0:32, :] = column(slope_ref, 32)
+    cols_ref[32:40, :] = column(shift_ref, 5)
+    mix_out_ref[...] = joined(jnp.concatenate([mix_ref[...], jnp.zeros((3, 32), F32)], 0))
 
 
 def shifted_sum(stack):
@@ -270,8 +276,10 @@
 
 
 def dual_known_kernel(
-    own_ref, first_ref, second_ref, kern_ref, bias_ref, known_ref, last_ref, tt_ref, lt_ref
+    own_ref, first_ref, second_ref, kern_ref, mix_ref, bias_ref, slope_ref, shift_ref,
+    known_ref, last_ref, cols_ref, mix_out_ref, tt_ref, lt_ref,
 ):
+    tail_weights(mix_ref, slope_ref, shift_ref, cols_ref, mix_out_ref)
     tt_ref[...] = jnp.zeros((80, 96), F32)
     lt_ref[...] = jnp.zeros((80, 128), F32)
     for dz in range(3):
@@ -287,7 +295,7 @@
     last_ref[...] = joined(lt_ref[...].T)
     x = dual_inputs(own_ref, first_ref, second_ref)
     tt = joined(tt_ref[...].T)
-    bias = column(bias_ref, 32)
+    bias = column(bias_ref, 32)[:, 0:1]
     for z in range(4):
         h = dot3(tt, x[z * 24 : z * 24 + 80])
         h = shifted_sum([h[i * 32 : (i + 1) * 32] for i in range(3)]) + bias
@@ -303,7 +311,7 @@
 
 def dual_kernel_body(
     total_ref, ta_ref, tb_ref, own_ref, first_ref, second_ref, known_ref, last_ref,
-    mix_ref, slope_ref, shift_ref, new_ref, send_ref, y_ref,
+    cols_ref, mix_ref, new_ref, send_ref, y_ref,
 ):
     y_ref[...] = jnp.zeros((80, 1024), F32)
     before, after = plane_sides(ta_ref, tb_ref, slice(0, 48))
@@ -315,8 +323,7 @@
                     i = k * 16 + z * 8 + b
                     y_ref[row : row + 1, b * 128 : (b + 1) * 128] = v[i : i + 1]
     spread_columns(y_ref, 1024)
-    slope, shift = column(slope_ref, 32), column(shift_ref, 5)
-    mix = joined(jnp.concatenate([mix_ref[...], jnp.zeros((3, 32), F32)], 0))
+    slope, shift, mix = cols_ref[0:32, 0:1], cols_ref[32:40, 0:1], mix_ref[...]
     h = dot3(last_ref[...], y_ref[...]) + known_ref[...]
     dual_rows = (
         plane_sides(first_ref, second_ref, slice(32, 40))[0],
@@ -406,8 +413,8 @@
 
 def primal_inner_kernel(
     sp_ref, sm_ref, first_ref, second_ref, back_ref, primal_ref, kern_ref, mix_ref,
-    bias_ref, slope_ref, shift_ref, part_ref, rim_ref, out_hbm,
-    tt_ref, lt_ref, lr_ref, x_ref, y_ref, out_ref, sem,
+    bias_ref, slope_ref, shift_ref, part_ref, rim_ref, out_ref, cols_ref, mix_out_ref,
+    tt_ref, lt_ref, lr_ref, x_ref, y_ref,
 ):
     p = lax.axis_index("plane")
     keeps = (p > 0, None, None, p < 7)
@@ -455,8 +462,9 @@
                         lr_ref[i : i + 1, k * 32 : (k + 1) * 32] = four[:, k * 32 : (k + 1) * 32]
     rim_ref[...] = joined(lr_ref[...].T)
     tt = joined(tt_ref[...].T)
-    bias, slope, shift = column(bias_ref, 32), column(slope_ref, 32), column(shift_ref, 5)
-    mix = joined(jnp.concatenate([mix_ref[...], jnp.zeros((3, 32), F32)], 0))
+    tail_weights(mix_ref, slope_ref, shift_ref, cols_ref, mix_out_ref)
+    bias = column(bias_ref, 32)[:, 0:1]
+    slope, shift, mix = cols_ref[0:32, 0:1], cols_ref[32:40, 0:1], mix_out_ref[...]
     own = dot3(joined(lt_ref[...].T), y_ref[...])
     for z in range(2):
         h = dot3(tt, x_ref[z * 32 : z * 32 + 96])
@@ -470,17 +478,18 @@
             else:
                 out = finish(g, mix, slope, shift)
                 for c in range(5):
-                    out_ref[c, z, r - 1 : r, :] = out[c : c + 1] + primal_ref[c, z, r : r + 1, :]
-    copy = pltpu.make_async_copy(out_ref, out_hbm.at[:, :, 1:3, :], sem)
-    copy.start()
-    copy.wait()
+                    out_ref[c, z, r : r + 1, :] = out[c : c + 1] + primal_ref[c, z, r : r + 1, :]
+    for z in range(2):
+        for c in range(5):
+            for r in (0, 3):
+                out_ref[c, z, r : r + 1, :] = primal_ref[c, z, r : r + 1, :]
 
 
 def primal_outer_kernel(
-    first_ref, second_ref, part_ref, rim_ref, primal_ref, mix_ref, slope_ref, shift_ref,
-    inner_hbm, out_hbm, y_ref, out_ref, sem,
+    first_ref, second_ref, part_ref, rim_ref, inner_ref, cols_ref, mix_ref,
+    out_hbm, y_ref, out_ref, sem,
 ):
-    del inner_hbm
+    out_ref[...] = inner_ref[...]
     p = lax.axis_index("plane")
     t = lax.axis_index("tile")
     keeps = (p > 0, None, None, p < 7)
@@ -502,21 +511,16 @@
     y_ref[0:8, :] = jnp.where(lane == 0, 0.0, pltpu.roll(mid, 1, 1))
     y_ref[16:24, :] = jnp.where(lane == 511, 0.0, pltpu.roll(mid, 511, 1))
     y_ref[24:32, :] = jnp.zeros((8, 512), F32)
-    slope, shift = column(slope_ref, 32), column(shift_ref, 5)
-    mix = joined(jnp.concatenate([mix_ref[...], jnp.zeros((3, 32), F32)], 0))
+    slope, shift, mix = cols_ref[0:32, 0:1], cols_ref[32:40, 0:1], mix_ref[...]
     h = dot3(rim_ref[...], y_ref[...]) + part_ref[...]
     copies = []
-    for rim, row in enumerate((0, 3)):
-        for z in range(2):
+    for z in range(2):
+        for rim, row in enumerate((0, 3)):
             i = (z * 2 + rim) * 32
             out = finish(h[i : i + 32], mix, slope, shift)
             for c in range(5):
-                out_ref[rim, c, z] = out[c : c + 1] + primal_ref[c, z, row : row + 1, :]
-        copies.append(
-            pltpu.make_async_copy(
-                out_ref.at[rim], out_hbm.at[:, :, row : row + 1, :], sem.at[rim]
-            )
-        )
+                out_ref[c, z, row : row + 1, :] += out[c : c + 1]
+        copies.append(pltpu.make_async_copy(out_ref.at[:, z], out_hbm.at[:, z], sem.at[z]))
         copies[-1].start()
     for copy in copies:
         copy.wait()
@@ -598,18 +602,21 @@
     total = call(total_kernel, [((48, 128), F32)], [VMEM])(got)[0]
     rows = swaps(total, total, "plane")
 
-    known, last = call(
-        dual_known_kernel, [((128, 1024), F32), ((128, 240), BF16)],
-        [VMEM] * 4 + [SMEM],
+    known, last, cols, mix = call(
+        dual_known_kernel,
+        [((128, 1024), F32), ((128, 240), BF16), ((40, 128), F32), ((8, 96), BF16)],
+        [VMEM] * 5 + [SMEM] * 3,
         [pltpu.VMEM((80, 96), F32), pltpu.VMEM((80, 128), F32)],
-    )(sp, *sides, jnp.transpose(dual_kernel, (2, 3, 4, 1, 0)), dual_bias)
+    )(
+        sp, *sides, jnp.transpose(dual_kernel, (2, 3, 4, 1, 0)), dual_mixing,
+        dual_bias, dual_slope, dual_shift,
+    )
 
     new_rows, send = call(
         dual_kernel_body, [((5, 2, 1, 1024), F32), ((16, 8, 4, 128), F32)],
-        [VMEM] * 9 + [SMEM] * 2, [pltpu.VMEM((80, 1024), F32)],
+        [VMEM] * 10, [pltpu.VMEM((80, 1024), F32)],
     )(
-        total, *rows, sp, *sides, known, last, dual_mixing,
-        dual_slope, dual_shift,
+        total, *rows, sp, *sides, known, last, cols, mix,
     )
     leading = lax.all_to_all(send, "tile", 0, 0, tiled=True)
 
@@ -639,24 +646,24 @@
     )
     edges = swaps(edge_a, edge_b, "tile")
 
-    part, rim, inner = pl.pallas_call(
+    part, rim, inner, cols, mix = pl.pallas_call(
         primal_inner_kernel,
         name="primal_inner",
         out_shape=(
             jax.ShapeDtypeStruct((128, 512), F32),
             jax.ShapeDtypeStruct((128, 96), BF16),
             jax.ShapeDtypeStruct((5, 2, 4, 512), F32),
+            jax.ShapeDtypeStruct((40, 128), F32),
+            jax.ShapeDtypeStruct((8, 96), BF16),
         ),
         in_specs=[VMEM] * 8 + [SMEM] * 3,
-        out_specs=(VMEM, VMEM, HBM),
+        out_specs=(VMEM,) * 5,
         scratch_shapes=[
             pltpu.VMEM((96, 384), F32),
             pltpu.VMEM((80, 256), F32),
             pltpu.VMEM((32, 128), F32),
             pltpu.VMEM((128, 512), F32),
             pltpu.VMEM((80, 512), F32),
-            pltpu.VMEM((5, 2, 2, 512), F32),
-            pltpu.SemaphoreType.DMA,
         ],
         compiler_params=pltpu.CompilerParams(vmem_limit_bytes=8 << 20),
     )(
@@ -668,17 +675,16 @@
         primal_outer_kernel,
         name="primal_outer",
         out_shape=jax.ShapeDtypeStruct((5, 2, 4, 512), F32),
-        in_specs=[VMEM] * 6 + [SMEM] * 2 + [HBM],
+        in_specs=[VMEM] * 7,
         out_specs=HBM,
         scratch_shapes=[
             pltpu.VMEM((32, 512), F32),
-            pltpu.VMEM((2, 5, 2, 1, 512), F32),
+            pltpu.VMEM((5, 2, 4, 512), F32),
             pltpu.SemaphoreType.DMA((2,)),
         ],
-        input_output_aliases={8: 0},
         compiler_params=pltpu.CompilerParams(vmem_limit_bytes=8 << 20),
     )(
-        *edges, part, rim, primal, primal_mixing, primal_slope, primal_shift, hbm(inner),
+        *edges, part, rim, inner, cols, mix,
     )
     return new_primal, new_dual
 

time: 72.3 us -> 71.2 us (0.985)
  Pallas kernels: 20.4 us -> 18.7 us
  transfers between devices with their start and end apart: 9 -> 9, of which waited for: 3 -> 3; matrix products, arithmetic and copies ran while one was open for 0% -> 0% of each run, Pallas kernels for 16% -> 15%
where the time goes in v9:
time: 71.2 us; the launch traced here: 70.9 us
  Pallas kernels  18.7 us (26%)
  starting transfers between devices  17 us (24%)
  blocking collectives  12 us (17%)
  local copies, waits for them, and re-layouts  11.6 us (16%)
  waiting for transfers between devices  10.7 us (15%)
  between operations  0.83 us (1%)
    all_to_all x1, blocking collectives, per_device(): leading = lax.all_to_all(send, 'tile', 0, 0, tiled=True)  12 us
    ppermute x4, starting transfers between devices, swaps(): b = lax.ppermute(second, axis, pairs)  12 us
    unnamed x30, local copies, waits for them, and re-layouts  11.6 us
    pallas_call x1, Pallas kernels, per_device(): pl.pallas_call(project_kernel, name='project', out_shape=(jax.ShapeDtypeS...  6.85 us
    all_to_all x1, waiting for transfers between devices, per_device(): got = lax.all_to_all(terms, 'tile', 0, 0, tiled=True)  6.71 us
    pallas_call x1, Pallas kernels, per_device(): pl.pallas_call(back_kernel, name='back', out_shape=(jax.ShapeDtypeStruct(...  5.27 us
    ppermute x4, waiting for transfers between devices, swaps(): b = lax.ppermute(second, axis, pairs)  3.97 us
    all_to_all x1, starting transfers between devices, per_device(): got = lax.all_to_all(terms, 'tile', 0, 0, tiled=True)  3.55 us
  transfers between devices with their start and end apart: 9, of which 3 were waited for; matrix products, arithmetic and copies ran while one was open for 0% of the time, Pallas kernels for 15%

profile of v9, /device:TPU:0, one launch (start us, length us, event | category | flops | bytes accessed | tf_op | source)
XLA Modules:
  0.0 70.9 jit_solution(10005065110367958399)
XLA Ops:
  0.6 1.0 %shard_map.176.after_ref.own_ref = f32[32,1024]{1,0:T(8,128)S(1)} custom-call(f32[5,2,1,1024]{3,2,1,0:T(1,128)} %dual_hbm.1, f32[2,1,1024]{2,1,0:T(1,128)} %measured_hbm.1, f32[5,2,4,512]{3,2,1,0:T(4,128)} %primal_ref.3), custom_call_target="tpu_custom_call" | custom-call | tf_op jit(solution)/shard_map/pallas_call | solution.py:557
  1.6 6.7 %collective-permute-start.1 = (f32[32,1024]{1,0:T(8,128)S(1)}, f32[32,1024]{1,0:T(8,128)S(1)}, u32[]{:S(2)}, u32[]{:S(2)}) collective-permute-start(f32[32,1024]{1,0:T(8,128)S(1)} %shard_map.176.after_ref.own_ref), channel_id=1, source_target_pairs={{0,15},{1,2},{2,1},{3,4},{4,3},{5,6},{6,5},{7,8},{8,7},{9,10},{10,... | collective-permute-start | bytes 393224 | tf_op jit(solution)/shard_map/ppermute | solution.py:544
  8.3 6.9 %project.1 = (f32[16,3,16,128]{3,2,1,0:T(8,128)}, bf16[104,256,128]{2,1,0:T(8,128)(2,1)S(1)}, bf16[104,256,128]{2,1,0:T(8,128)(2,1)S(1)}) custom-call(s32[12,1,16]{2,1,0:T(1,128)} %bitcast.10, s32[12,16,16]{2,1,0:T(8,128)} %bitcast.8, s32[1,16]{1,0:T(1,128)} %cnt_hbm.3, f32[5,2,4,512]{3,2,1,0:T(4,128)} %primal_ref.3, f32[16,6,256,128]{3,2,1,0:T(8,128)} %bitcast.7, ...), custom_call_target="tpu_custom_call" | custom-call | flops 2147483648 | bytes 26214400 | tf_op jit(solution)/shard_map/project/pallas_call | solution.py:570
  15.2 2.8 %copy-done = bf16[104,256,128]{2,1,0:T(8,128)(2,1)} copy-done((bf16[104,256,128]{2,1,0:T(8,128)(2,1)}, bf16[104,256,128]{2,1,0:T(8,128)(2,1)S(1)}, u32[]{:S(2)}) %copy-start) | copy-done | bytes 6815768
  18.0 2.9 %copy-done.2 = bf16[104,256,128]{2,1,0:T(8,128)(2,1)} copy-done((bf16[104,256,128]{2,1,0:T(8,128)(2,1)}, bf16[104,256,128]{2,1,0:T(8,128)(2,1)S(1)}, u32[]{:S(2)}) %copy-start.2) | copy-done | bytes 6815768
  20.9 3.6 %all-to-all-start = ((f32[16,3,16,128]{3,2,1,0:T(8,128)}), f32[16,3,16,128]{3,2,1,0:T(8,128)S(1)}, u32[]{:S(2)}, u32[]{:S(2)}) async-start(f32[16,3,16,128]{3,2,1,0:T(8,128)} %get-tuple-element.28), calls=%async_computation | async-start | bytes 786432 | tf_op jit(solution)/shard_map/all_to_all | solution.py:601
  24.5 0.1 shard_map.178
  24.6 0.1 collective-permute-start.4
  24.7 2.9 %collective-permute-start.5 = (f32[64,1024]{1,0:T(8,128)S(1)}, f32[64,1024]{1,0:T(8,128)S(1)}, u32[]{:S(2)}, u32[]{:S(2)}) collective-permute-start(f32[64,1024]{1,0:T(8,128)S(1)} %get-tuple-element.33), channel_id=1, source_target_pairs={{0,112},{16,32},{32,16},{48,64},{64,48},{80,96},{96,80},{112,0},{1... | collective-permute-start | bytes 786440 | tf_op jit(solution)/shard_map/ppermute | solution.py:544
  27.5 6.7 %all-to-all-done.got_ref = f32[16,3,16,128]{3,2,1,0:T(8,128)S(1)} async-done(((f32[16,3,16,128]{3,2,1,0:T(8,128)}), f32[16,3,16,128]{3,2,1,0:T(8,128)S(1)}, u32[]{:S(2)}, u32[]{:S(2)}) %all-to-all-start) | async-done | bytes 393248 | tf_op jit(solution)/shard_map/all_to_all | solution.py:601
  34.3 0.4 collective-permute-start.3
  34.7 1.3 %collective-permute-start.2 = (f32[48,128]{1,0:T(8,128)S(1)}, f32[48,128]{1,0:T(8,128)S(1)}, u32[]{:S(2)}, u32[]{:S(2)}) collective-permute-start(f32[48,128]{1,0:T(8,128)S(1)} %shard_map.177.total_ref), channel_id=1, source_target_pairs={{0,16},{16,0},{32,48},{48,32},{64,80},{80,64},{96,112},{112,96},{1... | collective-permute-start | bytes 73736 | tf_op jit(solution)/shard_map/ppermute | solution.py:542
  36.0 1.4 %shard_map.179 = (f32[128,1024]{1,0:T(8,128)S(1)}, bf16[128,240]{1,0:T(8,128)(2,1)S(1)}, f32[40,128]{1,0:T(8,128)S(1)}, bf16[8,96]{1,0:T(8,128)(2,1)S(1)}) custom-call(f32[64,1024]{1,0:T(8,128)S(1)} %get-tuple-element.31.own_ref.sp_ref, f32[64,1024]{1,0:T(8,128)S(1)} %collective-permute-done.4.first_ref, f32[64,1024]{1,0:T(8,128)S(1)} %collective-permute-done.5.second_ref, ...), custom_call_target="tpu_custom_call" | custom-call | tf_op jit(solution)/shard_map/pallas_call | solution.py:605
  37.4 1.4 %collective-permute-done.3.tb_ref = f32[48,128]{1,0:T(8,128)S(1)} collective-permute-done((f32[48,128]{1,0:T(8,128)S(1)}, f32[48,128]{1,0:T(8,128)S(1)}, u32[]{:S(2)}, u32[]{:S(2)}) %collective-permute-start.3) | collective-permute-done | bytes 24608 | tf_op jit(solution)/shard_map/ppermute | solution.py:544
  38.8 0.7 shard_map.180
  39.5 12.0 %all_to_all.10.nd_ref = f32[16,8,4,128]{3,2,1,0:T(4,128)S(1)} all-to-all(f32[16,8,4,128]{3,2,1,0:T(4,128)S(1)} %get-tuple-element.38), channel_id=1, replica_groups=mesh['plane'=8,'tile'=16] {'tile'}, dimensions={0} | all-to-all | bytes 524288 | tf_op jit(solution)/shard_map/all_to_all | solution.py:621
  51.5 2.9 %copy-done.1 = bf16[104,256,128]{2,1,0:T(8,128)(2,1)S(1)} copy-done((bf16[104,256,128]{2,1,0:T(8,128)(2,1)S(1)}, bf16[104,256,128]{2,1,0:T(8,128)(2,1)}, u32[]{:S(2)}) %copy-start.1) | copy-done | bytes 6815768
  54.4 2.9 %copy-done.3 = bf16[104,256,128]{2,1,0:T(8,128)(2,1)S(1)} copy-done((bf16[104,256,128]{2,1,0:T(8,128)(2,1)S(1)}, bf16[104,256,128]{2,1,0:T(8,128)(2,1)}, u32[]{:S(2)}) %copy-start.3) | copy-done | bytes 6815768
  57.4 5.3 %back.1 = (f32[64,128]{1,0:T(8,128)S(1)}, f32[16,128]{1,0:T(8,128)S(1)}, f32[16,128]{1,0:T(8,128)S(1)}, f32[5,2,1,1024]{3,2,1,0:T(1,128)}) custom-call(s32[12,1,16]{2,1,0:T(1,128)} %bitcast.11, s32[12,16,16]{2,1,0:T(8,128)} %bitcast.9, s32[1,16]{1,0:T(1,128)} %cnt_hbm.3, f32[16,8,4,128]{3,2,1,0:T(4,128)S(1)} %all_to_all.10.nd_ref, ...), custom_call_target="tpu_custom_call" | custom-call | tf_op jit(solution)/shard_map/back/pallas_call | solution.py:623
  62.6 0.1 collective-permute-start.6
  62.8 2.1 %collective-permute-start.7 = (f32[16,128]{1,0:T(8,128)S(1)}, f32[16,128]{1,0:T(8,128)S(1)}, u32[]{:S(2)}, u32[]{:S(2)}) collective-permute-start(f32[16,128]{1,0:T(8,128)S(1)} %get-tuple-element.43), channel_id=1, source_target_pairs={{0,15},{1,2},{2,1},{3,4},{4,3},{5,6},{6,5},{7,8},{8,7},{9,10},{10,... | collective-permute-start | bytes 24584 | tf_op jit(solution)/shard_map/ppermute | solution.py:544
  64.8 2.4 %primal_inner.1 = (f32[128,512]{1,0:T(8,128)S(1)}, bf16[128,96]{1,0:T(8,128)(2,1)S(1)}, f32[5,2,4,512]{3,2,1,0:T(4,128)S(1)}, f32[40,128]{1,0:T(8,128)S(1)}, bf16[8,96]{1,0:T(8,128)(2,1)S(1)}) custom-call(f32[64,1024]{1,0:T(8,128)S(1)} %get-tuple-element.31.own_ref.sp_ref, f32[64,1024]{1,0:T(8,128)S(1)} %get-tuple-element.44.sm_ref, ...), custom_call_target="tpu_custom_call" | custom-call | tf_op jit(solution)/shard_map/primal_inner/pallas_call | solution.py:649
  67.2 2.6 %collective-permute-done.7.second_ref = f32[16,128]{1,0:T(8,128)S(1)} collective-permute-done((f32[16,128]{1,0:T(8,128)S(1)}, f32[16,128]{1,0:T(8,128)S(1)}, u32[]{:S(2)}, u32[]{:S(2)}) %collective-permute-start.7) | collective-permute-done | bytes 8224 | tf_op jit(solution)/shard_map/ppermute | solution.py:544
  69.8 1.1 %primal_outer.1 = f32[5,2,4,512]{3,2,1,0:T(4,128)} custom-call(f32[16,128]{1,0:T(8,128)S(1)} %collective-permute-done.6.first_ref, f32[16,128]{1,0:T(8,128)S(1)} %collective-permute-done.7.second_ref, f32[128,512]{1,0:T(8,128)S(1)} %get-tuple-element.46.part_ref, bf16[128,96]{1,0:T(8,128)(2,1)S(1)} %get-tuple-element.47.rim_ref, ...), custom_call_target="tpu_custom_call" | custom-call | tf_op jit(solution)/shard_map/primal_outer/pallas_call | solution.py:674
  (34 shorter events, 0.1 us)
Async XLA Ops:
  1.6 19.3 %collective-permute-start.1 = (f32[32,1024]{1,0:T(8,128)S(1)}, f32[32,1024]{1,0:T(8,128)S(1)}, u32[]{:S(2)}, u32[]{:S(2)}) collective-permute-start(f32[32,1024]{1,0:T(8,128)S(1)} %shard_map.176.after_ref.own_ref), channel_id=1, source_target_pairs={{0,15},{1,2},{2,1},{3,4},{4,3},{5,6},{6,5},{7,8},{8,7},{9,10},{10,... | collective-permute-start | bytes 393224 | tf_op jit(solution)/shard_map/ppermute | solution.py:544
  8.3 12.6 %collective-permute-start = (f32[32,1024]{1,0:T(8,128)S(1)}, f32[32,1024]{1,0:T(8,128)S(1)}, u32[]{:S(2)}, u32[]{:S(2)}) collective-permute-start(f32[32,1024]{1,0:T(8,128)S(1)} %shard_map.176.after_ref.own_ref), channel_id=1, source_target_pairs={{0,1},{1,0},{2,3},{3,2},{4,5},{5,4},{6,7},{7,6},{8,9},{9,8},{10,11... | collective-permute-start | bytes 393224 | tf_op jit(solution)/shard_map/ppermute | solution.py:542
  8.3 16.2 %copy-start.4 = (f32[5,2,4,512]{3,2,1,0:T(4,128)S(1)}, f32[5,2,4,512]{3,2,1,0:T(4,128)}, u32[]{:S(2)}) copy-start(f32[5,2,4,512]{3,2,1,0:T(4,128)} %primal_ref.3) | copy-start | bytes 245764
  8.3 27.6 %copy-start.5 = (f32[32,7,3,3,3]{0,1,4,3,2:T(8,128)S(1)}, f32[32,7,3,3,3]{0,1,4,3,2:T(8,128)}, u32[]{:S(2)}) copy-start(f32[32,7,3,3,3]{0,1,4,3,2:T(8,128)} %param.24) | copy-start | bytes 72580
  8.3 27.7 %copy-start.7 = (f32[5,32]{1,0:T(8,128)S(1)}, f32[5,32]{1,0:T(8,128)}, u32[]{:S(2)}) copy-start(f32[5,32]{1,0:T(8,128)} %mix_ref.2) | copy-start | bytes 1924
  8.3 27.7 %copy-start.9 = (f32[32]{0:T(128)S(1)}, f32[32]{0:T(128)}, u32[]{:S(2)}) copy-start(f32[32]{0:T(128)} %bias_ref.2) | copy-start | bytes 388
  8.3 27.7 %copy-start.10 = (f32[32]{0:T(128)S(1)}, f32[32]{0:T(128)}, u32[]{:S(2)}) copy-start(f32[32]{0:T(128)} %slope_ref.2) | copy-start | bytes 388
  8.3 27.7 %copy-start.11 = (f32[5]{0:T(128)S(1)}, f32[5]{0:T(128)}, u32[]{:S(2)}) copy-start(f32[5]{0:T(128)} %shift_ref.2) | copy-start | bytes 64
  15.2 2.8 %copy-start = (bf16[104,256,128]{2,1,0:T(8,128)(2,1)}, bf16[104,256,128]{2,1,0:T(8,128)(2,1)S(1)}, u32[]{:S(2)}) copy-start(bf16[104,256,128]{2,1,0:T(8,128)(2,1)S(1)} %get-tuple-element.39.wh_ref) | copy-start | bytes 20447236
  18.0 2.9 %copy-start.2 = (bf16[104,256,128]{2,1,0:T(8,128)(2,1)}, bf16[104,256,128]{2,1,0:T(8,128)(2,1)S(1)}, u32[]{:S(2)}) copy-start(bf16[104,256,128]{2,1,0:T(8,128)(2,1)S(1)} %get-tuple-element.40.wl_ref) | copy-start | bytes 20447236
  20.9 13.3 %all-to-all-start = ((f32[16,3,16,128]{3,2,1,0:T(8,128)}), f32[16,3,16,128]{3,2,1,0:T(8,128)S(1)}, u32[]{:S(2)}, u32[]{:S(2)}) async-start(f32[16,3,16,128]{3,2,1,0:T(8,128)} %get-tuple-element.28), calls=%async_computation | async-start | bytes 786432 | tf_op jit(solution)/shard_map/all_to_all | solution.py:601
  24.6 11.4 %collective-permute-start.4 = (f32[64,1024]{1,0:T(8,128)S(1)}, f32[64,1024]{1,0:T(8,128)S(1)}, u32[]{:S(2)}, u32[]{:S(2)}) collective-permute-start(f32[64,1024]{1,0:T(8,128)S(1)} %get-tuple-element.32), channel_id=1, source_target_pairs={{0,16},{16,0},{32,48},{48,32},{64,80},{80,64},{96,112},{112,96},{1... | collective-permute-start | bytes 786440 | tf_op jit(solution)/shard_map/ppermute | solution.py:542
  24.7 11.3 %collective-permute-start.5 = (f32[64,1024]{1,0:T(8,128)S(1)}, f32[64,1024]{1,0:T(8,128)S(1)}, u32[]{:S(2)}, u32[]{:S(2)}) collective-permute-start(f32[64,1024]{1,0:T(8,128)S(1)} %get-tuple-element.33), channel_id=1, source_target_pairs={{0,112},{16,32},{32,16},{48,64},{64,48},{80,96},{96,80},{112,0},{1... | collective-permute-start | bytes 786440 | tf_op jit(solution)/shard_map/ppermute | solution.py:544
  34.3 4.5 %collective-permute-start.3 = (f32[48,128]{1,0:T(8,128)S(1)}, f32[48,128]{1,0:T(8,128)S(1)}, u32[]{:S(2)}, u32[]{:S(2)}) collective-permute-start(f32[48,128]{1,0:T(8,128)S(1)} %shard_map.177.total_ref), channel_id=1, source_target_pairs={{0,112},{16,32},{32,16},{48,64},{64,48},{80,96},{96,80},{112,0},{1... | collective-permute-start | bytes 73736 | tf_op jit(solution)/shard_map/ppermute | solution.py:544
  34.7 4.1 %collective-permute-start.2 = (f32[48,128]{1,0:T(8,128)S(1)}, f32[48,128]{1,0:T(8,128)S(1)}, u32[]{:S(2)}, u32[]{:S(2)}) collective-permute-start(f32[48,128]{1,0:T(8,128)S(1)} %shard_map.177.total_ref), channel_id=1, source_target_pairs={{0,16},{16,0},{32,48},{48,32},{64,80},{80,64},{96,112},{112,96},{1... | collective-permute-start | bytes 73736 | tf_op jit(solution)/shard_map/ppermute | solution.py:542
  51.5 2.9 %copy-start.1 = (bf16[104,256,128]{2,1,0:T(8,128)(2,1)S(1)}, bf16[104,256,128]{2,1,0:T(8,128)(2,1)}, u32[]{:S(2)}) copy-start(bf16[104,256,128]{2,1,0:T(8,128)(2,1)} %copy-done) | copy-start | bytes 20447236
  54.4 2.9 %copy-start.3 = (bf16[104,256,128]{2,1,0:T(8,128)(2,1)S(1)}, bf16[104,256,128]{2,1,0:T(8,128)(2,1)}, u32[]{:S(2)}) copy-start(bf16[104,256,128]{2,1,0:T(8,128)(2,1)} %copy-done.2) | copy-start | bytes 20447236
  57.3 7.5 %copy-start.6 = (f32[32,6,3,3,3]{0,4,3,2,1:T(4,128)S(1)}, f32[32,6,3,3,3]{0,4,3,2,1:T(4,128)}, u32[]{:S(2)}) copy-start(f32[32,6,3,3,3]{0,4,3,2,1:T(4,128)} %param.29) | copy-start | bytes 62212
  57.3 7.5 %copy-start.8 = (f32[5,32]{1,0:T(8,128)S(1)}, f32[5,32]{1,0:T(8,128)}, u32[]{:S(2)}) copy-start(f32[5,32]{1,0:T(8,128)} %mix_ref.3) | copy-start | bytes 1924
  57.3 7.5 %copy-start.12 = (f32[32]{0:T(128)S(1)}, f32[32]{0:T(128)}, u32[]{:S(2)}) copy-start(f32[32]{0:T(128)} %bias_ref.3) | copy-start | bytes 388
  57.4 7.5 %copy-start.13 = (f32[32]{0:T(128)S(1)}, f32[32]{0:T(128)}, u32[]{:S(2)}) copy-start(f32[32]{0:T(128)} %slope_ref.3) | copy-start | bytes 388
  57.4 7.5 %copy-start.14 = (f32[5]{0:T(128)S(1)}, f32[5]{0:T(128)}, u32[]{:S(2)}) copy-start(f32[5]{0:T(128)} %shift_ref.3) | copy-start | bytes 64
  62.6 4.6 %collective-permute-start.6 = (f32[16,128]{1,0:T(8,128)S(1)}, f32[16,128]{1,0:T(8,128)S(1)}, u32[]{:S(2)}, u32[]{:S(2)}) collective-permute-start(f32[16,128]{1,0:T(8,128)S(1)} %get-tuple-element.42), channel_id=1, source_target_pairs={{0,1},{1,0},{2,3},{3,2},{4,5},{5,4},{6,7},{7,6},{8,9},{9,8},{10,11... | collective-permute-start | bytes 24584 | tf_op jit(solution)/shard_map/ppermute | solution.py:542
  62.8 7.0 %collective-permute-start.7 = (f32[16,128]{1,0:T(8,128)S(1)}, f32[16,128]{1,0:T(8,128)S(1)}, u32[]{:S(2)}, u32[]{:S(2)}) collective-permute-start(f32[16,128]{1,0:T(8,128)S(1)} %get-tuple-element.43), channel_id=1, source_target_pairs={{0,15},{1,2},{2,1},{3,4},{4,3},{5,6},{6,5},{7,8},{8,7},{9,10},{10,... | collective-permute-start | bytes 24584 | tf_op jit(solution)/shard_map/ppermute | solution.py:544

commit v10 on v9

--- a/solution.py
+++ b/solution.py
@@ -9,7 +9,6 @@
 F32 = jnp.float32
 BF16 = jnp.bfloat16
 VMEM = pl.BlockSpec(memory_space=pltpu.VMEM)
-SMEM = pl.BlockSpec(memory_space=pltpu.SMEM)
 HBM = pl.BlockSpec(memory_space=pltpu.HBM)
 
 
@@ -32,19 +31,16 @@
     return jnp.dot(left, jnp.concatenate([hi, hi, lo], 0), preferred_element_type=F32)
 
 
-def column(ref, count):
-    rows = -(-count // 8) * 8
-    index = lax.broadcasted_iota(jnp.int32, (rows, 128), 0)
-    out = jnp.zeros((rows, 128), F32)
-    for i in range(count):
-        out = jnp.where(index == i, ref[i], out)
-    return out
-
-
-def tail_weights(mix_ref, slope_ref, shift_ref, cols_ref, mix_out_ref):
-    cols_ref[0:32, :] = column(slope_ref, 32)
-    cols_ref[32:40, :] = column(shift_ref, 5)
+def tail_weights(mix_ref, bias_ref, slope_ref, shift_ref, cols_ref, mix_out_ref, vec_ref):
+    vec_ref[...] = jnp.zeros((8, 128), F32)
+    vec_ref[0:1, 0:32] = bias_ref[...]
+    vec_ref[1:2, 0:32] = slope_ref[...]
+    vec_ref[2:3, 0:5] = shift_ref[...]
+    columns = vec_ref[...].T
+    cols_ref[0:32, :] = jnp.broadcast_to(columns[0:32, 1:2], (32, 128))
+    cols_ref[32:40, :] = jnp.broadcast_to(columns[0:8, 2:3], (8, 128))
     mix_out_ref[...] = joined(jnp.concatenate([mix_ref[...], jnp.zeros((3, 32), F32)], 0))
+    return columns[0:32, 0:1]
 
 
 def shifted_sum(stack):
@@ -277,9 +273,11 @@
 
 def dual_known_kernel(
     own_ref, first_ref, second_ref, kern_ref, mix_ref, bias_ref, slope_ref, shift_ref,
-    known_ref, last_ref, cols_ref, mix_out_ref, tt_ref, lt_ref,
+    known_ref, last_ref, cols_ref, mix_out_ref, tt_ref, lt_ref, vec_ref,
 ):
-    tail_weights(mix_ref, slope_ref, shift_ref, cols_ref, mix_out_ref)
+    bias = tail_weights(
+        mix_ref, bias_ref, slope_ref, shift_ref, cols_ref, mix_out_ref, vec_ref
+    )
     tt_ref[...] = jnp.zeros((80, 96), F32)
     lt_ref[...] = jnp.zeros((80, 128), F32)
     for dz in range(3):
@@ -295,7 +293,6 @@
     last_ref[...] = joined(lt_ref[...].T)
     x = dual_inputs(own_ref, first_ref, second_ref)
     tt = joined(tt_ref[...].T)
-    bias = column(bias_ref, 32)[:, 0:1]
     for z in range(4):
         h = dot3(tt, x[z * 24 : z * 24 + 80])
         h = shifted_sum([h[i * 32 : (i + 1) * 32] for i in range(3)]) + bias
@@ -414,7 +411,7 @@
 def primal_inner_kernel(
     sp_ref, sm_ref, first_ref, second_ref, back_ref, primal_ref, kern_ref, mix_ref,
     bias_ref, slope_ref, shift_ref, part_ref, rim_ref, out_ref, cols_ref, mix_out_ref,
-    tt_ref, lt_ref, lr_ref, x_ref, y_ref,
+    tt_ref, lt_ref, lr_ref, x_ref, y_ref, vec_ref,
 ):
     p = lax.axis_index("plane")
     keeps = (p > 0, None, None, p < 7)
@@ -462,8 +459,9 @@
                         lr_ref[i : i + 1, k * 32 : (k + 1) * 32] = four[:, k * 32 : (k + 1) * 32]
     rim_ref[...] = joined(lr_ref[...].T)
     tt = joined(tt_ref[...].T)
-    tail_weights(mix_ref, slope_ref, shift_ref, cols_ref, mix_out_ref)
-    bias = column(bias_ref, 32)[:, 0:1]
+    bias = tail_weights(
+        mix_ref, bias_ref, slope_ref, shift_ref, cols_ref, mix_out_ref, vec_ref
+    )
     slope, shift, mix = cols_ref[0:32, 0:1], cols_ref[32:40, 0:1], mix_out_ref[...]
     own = dot3(joined(lt_ref[...].T), y_ref[...])
     for z in range(2):
@@ -605,11 +603,15 @@
     known, last, cols, mix = call(
         dual_known_kernel,
         [((128, 1024), F32), ((128, 240), BF16), ((40, 128), F32), ((8, 96), BF16)],
-        [VMEM] * 5 + [SMEM] * 3,
-        [pltpu.VMEM((80, 96), F32), pltpu.VMEM((80, 128), F32)],
+        [VMEM] * 8,
+        [
+            pltpu.VMEM((80, 96), F32),
+            pltpu.VMEM((80, 128), F32),
+            pltpu.VMEM((8, 128), F32),
+        ],
     )(
         sp, *sides, jnp.transpose(dual_kernel, (2, 3, 4, 1, 0)), dual_mixing,
-        dual_bias, dual_slope, dual_shift,
+        dual_bias.reshape(1, 32), dual_slope.reshape(1, 32), dual_shift.reshape(1, 5),
     )
 
     new_rows, send = call(
@@ -629,7 +631,7 @@
             jax.ShapeDtypeStruct((16, 128), F32),
             jax.ShapeDtypeStruct((5, 2, 1, 1024), F32),
         ),
-        in_specs=[HBM, HBM, HBM, VMEM, VMEM, VMEM, VMEM],
+        in_specs=[VMEM] * 7,
         out_specs=(VMEM, VMEM, VMEM, HBM),
         scratch_shapes=[
             pltpu.VMEM((16, 8, 8, 128), F32),
@@ -642,7 +644,7 @@
         ],
         compiler_params=pltpu.CompilerParams(vmem_limit_bytes=4 << 20),
     )(
-        hbm(pix), hbm(bins), hbm(slot_count), leading, w_hi, w_lo, new_rows,
+        pix, bins, slot_count, leading, w_hi, w_lo, new_rows,
     )
     edges = swaps(edge_a, edge_b, "tile")
 
@@ -656,7 +658,7 @@
             jax.ShapeDtypeStruct((40, 128), F32),
             jax.ShapeDtypeStruct((8, 96), BF16),
         ),
-        in_specs=[VMEM] * 8 + [SMEM] * 3,
+        in_specs=[VMEM] * 11,
         out_specs=(VMEM,) * 5,
         scratch_shapes=[
             pltpu.VMEM((96, 384), F32),
@@ -664,11 +666,13 @@
             pltpu.VMEM((32, 128), F32),
             pltpu.VMEM((128, 512), F32),
             pltpu.VMEM((80, 512), F32),
+            pltpu.VMEM((8, 128), F32),
         ],
         compiler_params=pltpu.CompilerParams(vmem_limit_bytes=8 << 20),
     )(
         sp, sm, *sides, back, primal, jnp.transpose(primal_kernel, (1, 2, 3, 4, 0)),
-        primal_mixing, primal_bias, primal_slope, primal_shift,
+        primal_mixing, primal_bias.reshape(1, 32), primal_slope.reshape(1, 32),
+        primal_shift.reshape(1, 5),
     )
 
     new_primal = pl.pallas_call(

time: 71.2 us -> 71 us (level)
  Pallas kernels: 18.7 us -> 17.5 us
  waiting for transfers between devices: 10.7 us -> 11.7 us
    ppermute x4, waiting for transfers between devices: 3.97 us -> 4.98 us  [swaps(): b = lax.ppermute(second, axis, pairs)]
    unnamed x30 -> x36, local copies, waits for them, and re-layouts: 11.6 us -> 11.6 us
  transfers between devices with their start and end apart: 9 -> 9, of which waited for: 3 -> 3; matrix products, arithmetic and copies ran while one was open for 0% -> 0% of each run, Pallas kernels for 15% -> 14%
where the time goes in v10:
time: 71 us; the launch traced here: 70.7 us
  Pallas kernels  17.5 us (25%)
  starting transfers between devices  17 us (24%)
  blocking collectives  12 us (17%)
  waiting for transfers between devices  11.7 us (16%)
  local copies, waits for them, and re-layouts  11.6 us (16%)
  between operations  0.86 us (1%)
    all_to_all x1, blocking collectives, per_device(): leading = lax.all_to_all(send, 'tile', 0, 0, tiled=True)  12 us
    ppermute x4, starting transfers between devices, swaps(): b = lax.ppermute(second, axis, pairs)  12 us
    unnamed x36, local copies, waits for them, and re-layouts  11.6 us
    pallas_call x1, Pallas kernels, per_device(): pl.pallas_call(project_kernel, name='project', out_shape=(jax.ShapeDtypeS...  6.9 us
    all_to_all x1, waiting for transfers between devices, per_device(): got = lax.all_to_all(terms, 'tile', 0, 0, tiled=True)  6.7 us
    pallas_call x1, Pallas kernels, per_device(): pl.pallas_call(back_kernel, name='back', out_shape=(jax.ShapeDtypeStruct(...  5.01 us
    ppermute x4, waiting for transfers between devices, swaps(): b = lax.ppermute(second, axis, pairs)  4.98 us
    all_to_all x1, starting transfers between devices, per_device(): got = lax.all_to_all(terms, 'tile', 0, 0, tiled=True)  3.55 us
  transfers between devices with their start and end apart: 9, of which 3 were waited for; matrix products, arithmetic and copies ran while one was open for 0% of the time, Pallas kernels for 14%

profile of v10, /device:TPU:0, one launch (start us, length us, event | category | flops | bytes accessed | tf_op | source)
XLA Modules:
  0.0 70.7 jit_solution(3297822191908036138)
XLA Ops:
  0.6 1.0 %shard_map.176.after_ref.own_ref = f32[32,1024]{1,0:T(8,128)S(1)} custom-call(f32[5,2,1,1024]{3,2,1,0:T(1,128)} %dual_hbm.1, f32[2,1,1024]{2,1,0:T(1,128)} %measured_hbm.1, f32[5,2,4,512]{3,2,1,0:T(4,128)} %primal_ref.3), custom_call_target="tpu_custom_call" | custom-call | tf_op jit(solution)/shard_map/pallas_call | solution.py:555
  1.6 6.7 %collective-permute-start.1 = (f32[32,1024]{1,0:T(8,128)S(1)}, f32[32,1024]{1,0:T(8,128)S(1)}, u32[]{:S(2)}, u32[]{:S(2)}) collective-permute-start(f32[32,1024]{1,0:T(8,128)S(1)} %shard_map.176.after_ref.own_ref), channel_id=1, source_target_pairs={{0,15},{1,2},{2,1},{3,4},{4,3},{5,6},{6,5},{7,8},{8,7},{9,10},{10,... | collective-permute-start | bytes 393224 | tf_op jit(solution)/shard_map/ppermute | solution.py:542
  8.4 6.9 %project.1 = (f32[16,3,16,128]{3,2,1,0:T(8,128)}, bf16[104,256,128]{2,1,0:T(8,128)(2,1)S(1)}, bf16[104,256,128]{2,1,0:T(8,128)(2,1)S(1)}) custom-call(s32[12,1,16]{2,1,0:T(1,128)} %bitcast.15, s32[12,16,16]{2,1,0:T(8,128)} %bitcast.11, s32[1,16]{1,0:T(1,128)} %cnt_hbm.3, f32[5,2,4,512]{3,2,1,0:T(4,128)} %primal_ref.3, f32[16,6,256,128]{3,2,1,0:T(8,128)} %bitcast.23, ...), custom_call_target="tpu_custom_call" | custom-call | flops 2147483648 | bytes 26214400 | tf_op jit(solution)/shard_map/project/pallas_call | solution.py:568
  15.3 2.8 %copy-done = bf16[104,256,128]{2,1,0:T(8,128)(2,1)} copy-done((bf16[104,256,128]{2,1,0:T(8,128)(2,1)}, bf16[104,256,128]{2,1,0:T(8,128)(2,1)S(1)}, u32[]{:S(2)}) %copy-start) | copy-done | bytes 6815768
  18.1 2.9 %copy-done.2 = bf16[104,256,128]{2,1,0:T(8,128)(2,1)} copy-done((bf16[104,256,128]{2,1,0:T(8,128)(2,1)}, bf16[104,256,128]{2,1,0:T(8,128)(2,1)S(1)}, u32[]{:S(2)}) %copy-start.2) | copy-done | bytes 6815768
  21.0 3.6 %all-to-all-start = ((f32[16,3,16,128]{3,2,1,0:T(8,128)}), f32[16,3,16,128]{3,2,1,0:T(8,128)S(1)}, u32[]{:S(2)}, u32[]{:S(2)}) async-start(f32[16,3,16,128]{3,2,1,0:T(8,128)} %get-tuple-element.28), calls=%async_computation | async-start | bytes 786432 | tf_op jit(solution)/shard_map/all_to_all | solution.py:599
  24.5 0.1 shard_map.178
  24.6 0.1 collective-permute-start.4
  24.7 2.9 %collective-permute-start.5 = (f32[64,1024]{1,0:T(8,128)S(1)}, f32[64,1024]{1,0:T(8,128)S(1)}, u32[]{:S(2)}, u32[]{:S(2)}) collective-permute-start(f32[64,1024]{1,0:T(8,128)S(1)} %get-tuple-element.33), channel_id=1, source_target_pairs={{0,112},{16,32},{32,16},{48,64},{64,48},{80,96},{96,80},{112,0},{1... | collective-permute-start | bytes 786440 | tf_op jit(solution)/shard_map/ppermute | solution.py:542
  27.6 6.7 %all-to-all-done.got_ref = f32[16,3,16,128]{3,2,1,0:T(8,128)S(1)} async-done(((f32[16,3,16,128]{3,2,1,0:T(8,128)}), f32[16,3,16,128]{3,2,1,0:T(8,128)S(1)}, u32[]{:S(2)}, u32[]{:S(2)}) %all-to-all-start) | async-done | bytes 393248 | tf_op jit(solution)/shard_map/all_to_all | solution.py:599
  34.3 0.4 collective-permute-start.3
  34.7 1.3 %collective-permute-start.2 = (f32[48,128]{1,0:T(8,128)S(1)}, f32[48,128]{1,0:T(8,128)S(1)}, u32[]{:S(2)}, u32[]{:S(2)}) collective-permute-start(f32[48,128]{1,0:T(8,128)S(1)} %shard_map.177.total_ref), channel_id=1, source_target_pairs={{0,16},{16,0},{32,48},{48,32},{64,80},{80,64},{96,112},{112,96},{1... | collective-permute-start | bytes 73736 | tf_op jit(solution)/shard_map/ppermute | solution.py:540
  36.1 0.9 %shard_map.179 = (f32[128,1024]{1,0:T(8,128)S(1)}, bf16[128,240]{1,0:T(8,128)(2,1)S(1)}, f32[40,128]{1,0:T(8,128)S(1)}, bf16[8,96]{1,0:T(8,128)(2,1)S(1)}) custom-call(f32[64,1024]{1,0:T(8,128)S(1)} %get-tuple-element.31.own_ref.sp_ref, f32[64,1024]{1,0:T(8,128)S(1)} %collective-permute-done.4.first_ref, f32[64,1024]{1,0:T(8,128)S(1)} %collective-permute-done.5.second_ref, ...), custom_call_target="tpu_custom_call" | custom-call | tf_op jit(solution)/shard_map/pallas_call | solution.py:603
  37.0 1.9 %collective-permute-done.3.tb_ref = f32[48,128]{1,0:T(8,128)S(1)} collective-permute-done((f32[48,128]{1,0:T(8,128)S(1)}, f32[48,128]{1,0:T(8,128)S(1)}, u32[]{:S(2)}, u32[]{:S(2)}) %collective-permute-start.3) | collective-permute-done | bytes 24608 | tf_op jit(solution)/shard_map/ppermute | solution.py:542
  38.9 0.7 shard_map.180
  39.5 12.0 %all_to_all.10.nd_ref = f32[16,8,4,128]{3,2,1,0:T(4,128)S(1)} all-to-all(f32[16,8,4,128]{3,2,1,0:T(4,128)S(1)} %get-tuple-element.38), channel_id=1, replica_groups=mesh['plane'=8,'tile'=16] {'tile'}, dimensions={0} | all-to-all | bytes 524288 | tf_op jit(solution)/shard_map/all_to_all | solution.py:623
  51.6 2.9 %copy-done.1 = bf16[104,256,128]{2,1,0:T(8,128)(2,1)S(1)} copy-done((bf16[104,256,128]{2,1,0:T(8,128)(2,1)S(1)}, bf16[104,256,128]{2,1,0:T(8,128)(2,1)}, u32[]{:S(2)}) %copy-start.1) | copy-done | bytes 6815768
  54.5 2.9 %copy-done.3 = bf16[104,256,128]{2,1,0:T(8,128)(2,1)S(1)} copy-done((bf16[104,256,128]{2,1,0:T(8,128)(2,1)S(1)}, bf16[104,256,128]{2,1,0:T(8,128)(2,1)}, u32[]{:S(2)}) %copy-start.3) | copy-done | bytes 6815768
  57.4 5.0 %back.1 = (f32[64,128]{1,0:T(8,128)S(1)}, f32[16,128]{1,0:T(8,128)S(1)}, f32[16,128]{1,0:T(8,128)S(1)}, f32[5,2,1,1024]{3,2,1,0:T(1,128)}) custom-call(s32[12,1,16]{2,1,0:T(1,128)S(1)} %bitcast.16, s32[12,16,16]{2,1,0:T(8,128)S(1)} %bitcast.12, s32[1,16]{1,0:T(1,128)S(1)} %copy-done.11, f32[16,8,4,128]{3,2,1,0:T(4,128)S(1)} %all_to_all.10.nd_ref, ...), custom_call_target="tpu_custom_call" | custom-call | tf_op jit(solution)/shard_map/back/pallas_call | solution.py:625
  62.5 0.1 collective-permute-start.6
  62.6 2.1 %collective-permute-start.7 = (f32[16,128]{1,0:T(8,128)S(1)}, f32[16,128]{1,0:T(8,128)S(1)}, u32[]{:S(2)}, u32[]{:S(2)}) collective-permute-start(f32[16,128]{1,0:T(8,128)S(1)} %get-tuple-element.43), channel_id=1, source_target_pairs={{0,15},{1,2},{2,1},{3,4},{4,3},{5,6},{6,5},{7,8},{8,7},{9,10},{10,... | collective-permute-start | bytes 24584 | tf_op jit(solution)/shard_map/ppermute | solution.py:542
  64.7 1.9 %primal_inner.1 = (f32[128,512]{1,0:T(8,128)S(1)}, bf16[128,96]{1,0:T(8,128)(2,1)S(1)}, f32[5,2,4,512]{3,2,1,0:T(4,128)S(1)}, f32[40,128]{1,0:T(8,128)S(1)}, bf16[8,96]{1,0:T(8,128)(2,1)S(1)}) custom-call(f32[64,1024]{1,0:T(8,128)S(1)} %get-tuple-element.31.own_ref.sp_ref, f32[64,1024]{1,0:T(8,128)S(1)} %get-tuple-element.44.sm_ref, ...), custom_call_target="tpu_custom_call" | custom-call | tf_op jit(solution)/shard_map/primal_inner/pallas_call | solution.py:651
  66.5 3.1 %collective-permute-done.7.second_ref = f32[16,128]{1,0:T(8,128)S(1)} collective-permute-done((f32[16,128]{1,0:T(8,128)S(1)}, f32[16,128]{1,0:T(8,128)S(1)}, u32[]{:S(2)}, u32[]{:S(2)}) %collective-permute-start.7) | collective-permute-done | bytes 8224 | tf_op jit(solution)/shard_map/ppermute | solution.py:542
  69.6 1.1 %primal_outer.1 = f32[5,2,4,512]{3,2,1,0:T(4,128)} custom-call(f32[16,128]{1,0:T(8,128)S(1)} %collective-permute-done.6.first_ref, f32[16,128]{1,0:T(8,128)S(1)} %collective-permute-done.7.second_ref, f32[128,512]{1,0:T(8,128)S(1)} %get-tuple-element.46.part_ref, bf16[128,96]{1,0:T(8,128)(2,1)S(1)} %get-tuple-element.47.rim_ref, ...), custom_call_target="tpu_custom_call" | custom-call | tf_op jit(solution)/shard_map/primal_outer/pallas_call | solution.py:678
  (40 shorter events, 0.1 us)
Async XLA Ops:
  1.6 19.3 %collective-permute-start.1 = (f32[32,1024]{1,0:T(8,128)S(1)}, f32[32,1024]{1,0:T(8,128)S(1)}, u32[]{:S(2)}, u32[]{:S(2)}) collective-permute-start(f32[32,1024]{1,0:T(8,128)S(1)} %shard_map.176.after_ref.own_ref), channel_id=1, source_target_pairs={{0,15},{1,2},{2,1},{3,4},{4,3},{5,6},{6,5},{7,8},{8,7},{9,10},{10,... | collective-permute-start | bytes 393224 | tf_op jit(solution)/shard_map/ppermute | solution.py:542
  8.3 12.7 %collective-permute-start = (f32[32,1024]{1,0:T(8,128)S(1)}, f32[32,1024]{1,0:T(8,128)S(1)}, u32[]{:S(2)}, u32[]{:S(2)}) collective-permute-start(f32[32,1024]{1,0:T(8,128)S(1)} %shard_map.176.after_ref.own_ref), channel_id=1, source_target_pairs={{0,1},{1,0},{2,3},{3,2},{4,5},{5,4},{6,7},{7,6},{8,9},{9,8},{10,11... | collective-permute-start | bytes 393224 | tf_op jit(solution)/shard_map/ppermute | solution.py:540
  8.3 16.2 %copy-start.4 = (f32[5,2,4,512]{3,2,1,0:T(4,128)S(1)}, f32[5,2,4,512]{3,2,1,0:T(4,128)}, u32[]{:S(2)}) copy-start(f32[5,2,4,512]{3,2,1,0:T(4,128)} %primal_ref.3) | copy-start | bytes 245764
  8.3 27.7 %copy-start.6 = (f32[32,7,3,3,3]{0,1,4,3,2:T(8,128)S(1)}, f32[32,7,3,3,3]{0,1,4,3,2:T(8,128)}, u32[]{:S(2)}) copy-start(f32[32,7,3,3,3]{0,1,4,3,2:T(8,128)} %param.24) | copy-start | bytes 72580
  8.3 27.7 %copy-start.9 = (f32[5,32]{1,0:T(8,128)S(1)}, f32[5,32]{1,0:T(8,128)}, u32[]{:S(2)}) copy-start(f32[5,32]{1,0:T(8,128)} %mix_ref.2) | copy-start | bytes 1924
  8.3 27.7 %copy-start.12 = (f32[32]{0:T(128)S(1)}, f32[32]{0:T(128)}, u32[]{:S(2)}) copy-start(f32[32]{0:T(128)} %param.25) | copy-start | bytes 388
  8.3 27.7 %copy-start.13 = (f32[32]{0:T(128)S(1)}, f32[32]{0:T(128)}, u32[]{:S(2)}) copy-start(f32[32]{0:T(128)} %param.26) | copy-start | bytes 388
  8.3 27.7 %copy-start.14 = (f32[5]{0:T(128)S(1)}, f32[5]{0:T(128)}, u32[]{:S(2)}) copy-start(f32[5]{0:T(128)} %param.28) | copy-start | bytes 64
  8.3 43.2 %copy-start.5 = (s32[16,16,12]{1,0,2:T(8,128)S(1)}, s32[16,16,12]{1,0,2:T(8,128)}, u32[]{:S(2)}) copy-start(s32[16,16,12]{1,0,2:T(8,128)} %param.22) | copy-start | bytes 36868
  8.4 43.2 %copy-start.8 = (s32[1,16,12]{1,0,2:T(1,128)S(1)}, s32[1,16,12]{1,0,2:T(1,128)}, u32[]{:S(2)}) copy-start(s32[1,16,12]{1,0,2:T(1,128)} %param.21) | copy-start | bytes 2308
  8.4 43.2 %copy-start.11 = (s32[1,16]{1,0:T(1,128)S(1)}, s32[1,16]{1,0:T(1,128)}, u32[]{:S(2)}) copy-start(s32[1,16]{1,0:T(1,128)} %cnt_hbm.3) | copy-start | bytes 196
  21.0 13.3 %all-to-all-start = ((f32[16,3,16,128]{3,2,1,0:T(8,128)}), f32[16,3,16,128]{3,2,1,0:T(8,128)S(1)}, u32[]{:S(2)}, u32[]{:S(2)}) async-start(f32[16,3,16,128]{3,2,1,0:T(8,128)} %get-tuple-element.28), calls=%async_computation | async-start | bytes 786432 | tf_op jit(solution)/shard_map/all_to_all | solution.py:599
  24.6 11.4 %collective-permute-start.4 = (f32[64,1024]{1,0:T(8,128)S(1)}, f32[64,1024]{1,0:T(8,128)S(1)}, u32[]{:S(2)}, u32[]{:S(2)}) collective-permute-start(f32[64,1024]{1,0:T(8,128)S(1)} %get-tuple-element.32), channel_id=1, source_target_pairs={{0,16},{16,0},{32,48},{48,32},{64,80},{80,64},{96,112},{112,96},{1... | collective-permute-start | bytes 786440 | tf_op jit(solution)/shard_map/ppermute | solution.py:540
  24.7 11.3 %collective-permute-start.5 = (f32[64,1024]{1,0:T(8,128)S(1)}, f32[64,1024]{1,0:T(8,128)S(1)}, u32[]{:S(2)}, u32[]{:S(2)}) collective-permute-start(f32[64,1024]{1,0:T(8,128)S(1)} %get-tuple-element.33), channel_id=1, source_target_pairs={{0,112},{16,32},{32,16},{48,64},{64,48},{80,96},{96,80},{112,0},{1... | collective-permute-start | bytes 786440 | tf_op jit(solution)/shard_map/ppermute | solution.py:542
  34.3 4.5 %collective-permute-start.3 = (f32[48,128]{1,0:T(8,128)S(1)}, f32[48,128]{1,0:T(8,128)S(1)}, u32[]{:S(2)}, u32[]{:S(2)}) collective-permute-start(f32[48,128]{1,0:T(8,128)S(1)} %shard_map.177.total_ref), channel_id=1, source_target_pairs={{0,112},{16,32},{32,16},{48,64},{64,48},{80,96},{96,80},{112,0},{1... | collective-permute-start | bytes 73736 | tf_op jit(solution)/shard_map/ppermute | solution.py:542
  34.7 4.1 %collective-permute-start.2 = (f32[48,128]{1,0:T(8,128)S(1)}, f32[48,128]{1,0:T(8,128)S(1)}, u32[]{:S(2)}, u32[]{:S(2)}) collective-permute-start(f32[48,128]{1,0:T(8,128)S(1)} %shard_map.177.total_ref), channel_id=1, source_target_pairs={{0,16},{16,0},{32,48},{48,32},{64,80},{80,64},{96,112},{112,96},{1... | collective-permute-start | bytes 73736 | tf_op jit(solution)/shard_map/ppermute | solution.py:540
  51.6 2.9 %copy-start.1 = (bf16[104,256,128]{2,1,0:T(8,128)(2,1)S(1)}, bf16[104,256,128]{2,1,0:T(8,128)(2,1)}, u32[]{:S(2)}) copy-start(bf16[104,256,128]{2,1,0:T(8,128)(2,1)} %copy-done) | copy-start | bytes 20447236
  57.4 7.2 %copy-start.7 = (f32[32,6,3,3,3]{0,4,3,2,1:T(4,128)S(1)}, f32[32,6,3,3,3]{0,4,3,2,1:T(4,128)}, u32[]{:S(2)}) copy-start(f32[32,6,3,3,3]{0,4,3,2,1:T(4,128)} %param.29) | copy-start | bytes 62212
  57.4 7.2 %copy-start.10 = (f32[5,32]{1,0:T(8,128)S(1)}, f32[5,32]{1,0:T(8,128)}, u32[]{:S(2)}) copy-start(f32[5,32]{1,0:T(8,128)} %mix_ref.3) | copy-start | bytes 1924
  57.4 7.2 %copy-start.15 = (f32[32]{0:T(128)S(1)}, f32[32]{0:T(128)}, u32[]{:S(2)}) copy-start(f32[32]{0:T(128)} %param.30) | copy-start | bytes 388
  57.4 7.2 %copy-start.16 = (f32[32]{0:T(128)S(1)}, f32[32]{0:T(128)}, u32[]{:S(2)}) copy-start(f32[32]{0:T(128)} %param.31) | copy-start | bytes 388
  57.4 7.2 %copy-start.17 = (f32[5]{0:T(128)S(1)}, f32[5]{0:T(128)}, u32[]{:S(2)}) copy-start(f32[5]{0:T(128)} %param.33) | copy-start | bytes 64
  62.5 4.1 %collective-permute-start.6 = (f32[16,128]{1,0:T(8,128)S(1)}, f32[16,128]{1,0:T(8,128)S(1)}, u32[]{:S(2)}, u32[]{:S(2)}) collective-permute-start(f32[16,128]{1,0:T(8,128)S(1)} %get-tuple-element.42), channel_id=1, source_target_pairs={{0,1},{1,0},{2,3},{3,2},{4,5},{5,4},{6,7},{7,6},{8,9},{9,8},{10,11... | collective-permute-start | bytes 24584 | tf_op jit(solution)/shard_map/ppermute | solution.py:540
  62.6 7.0 %collective-permute-start.7 = (f32[16,128]{1,0:T(8,128)S(1)}, f32[16,128]{1,0:T(8,128)S(1)}, u32[]{:S(2)}, u32[]{:S(2)}) collective-permute-start(f32[16,128]{1,0:T(8,128)S(1)} %get-tuple-element.43), channel_id=1, source_target_pairs={{0,15},{1,2},{2,1},{3,4},{4,3},{5,6},{6,5},{7,8},{8,7},{9,10},{10,... | collective-permute-start | bytes 24584 | tf_op jit(solution)/shard_map/ppermute | solution.py:542
  (3 other events, 8.6 us)
